TPU v7x, 32 devices: a whole 2x2x4 slice. The times are simulated.
32 devices in a mesh: dp: 2 (over y), hid: 4 (over x, core), wid: 4 (over z).
Axes of the slice: x: 2, y: 2, z: 4, core: 2. Of those that a mesh axis runs over, the one named last changes fastest.
Arguments:
- hidden_in: bfloat16 [6144, 1536], P('dp', 'wid'), may hold values from -6 to 6
- cotangent: bfloat16 [6144, 1536], P('dp', 'wid'), may hold values from -6 to 6
- segments: int32 [8, 768], P(('dp', 'wid')), may hold values from 0 to 2, never falling along the last dimension, each value on 1 to 512 neighbouring positions
- gain_attn: bfloat16 [1536], P(('dp', 'wid')), may hold values from 0.5 to 1.5
- gain_mlp: bfloat16 [1536], P(('dp', 'wid')), may hold values from 0.5 to 1.5
- in_weight: bfloat16 [1536, 4, 1536], P(('dp', 'wid'), None, 'hid'), may hold values from -0.15625 to 0.15625
- beta_weight: bfloat16 [1536, 12], P(('dp', 'wid'), 'hid'), may hold values from -0.15625 to 0.15625
- out_weight: bfloat16 [1536, 1536], P('hid', ('dp', 'wid')), may hold values from -2.5 to 2.5
- gate_weight: bfloat16 [1536, 4096], P(('dp', 'wid'), 'hid'), may hold values from -0.15625 to 0.15625
- up_weight: bfloat16 [1536, 4096], P(('dp', 'wid'), 'hid'), may hold values from -0.15625 to 0.15625
- down_weight: bfloat16 [4096, 1536], P('hid', ('dp', 'wid')), may hold values from -0.1875 to 0.1875
Outputs:
- output: bfloat16 [6144, 1536], P('dp', 'wid')
- grad_input: float32 [6144, 1536], P('dp', 'wid')
- grad_gain_attn: float32 [1536], P(('dp', 'wid'))
- grad_gain_mlp: float32 [1536], P(('dp', 'wid'))
- grad_in_weight: float32 [1536, 4, 1536], P(('dp', 'wid'), None, 'hid')
- grad_beta_weight: float32 [1536, 12], P(('dp', 'wid'), 'hid')
- grad_out_weight: float32 [1536, 1536], P('hid', ('dp', 'wid'))
- grad_gate_weight: float32 [1536, 4096], P(('dp', 'wid'), 'hid')
- grad_up_weight: float32 [1536, 4096], P(('dp', 'wid'), 'hid')
- grad_down_weight: float32 [4096, 1536], P('hid', ('dp', 'wid'))
Inputs may be any that keep to these rules, and one draw needn't show every extreme that they name: `segments`: in each row (the 768 tokens of one block) ids never fall, each of the 3 ids occurs in one run of 1 to 512 tokens, and one run is exactly 512 long.
All inputs are finite; a program needn't handle non-finite values.
Results may differ from a plain program's by a relative error of at most 0.012.
The roundings to bfloat16 on the way count: a program that leaves them out, or rounds other values in their place, can miss the bound.
Values may be sent and summed in bfloat16 or wider, within the bound.
No kernel may reach another device: no remote copies, remote signals or barrier semaphores. Data moves between devices by JAX's collectives and lax.ppermute only.
A program may use at most 256 MiB of HBM per device.

v0:
```python
import jax
import jax.numpy as jnp
from jax import lax
from jax.sharding import PartitionSpec as P

HD = 128
BLK = 64


def householder_attention(
    queries, key_vecs, value_vecs, raw_dirs, beta_logit, segment_ids, block_size
):
    highest = lax.Precision.HIGHEST
    length, head_count, head_width = queries.shape
    block_count = length // block_size
    directions = raw_dirs * lax.rsqrt(jnp.sum(raw_dirs * raw_dirs, axis=-1, keepdims=True) + 1e-06)
    strengths = 2.0 * jax.nn.sigmoid(beta_logit)
    query_blocks = queries.reshape(block_count, block_size, head_count, head_width)
    key_blocks = key_vecs.reshape(block_count, block_size, head_count, head_width)
    dir_blocks = directions.reshape(block_count, block_size, head_count, head_width)
    strength_blocks = strengths.reshape(block_count, block_size, head_count).transpose(0, 2, 1)
    offsets = jnp.arange(block_size)
    strict_lower = (offsets[:, None] > offsets[None, :]).astype(jnp.float32)
    lower_incl = (offsets[:, None] >= offsets[None, :]).astype(jnp.float32)
    identity = jnp.eye(block_size, dtype=jnp.float32)
    gram_matrix = jnp.einsum("nshd,nthd->nhst", dir_blocks, dir_blocks, precision=highest)
    system = identity + strength_blocks[..., :, None] * gram_matrix * strict_lower
    right_side = identity * strength_blocks[..., :, None]
    tri_factor = jax.scipy.linalg.solve_triangular(
        system, right_side, lower=True, unit_diagonal=True
    )
    query_dirs = (
        jnp.einsum("nihd,nshd->nhis", query_blocks, dir_blocks, precision=highest) * lower_incl
    )
    dir_keys = (
        jnp.einsum("nthd,njhd->nhtj", dir_blocks, key_blocks, precision=highest) * strict_lower
    )
    factor_keys = jnp.einsum("nhst,nhtj->nhsj", tri_factor, dir_keys, precision=highest)
    inner_scores = jnp.einsum("nihd,njhd->nhij", query_blocks, key_blocks, precision=highest)
    inner_scores = inner_scores - jnp.einsum(
        "nhis,nhsj->nhij", query_dirs, factor_keys, precision=highest
    )
    keys_moved = key_blocks - jnp.einsum(
        "nhsj,nshd->njhd", factor_keys, dir_blocks, precision=highest
    )
    query_factor = jnp.einsum("nhis,nhst->nhit", query_dirs, tri_factor, precision=highest)
    queries_moved = query_blocks - jnp.einsum(
        "nhit,nthd->nihd", query_factor, dir_blocks, precision=highest
    )

    def sweep_step(moved_rows, item):
        block_index, keys_here, dirs_here, factor_here, inner_here, queries_here = item
        start = block_index * block_size
        zero_index = start * 0
        scores = jnp.einsum("ihd,jhd->hij", moved_rows, keys_here, precision=highest)
        scores = lax.dynamic_update_slice(scores, inner_here, (zero_index, start, zero_index))
        projected = jnp.einsum("ihd,shd->his", moved_rows, dirs_here, precision=highest)
        projected = jnp.einsum("his,hst->hit", projected, factor_here, precision=highest)
        moved_rows = moved_rows - jnp.einsum(
            "hit,thd->ihd", projected, dirs_here, precision=highest
        )
        moved_rows = lax.dynamic_update_slice(
            moved_rows, queries_here, (start, zero_index, zero_index)
        )
        return (moved_rows, scores)

    initial = jnp.zeros((length, head_count, head_width), jnp.float32)
    items = (
        jnp.arange(block_count, dtype=jnp.int32),
        keys_moved,
        dir_blocks,
        tri_factor,
        inner_scores,
        queries_moved,
    )
    _, scores = lax.scan(jax.checkpoint(sweep_step), initial, items, reverse=True)
    scores = scores.transpose(1, 2, 0, 3).reshape(head_count, length, length)
    position = jnp.arange(length)
    allowed = (position[None, :] <= position[:, None]) & (
        segment_ids[:, None] == segment_ids[None, :]
    )
    scores = jnp.where(allowed[None], scores * head_width ** (-0.5), -1e30)
    row_top = jnp.max(scores, axis=-1, keepdims=True)
    exponent = jnp.exp(scores - row_top)
    attn_probs = exponent / jnp.sum(exponent, axis=-1, keepdims=True)
    return jnp.einsum("hij,jhd->ihd", attn_probs, value_vecs, precision=highest)


def norm_back(values, scale_row, gain, grad_out):
    weighted = grad_out * gain
    grad_gain = jnp.sum(grad_out * values * scale_row, axis=0)
    grad_values = scale_row * weighted - values * scale_row**3 * jnp.mean(
        weighted * values, axis=-1, keepdims=True
    )
    return (grad_gain, grad_values)


def body(
    hidden_in,
    cotangent,
    segments,
    gain_attn,
    gain_mlp,
    in_weight,
    beta_weight,
    out_weight,
    gate_weight,
    up_weight,
    down_weight,
):
    highest = lax.Precision.HIGHEST
    token_in, token_grad = (
        lax.all_to_all(hidden_in, "wid", split_axis=0, concat_axis=1, tiled=True),
        lax.all_to_all(cotangent, "wid", split_axis=0, concat_axis=1, tiled=True),
    )
    gathered = (
        lax.all_gather(gain_attn, ("dp", "wid"), axis=0, tiled=True),
        lax.all_gather(gain_mlp, ("dp", "wid"), axis=0, tiled=True),
        lax.all_gather(in_weight, ("dp", "wid"), axis=0, tiled=True),
        lax.all_gather(beta_weight, ("dp", "wid"), axis=0, tiled=True),
        lax.all_gather(out_weight, ("dp", "wid"), axis=1, tiled=True),
        lax.all_gather(gate_weight, ("dp", "wid"), axis=0, tiled=True),
        lax.all_gather(up_weight, ("dp", "wid"), axis=0, tiled=True),
        lax.all_gather(down_weight, ("dp", "wid"), axis=1, tiled=True),
    )
    gain_one, gain_two, weight_in, weight_beta, weight_out, weight_gate, weight_up, weight_down = (
        gathered
    )
    gain_one = gain_one.astype(jnp.float32)
    gain_two = gain_two.astype(jnp.float32)
    row_count = token_in.shape[0]
    head_count = weight_beta.shape[1]
    seg_row = segments[0]
    inputs = token_in.astype(jnp.float32)
    scale_one = lax.rsqrt(jnp.mean(inputs * inputs, axis=-1, keepdims=True) + 1e-06)
    normed = (inputs * scale_one * gain_one).astype(jnp.bfloat16)
    projected = jnp.einsum(
        "td,dkc->tkc", normed, weight_in, preferred_element_type=jnp.float32
    ).astype(jnp.bfloat16)
    logits = jnp.dot(normed, weight_beta, preferred_element_type=jnp.float32)
    pieces = projected.astype(jnp.float32).reshape(row_count, 4, head_count, HD)
    query_in = pieces[:, 0]
    key_in = pieces[:, 1]
    value_in = pieces[:, 2]
    dirs_in = pieces[:, 3]

    def attend(queries, key_vecs, value_vecs, raw_dirs, beta_logit):
        return householder_attention(
            queries, key_vecs, value_vecs, raw_dirs, beta_logit, seg_row, BLK
        )

    attended = attend(query_in, key_in, value_in, dirs_in, logits)
    attended = attended.reshape(row_count, head_count * HD).astype(jnp.bfloat16)
    branch = lax.psum(jnp.dot(attended, weight_out, preferred_element_type=jnp.float32), "hid")
    middle = inputs + branch
    scale_two = lax.rsqrt(jnp.mean(middle * middle, axis=-1, keepdims=True) + 1e-06)
    mixed = (middle * scale_two * gain_two).astype(jnp.bfloat16)
    gate = jnp.dot(mixed, weight_gate, preferred_element_type=jnp.float32)
    upward = jnp.dot(mixed, weight_up, preferred_element_type=jnp.float32)
    sigmoid_gate = jax.nn.sigmoid(gate)
    silu_gate = gate * sigmoid_gate
    product = (silu_gate * upward).astype(jnp.bfloat16)
    feed = lax.psum(
        jnp.dot(product, weight_down, preferred_element_type=jnp.float32).astype(jnp.bfloat16),
        "hid",
    ).astype(jnp.float32)
    output = lax.all_to_all(
        (middle + feed).astype(jnp.bfloat16), "wid", split_axis=1, concat_axis=0, tiled=True
    )
    grad_product = jnp.einsum(
        "td,fd->tf", token_grad, weight_down, preferred_element_type=jnp.float32
    )
    grad_down = jnp.einsum("tf,td->fd", product, token_grad, preferred_element_type=jnp.float32)
    grad_gate_pre = (
        grad_product * upward * sigmoid_gate * (1.0 + gate * (1.0 - sigmoid_gate))
    ).astype(jnp.bfloat16)
    grad_up_pre = (grad_product * silu_gate).astype(jnp.bfloat16)
    grad_mixed_part = jnp.einsum(
        "tf,df->td", grad_gate_pre, weight_gate, preferred_element_type=jnp.float32
    )
    grad_mixed_part = grad_mixed_part + jnp.einsum(
        "tf,df->td", grad_up_pre, weight_up, preferred_element_type=jnp.float32
    )
    grad_gate = jnp.einsum("td,tf->df", mixed, grad_gate_pre, preferred_element_type=jnp.float32)
    grad_up = jnp.einsum("td,tf->df", mixed, grad_up_pre, preferred_element_type=jnp.float32)
    grad_mixed = lax.psum(grad_mixed_part, "hid")
    grad_gain_two, grad_middle = norm_back(middle, scale_two, gain_two, grad_mixed)
    grad_middle = grad_middle + token_grad.astype(jnp.float32)
    grad_branch = grad_middle.astype(jnp.bfloat16)
    grad_attended = jnp.einsum(
        "td,cd->tc", grad_branch, weight_out, preferred_element_type=jnp.float32
    )
    grad_out = jnp.einsum("tc,td->cd", attended, grad_branch, preferred_element_type=jnp.float32)
    grad_heads = grad_attended.reshape(row_count, head_count, HD)
    _, attend_again = jax.vjp(attend, query_in, key_in, value_in, dirs_in, logits)
    grads_attn = attend_again(grad_heads)
    grad_query, grad_key, grad_value, grad_dirs, grad_logit = grads_attn
    grad_proj = jnp.stack((grad_query, grad_key, grad_value, grad_dirs), axis=1)
    grad_proj = grad_proj.reshape(row_count, 4, head_count * HD).astype(jnp.bfloat16)
    grad_normed_part = jnp.einsum(
        "tkc,dkc->td", grad_proj, weight_in, preferred_element_type=jnp.float32
    )
    grad_normed_part = grad_normed_part + jnp.dot(
        grad_logit, weight_beta.astype(jnp.float32).T, precision=highest
    )
    grad_in = jnp.einsum("td,tkc->dkc", normed, grad_proj, preferred_element_type=jnp.float32)
    grad_beta = jnp.dot(normed.astype(jnp.float32).T, grad_logit, precision=highest)
    grad_normed = lax.psum(grad_normed_part, "hid")
    grad_gain_one, grad_inputs = norm_back(inputs, scale_one, gain_one, grad_normed)
    grad_inputs = grad_inputs + grad_middle
    grad_input = lax.all_to_all(grad_inputs, "wid", split_axis=1, concat_axis=0, tiled=True)
    shares = (
        lax.psum_scatter(grad_gain_one, ("dp", "wid"), scatter_dimension=0, tiled=True),
        lax.psum_scatter(grad_gain_two, ("dp", "wid"), scatter_dimension=0, tiled=True),
        lax.psum_scatter(grad_in, ("dp", "wid"), scatter_dimension=0, tiled=True),
        lax.psum_scatter(grad_beta, ("dp", "wid"), scatter_dimension=0, tiled=True),
        lax.psum_scatter(grad_out, ("dp", "wid"), scatter_dimension=1, tiled=True),
        lax.psum_scatter(grad_gate, ("dp", "wid"), scatter_dimension=0, tiled=True),
        lax.psum_scatter(grad_up, ("dp", "wid"), scatter_dimension=0, tiled=True),
        lax.psum_scatter(grad_down, ("dp", "wid"), scatter_dimension=1, tiled=True),
    )
    return (
        output,
        grad_input,
        shares[0],
        shares[1],
        shares[2],
        shares[3],
        shares[4],
        shares[5],
        shares[6],
        shares[7],
    )


def solution(mesh):
    placed = (
        P("dp", "wid"),
        P("dp", "wid"),
        P(("dp", "wid"), None),
        P(("dp", "wid")),
        P(("dp", "wid")),
        P(("dp", "wid"), None, "hid"),
        P(("dp", "wid"), "hid"),
        P("hid", ("dp", "wid")),
        P(("dp", "wid"), "hid"),
        P(("dp", "wid"), "hid"),
        P("hid", ("dp", "wid")),
    )
    return jax.shard_map(
        body,
        mesh=mesh,
        in_specs=placed,
        out_specs=(
            P("dp", "wid"),
            P("dp", "wid"),
            P(("dp", "wid")),
            P(("dp", "wid")),
            P(("dp", "wid"), None, "hid"),
            P(("dp", "wid"), "hid"),
            P("hid", ("dp", "wid")),
            P(("dp", "wid"), "hid"),
            P(("dp", "wid"), "hid"),
            P("hid", ("dp", "wid")),
        ),
        check_vma=False,
    )
```

profile of v0, /device:TPU:0, one launch (start us, length us, event | category | flops | bytes accessed | tf_op | source)
XLA Modules:
  0.0 2532.7 jit_solution(9748514839555380016)
XLA Ops:
  9.3 6.5 all-to-all-start
  18.4 89.2 %all-reduce.5 = (bf16[1536]{0:T(1024)(128)(2,1)S(1)}, bf16[1536]{0:T(1024)(128)(2,1)S(1)}) all-reduce(bf16[1536]{0:T(1024)(128)(2,1)S(1)} %dynamic-update-slice, bf16[1536]{0:T(1024)(128)(2,1)S(1)} %dynamic-update-slice.1), channel_id=1, replica_groups=mesh['dp'=2,'hid'=4,'wid'=4] {'dp','wid'}, use_global_device_ids=true, to_apply=%add | all-reduce | flops 3072 | bytes 12288
  107.6 27.1 %all-gather = bf16[8,192,3]{1,2,0:T(4,128)(2,1)S(1)} all-gather(bf16[1,192,3]{1,2,0:T(4,128)(2,1)S(1)} %bitcast.620), channel_id=1, replica_groups=mesh['dp'=2,'hid'=4,'wid'=4] {'dp','wid'}, dimensions={0}, use_global_device_ids=true | all-gather | bytes 10368 | tf_op jit(solution)/shard_map/all_gather | solution.py:120
  142.9 6.2 fusion.66
  158.4 177.4 %custom-call.8 = f32[12,3,1,64,64]{3,4,2,1,0:T(8,128)S(1)} custom-call(f32[12,3,1,64,64]{4,3,2,1,0:T(8,128)S(1)} %add_bitcast_fusion), custom_call_target="InvertDiagBlocksLowerTriangular" | custom-call | tf_op jit(solution)/shard_map/jit(_solve_triangular)/vmap(vmap())/triangular_solve/custom-call.1 | solution.py:29
  361.2 4.5 fusion.82
  372.9 6.7 broadcast_in_dim.127
  379.6 3.7 broadcast.244.clone.1
  383.4 167.9 %while.59 = (s32[]{:T(128)}, f32[768,3,128]{0,2,1:T(8,128)S(1)}, f32[12,3,768,64]{2,3,1,0:T(8,128)}, f32[12,768,3,128]{1,3,2,0:T(8,128)}, f32[12,64,3,128]{3,1,2...) while((s32[]{:T(128)}, f32[768,3,128]{0,2,1:T(8,128)S(1)}, ...), condition=%wide.region_12.14_spmd.clone, body=%wide.region_11.13_spmd.sunk.clone | while | flops 793018368 | bytes 12189915 | solution.py:76
  551.2 3.7 broadcast.244.clone
  555.0 154.8 %while.58 = (s32[]{:T(128)}, f32[768,3,128]{0,2,1:T(8,128)S(1)}, f32[12,3,768,64]{2,3,1,0:T(8,128)}, f32[12,64,3,128]{3,1,2,0:T(8,128)}, f32[12,3,64,64]{2,3,1,0...) while((s32[]{:T(128)}, f32[768,3,128]{0,2,1:T(8,128)S(1)}, ...), condition=%wide.region_3.5_spmd.clone, body=%wide.region_2.4_spmd.sunk.clone | while | flops 793018368 | bytes 9830607 | solution.py:76
  709.9 6.3 select_reduce_fusion.1
  719.0 4.1 exponential_reduce_fusion
  726.5 3.7 convolution_convert_fusion.1
  730.3 5.0 fusion.167
  736.5 3.8 all-to-all-start.2
  740.9 39.9 %all-to-all-done.2 = bf16[4,768,384]{2,1,0:T(8,128)(2,1)S(1)} async-done(((bf16[4,768,384]{2,1,0:T(8,128)(2,1)}), bf16[4,768,384]{2,1,0:T(8,128)(2,1)S(1)}, u32[]{:S(2)}, u32[]{:S(2)}) %all-to-all-start.2) | async-done | bytes 2359328 | tf_op jit(solution)/shard_map/all_to_all | solution.py:114
  784.2 43.4 %all-reduce.11.cloned.1.call-done = f32[768,1536]{1,0:T(8,128)} async-done(((f32[768,1536]{1,0:T(8,128)}), f32[768,1536]{1,0:T(8,128)}) %all-reduce.11.cloned.1.call-update) | async-done | bytes 4718608 | tf_op jit(solution)/shard_map/psum | solution.py:154
  827.6 4.4 multiply_reduce_fusion.5
  836.0 54.2 %all-gather.11.cloned.1.call-done = bf16[1536,1024]{1,0:T(8,128)(2,1)} async-done(((bf16[192,1024]{1,0:T(8,128)(2,1)}), bf16[1536,1024]{1,0:T(8,128)(2,1)}) %all-gather.11.cloned.1.call-update) | async-done | bytes 3145744 | tf_op jit(solution)/shard_map/all_gather | solution.py:122
  890.2 6.9 fusion.168
  897.1 54.2 %all-gather.13.cloned.1.call-done = bf16[1536,1024]{1,0:T(8,128)(2,1)} async-done(((bf16[192,1024]{1,0:T(8,128)(2,1)}), bf16[1536,1024]{1,0:T(8,128)(2,1)}) %all-gather.13.cloned.1.call-update) | async-done | bytes 3145744 | tf_op jit(solution)/shard_map/all_gather | solution.py:123
  951.2 6.8 fusion.169
  958.1 54.2 %all-gather.15.cloned.1.call-done = bf16[1024,1536]{0,1:T(8,128)(2,1)} async-done(((bf16[1024,192]{0,1:T(8,128)(2,1)}), bf16[1024,1536]{0,1:T(8,128)(2,1)}) %all-gather.15.cloned.1.call-update) | async-done | bytes 3145744 | tf_op jit(solution)/shard_map/all_gather | solution.py:124
  1012.3 7.9 multiply_convert_fusion.2
  1023.2 4.5 convolution_add_fusion
  1029.1 5.7 convolution_convert_fusion
  1034.9 3.6 multiply_bitcast_fusion
  1041.8 78.6 %all-reduce.15.cloned.1.call-done = f32[768,1536]{1,0:T(8,128)} async-done(((f32[768,1536]{1,0:T(8,128)}), f32[768,1536]{1,0:T(8,128)}) %all-reduce.15.cloned.1.call-update) | async-done | bytes 4718608 | tf_op jit(solution)/shard_map/psum | solution.py:186
  1120.5 5.7 multiply_reduce_fusion.1
  1126.2 52.5 %all-reduce.13.cloned.1.call-done = bf16[768,1536]{1,0:T(8,128)(2,1)} async-done(((bf16[768,1536]{1,0:T(8,128)(2,1)}), bf16[768,1536]{1,0:T(8,128)(2,1)}) %all-reduce.13.cloned.1.call-update) | async-done | bytes 2359312 | tf_op jit(solution)/shard_map/psum | solution.py:163
  1178.7 7.7 convert_add_fusion
  1188.5 9.1 subtract_exponential_fusion
  1200.2 3.5 select_multiply_fusion
  1203.7 3.6 copy.345
  1207.3 388.9 %while.60 = (s32[]{:T(128)}, f32[768,3,128]{2,0,1:T(8,128)}, f32[12,64,3,128]{3,1,2,0:T(8,128)}, f32[12,64,3,128]{3,1,2,0:T(8,128)}, f32[12,3,64,64]{3,2,1,0:T(8...) while((s32[]{:T(128)}, f32[768,3,128]{2,0,1:T(8,128)}, ...), condition=%wide.region_19.21_spmd.clone.clone, body=%wide.region_18.20_spmd.clone.sunk.clone | while | flops 1926684672 | bytes 39472068 | solution.py:76
  1603.7 3.4 convolution_add_fusion.3
  1610.3 3.5 convolution_add_fusion.2
  1621.0 3.5 convolution_bitcast_fusion.14
  1629.1 3.8 fusion.75
  1641.2 3.4 convolution_bitcast_fusion.17
  1651.0 10.9 fusion.86
  1664.1 3.8 fusion.81
  1677.8 5.9 fusion.125
  1683.7 4.5 bitcast_add_fusion
  1689.8 4.1 fusion.140
  1694.1 7.7 fusion.60
  1702.9 5.3 fusion.103
  1709.8 6.0 fusion.173
  1715.9 6.3 fusion.174
  1723.9 6.0 fusion.175
  1733.2 4.8 all-to-all-start.1
  1737.9 44.5 %all-reduce.17.cloned.1.call-done = f32[768,1536]{1,0:T(8,128)} async-done(((f32[768,1536]{1,0:T(8,128)}), f32[768,1536]{1,0:T(8,128)}) %all-reduce.17.cloned.1.call-update) | async-done | bytes 4718608 | tf_op jit(solution)/shard_map/psum | solution.py:208
  1782.5 5.1 multiply_reduce_fusion.2
  1787.6 4.5 subtract_add_fusion
  1794.5 5.1 all-to-all-start.3
  1800.3 116.1 %reduce-scatter.19.cloned.1.call-done = f32[192,3]{1,0:T(8,128)} async-done(((f32[1536,3]{1,0:T(8,128)}), f32[192,3]{1,0:T(8,128)}) %reduce-scatter.19.cloned.1.call-update) | async-done | bytes 2320
  1917.9 36.1 %all-reduce.4 = (f32[1536]{0:T(1024)S(1)}, f32[1536]{0:T(1024)S(1)}) all-reduce(f32[1536]{0:T(1024)S(1)} %get-tuple-element.653, f32[1536]{0:T(1024)S(1)} %copy-done.83), channel_id=2, replica_groups=mesh['dp'=2,'hid'=4,'wid'=4] {'dp','wid'}, use_global_device_ids=true, to_apply=%region_26.29.clone | all-reduce | flops 3072 | bytes 24576
  1955.3 127.3 %reduce-scatter.9.cloned.1.call-done = f32[192,4,384]{2,0,1:T(8,128)} async-done(((f32[1536,4,384]{2,0,1:T(8,128)}), f32[192,4,384]{2,0,1:T(8,128)}) %reduce-scatter.9.cloned.1.call-update) | async-done | bytes 1179664 | tf_op jit(solution)/shard_map/reduce_scatter | solution.py:215
  2085.7 69.2 %reduce-scatter.11.cloned.1.call-done = f32[384,192]{0,1:T(8,128)} async-done(((f32[384,1536]{0,1:T(8,128)}), f32[384,192]{0,1:T(8,128)}) %reduce-scatter.11.cloned.1.call-update) | async-done | bytes 294928 | tf_op jit(solution)/shard_map/reduce_scatter | solution.py:217
  2154.8 121.6 %reduce-scatter.13.cloned.1.call-done = f32[192,1024]{1,0:T(8,128)} async-done(((f32[1536,1024]{1,0:T(8,128)}), f32[192,1024]{1,0:T(8,128)}) %reduce-scatter.13.cloned.1.call-update) | async-done | bytes 786448 | tf_op jit(solution)/shard_map/reduce_scatter | solution.py:218
  2276.4 121.5 %reduce-scatter.15.cloned.1.call-done = f32[192,1024]{1,0:T(8,128)} async-done(((f32[1536,1024]{1,0:T(8,128)}), f32[192,1024]{1,0:T(8,128)}) %reduce-scatter.15.cloned.1.call-update) | async-done | bytes 786448 | tf_op jit(solution)/shard_map/reduce_scatter | solution.py:219
  2398.0 121.5 %reduce-scatter.17.cloned.1.call-done = f32[1024,192]{0,1:T(8,128)} async-done(((f32[1024,1536]{0,1:T(8,128)}), f32[1024,192]{0,1:T(8,128)}) %reduce-scatter.17.cloned.1.call-update) | async-done | bytes 786448 | tf_op jit(solution)/shard_map/reduce_scatter | solution.py:220
  2520.9 4.8 copy.419
  (1043 shorter events, 833.8 us)
Async XLA Ops:
  7.2 135.7 %all-gather.7.cloned.1.call-start = ((), (), s32[]{:S(2)}) async-start(), calls=%async_computation.10 | async-start | bytes 5308416 | tf_op jit(solution)/shard_map/all_gather | solution.py:119
  9.2 7.3 copy-start.87
  9.2 8.6 copy-start.90
  9.2 8.9 copy-start.91
  9.2 98.3 %copy-start.86 = (bf16[192,3]{0,1:T(4,128)(2,1)S(1)}, bf16[192,3]{0,1:T(4,128)(2,1)}, u32[]{:S(2)}) copy-start(bf16[192,3]{0,1:T(4,128)(2,1)} %param.27) | copy-start | bytes 3460
  9.2 125.5 %copy-start.85 = (s32[1,768]{1,0:T(1,128)S(1)}, s32[1,768]{1,0:T(1,128)}, u32[]{:S(2)}) copy-start(s32[1,768]{1,0:T(1,128)} %param.23) | copy-start | bytes 9220
  9.3 128.9 %all-to-all-start = ((bf16[4,768,384]{2,1,0:T(8,128)(2,1)}), bf16[4,768,384]{2,1,0:T(8,128)(2,1)S(1)}, u32[]{:S(2)}, u32[]{:S(2)}) async-start(bf16[4,768,384]{2,1,0:T(8,128)(2,1)} %bitcast.612), calls=%async_computation | async-start | bytes 4718592 | tf_op jit(solution)/shard_map/all_to_all | solution.py:113
  15.7 714.6 %all-gather.9.cloned.1.call-start = ((), (), s32[]{:S(2)}) async-start(), calls=%async_computation.11 | async-start | bytes 1327104 | tf_op jit(solution)/shard_map/all_gather | solution.py:121
  16.5 811.1 %all-reduce.11.cloned.1.call-start = ((), (), s32[]{:S(2)}) async-start(), calls=%async_computation.12 | async-start | bytes 9437184 | tf_op jit(solution)/shard_map/psum | solution.py:154
  107.6 33.2 %copy-start.69 = (f32[1536]{0:T(1024)}, f32[1536]{0:T(1024)S(1)}, u32[]{:S(2)}) copy-start(f32[1536]{0:T(1024)S(1)} %convert_element_type.109) | copy-start | bytes 18436
  134.8 6.4 copy-start.72
  135.5 22.3 copy-start.58
  135.6 22.2 copy-start.65
  135.6 22.2 copy-start.79
  142.9 14.9 copy-start.61
  154.7 213.8 %copy-start = (f32[12,64,3,128]{3,1,0,2:T(8,128)}, f32[12,64,3,128]{3,1,0,2:T(8,128)S(1)}, u32[]{:S(2)}) copy-start(f32[12,64,3,128]{3,1,0,2:T(8,128)S(1)} %broadcast_multiply_fusion) | copy-start | bytes 3538948
  339.0 13.2 copy-start.10
  346.9 14.3 copy-start.14
  555.0 154.8 %copy-start.50 = (pred[768,12,64]{0,2,1:T(8,128)(4,1)S(1)}, pred[768,12,64]{0,2,1:T(8,128)(4,1)}, u32[]{:S(2)}) copy-start(pred[768,12,64]{0,2,1:T(8,128)(4,1)} %fusion.65) | copy-start | bytes 1769476
  709.8 6.4 slice-start.2
  709.9 7.2 slice-start.3
  709.9 9.2 copy-start.7
  730.3 5.1 copy-start.48
  735.4 154.8 %all-gather.11.cloned.1.call-start = ((), (), s32[]{:S(2)}) async-start(), calls=%async_computation.13 | async-start | bytes 3538944 | tf_op jit(solution)/shard_map/all_gather | solution.py:122
  735.9 215.3 %all-gather.13.cloned.1.call-start = ((), (), s32[]{:S(2)}) async-start(), calls=%async_computation.14 | async-start | bytes 3538944 | tf_op jit(solution)/shard_map/all_gather | solution.py:123
  736.5 44.3 %all-to-all-start.2 = ((bf16[4,768,384]{2,1,0:T(8,128)(2,1)}), bf16[4,768,384]{2,1,0:T(8,128)(2,1)S(1)}, u32[]{:S(2)}, u32[]{:S(2)}) async-start(bf16[4,768,384]{2,1,0:T(8,128)(2,1)} %bitcast.613), calls=%async_computation.2 | async-start | bytes 4718592 | tf_op jit(solution)/shard_map/all_to_all | solution.py:114
  740.3 272.0 %all-gather.15.cloned.1.call-start = ((), (), s32[]{:S(2)}) async-start(), calls=%async_computation.15 | async-start | bytes 3538944 | tf_op jit(solution)/shard_map/all_gather | solution.py:124
  740.9 379.6 %all-reduce.15.cloned.1.call-start = ((), (), s32[]{:S(2)}) async-start(), calls=%async_computation.17 | async-start | bytes 9437184 | tf_op jit(solution)/shard_map/psum | solution.py:186
  784.2 228.1 %copy-start.44 = (bf16[4,96,8,384]{3,2,0,1:T(8,128)(2,1)}, bf16[4,96,8,384]{3,2,0,1:T(8,128)(2,1)S(1)}, u32[]{:S(2)}) copy-start(bf16[4,96,8,384]{3,2,0,1:T(8,128)(2,1)S(1)} %copy.300) | copy-start | bytes 7077892
  1012.3 7.9 copy-start.88
  1027.7 151.0 %all-reduce.13.cloned.1.call-start = ((), (), s32[]{:S(2)}) async-start(), calls=%async_computation.16 | async-start | bytes 4718592 | tf_op jit(solution)/shard_map/psum | solution.py:163
  1034.8 747.6 %all-reduce.17.cloned.1.call-start = ((), (), s32[]{:S(2)}) async-start(), calls=%async_computation.18 | async-start | bytes 9437184 | tf_op jit(solution)/shard_map/psum | solution.py:208
  1120.5 68.0 %slice-start = ((s8[7077888]{0:T(1024)(128)(4,1)}), s8[2883584]{0:T(1024)(128)(4,1)S(1)}, s32[]{:S(2)}) async-start(s8[7077888]{0:T(1024)(128)(4,1)} %bitcast.575), calls=%async_computation.25 | async-start | bytes 5767168
  1178.7 7.7 copy-start.56
  1178.7 9.8 slice-start.1
  1188.5 9.1 copy-start.51
  1207.3 389.0 %copy-start.1 = (f32[12,64,3,128]{3,1,0,2:T(8,128)S(1)}, f32[12,64,3,128]{3,1,0,2:T(8,128)}, u32[]{:S(2)}) copy-start(f32[12,64,3,128]{3,1,0,2:T(8,128)} %copy-done) | copy-start | bytes 3538948
  1251.8 3.7 copy-start.19
  1284.4 3.7 copy-start.19
  1316.6 3.7 copy-start.19
  1349.3 3.6 copy-start.19
  1381.5 3.7 copy-start.19
  1414.2 3.7 copy-start.19
  1479.1 3.6 copy-start.19
  1543.9 3.7 copy-start.19
  1576.1 3.7 copy-start.19
  1646.8 4.2 copy-start.52
  1664.1 3.8 copy-start.41
  1677.7 5.9 copy-start.74
  1677.7 5.9 copy-start.71
  1677.7 5.9 copy-start.73
  1688.2 228.2 %reduce-scatter.19.cloned.1.call-start = ((), (), s32[]{:S(2)}) async-start(), calls=%async_computation.24 | async-start | bytes 884736
  1694.0 388.6 %reduce-scatter.9.cloned.1.call-start = ((), (), s32[]{:S(2)}) async-start(), calls=%async_computation.19 | async-start | bytes 10616832 | tf_op jit(solution)/shard_map/reduce_scatter | solution.py:215
  1701.8 453.0 %reduce-scatter.11.cloned.1.call-start = ((), (), s32[]{:S(2)}) async-start(), calls=%async_computation.20 | async-start | bytes 2654208 | tf_op jit(solution)/shard_map/reduce_scatter | solution.py:217
  1708.2 568.2 %reduce-scatter.13.cloned.1.call-start = ((), (), s32[]{:S(2)}) async-start(), calls=%async_computation.21 | async-start | bytes 7077888 | tf_op jit(solution)/shard_map/reduce_scatter | solution.py:218
  1715.8 682.1 %reduce-scatter.15.cloned.1.call-start = ((), (), s32[]{:S(2)}) async-start(), calls=%async_computation.22 | async-start | bytes 7077888 | tf_op jit(solution)/shard_map/reduce_scatter | solution.py:219
  1722.2 797.3 %reduce-scatter.17.cloned.1.call-start = ((), (), s32[]{:S(2)}) async-start(), calls=%async_computation.23 | async-start | bytes 7077888 | tf_op jit(solution)/shard_map/reduce_scatter | solution.py:220
  1733.2 49.3 %copy-start.70 = (f32[1536]{0:T(1024)S(1)}, f32[1536]{0:T(1024)}, u32[]{:S(2)}) copy-start(f32[1536]{0:T(1024)} %copy-done.69) | copy-start | bytes 18436
  1733.2 49.3 %copy-start.82 = (f32[768]{0:T(1024)S(1)}, f32[768]{0:T(1024)}, u32[]{:S(2)}) copy-start(f32[768]{0:T(1024)} %copy-done.81) | copy-start | bytes 9220
  1733.2 61.4 %all-to-all-start.1 = ((bf16[768,4,384]{2,0,1:T(8,128)(2,1)}), bf16[768,4,384]{2,0,1:T(8,128)(2,1)S(1)}, u32[]{:S(2)}, u32[]{:S(2)}) async-start(bf16[768,4,384]{2,0,1:T(8,128)(2,1)} %bitcast.603), calls=%async_computation.1 | async-start | bytes 4718592 | tf_op jit(solution)/shard_map/all_to_all | solution.py:167
  1737.9 49.6 %copy-start.84 = (f32[768]{0:T(1024)S(1)}, f32[768]{0:T(1024)}, u32[]{:S(2)}) copy-start(f32[768]{0:T(1024)} %get-tuple-element.744) | copy-start | bytes 9220
  1782.5 5.1 copy-start.22
  1794.5 123.4 %copy-start.83 = (f32[1536]{0:T(1024)S(1)}, f32[1536]{0:T(1024)}, u32[]{:S(2)}) copy-start(f32[1536]{0:T(1024)} %get-tuple-element.651) | copy-start | bytes 18436
  1794.5 160.8 %all-to-all-start.3 = ((f32[768,4,384]{2,0,1:T(8,128)}), f32[768,4,384]{2,0,1:T(8,128)}, u32[]{:S(2)}, u32[]{:S(2)}) async-start(f32[768,4,384]{2,0,1:T(8,128)} %bitcast.585), calls=%async_computation.3 | async-start | bytes 9437184 | tf_op jit(solution)/shard_map/all_to_all | solution.py:211
  (142 other events, 295.4 us)
Sparse Core Ops, SparseCore 0:
  10.7 117.8 all-gather.6
  130.7 40.6 all-gather.8
  735.5 92.0 all-reduce.10
  829.5 60.6 all-gather.10
  892.1 59.0 all-gather.12
  953.2 59.0 all-gather.14
  1027.8 92.6 all-reduce.14
  1122.8 55.8 all-reduce.12
  1688.3 94.0 all-reduce.16
  1786.2 130.1 reduce-scatter.18
  1920.4 162.1 reduce-scatter.8
  2086.9 67.8 reduce-scatter.10
  2159.4 116.9 reduce-scatter.12
  2280.9 117.0 reduce-scatter.14
  2402.4 117.0 reduce-scatter.16
where the time goes:
time: 2550 us; the launch traced here: 2530 us
  waiting for transfers between devices  1100 us (43%)
  matrix products  573 us (22%)
  local copies, waits for them, and re-layouts  386 us (15%)
  other arithmetic  255 us (10%)
  blocking collectives  152 us (6%)
  loops' own time  27.4 us (1%)
    another operation x6, other arithmetic, householder_attention(): jax.scipy.linalg.solve_triangular(system, right_side, lower=True, unit_di...  178 us
    reduce_scatter x1, waiting for transfers between devices, body(): lax.psum_scatter(grad_in, ('dp', 'wid'), scatter_dimension=0, tiled=True)  127 us
    unnamed x2, blocking collectives  125 us
    reduce_scatter x1, waiting for transfers between devices, body(): lax.psum_scatter(grad_gate, ('dp', 'wid'), scatter_dimension=0, tiled=True)  122 us
    reduce_scatter x1, waiting for transfers between devices, body(): lax.psum_scatter(grad_up, ('dp', 'wid'), scatter_dimension=0, tiled=True)  122 us
    reduce_scatter x1, waiting for transfers between devices, body(): lax.psum_scatter(grad_down, ('dp', 'wid'), scatter_dimension=1, tiled=True)  122 us
    unnamed x16, waiting for transfers between devices  119 us
    dot_general x48, matrix products, sweep_step(): jnp.einsum('ihd,jhd->hij', moved_rows, keys_here, precision=highest)  107 us
  transfers between devices with their start and end apart: 19, of which 14 were waited for; matrix products, arithmetic and copies ran while one was open for 26% of the time, Pallas kernels for 0%

commit v1 on v0

v1 whole, which is shorter than its diff:
```python
import jax, jax.numpy as jnp
from jax import lax
from jax.experimental import pallas as pl
from jax.experimental.pallas import tpu as pltpu
from jax.sharding import PartitionSpec as P

HD = 128
F32 = jnp.float32
BF = jnp.bfloat16


def split(a):
    hi = a.astype(BF)
    return hi, (a - hi.astype(F32)).astype(BF)


def mm(a, b, ca, cb):
    dims = (((ca,), (cb,)), ((), ()))

    def one(x, y):
        return lax.dot_general(x, y, dims, preferred_element_type=F32)

    if isinstance(a, tuple) and isinstance(b, tuple):
        return one(a[0], b[0]) + (one(a[0], b[1]) + one(a[1], b[0]))
    if isinstance(a, tuple):
        return one(a[0], b) + one(a[1], b)
    if isinstance(b, tuple):
        return one(a, b[0]) + one(a, b[1])
    return one(a, b)


def beside(items):
    return tuple(jnp.concatenate([i[p] for i in items], axis=1) for p in range(2))


def cat(items):
    return tuple(jnp.concatenate([i[p] for i in items], axis=0) for p in range(2))


def grids(size):
    return (
        lax.broadcasted_iota(jnp.int32, (size, size), 0),
        lax.broadcasted_iota(jnp.int32, (size, size), 1),
    )


def to_col(row, eye):
    return jnp.sum(jnp.where(eye, row, 0.0), axis=1, keepdims=True)


def strengths(gram, logit_row, eye):
    square = jnp.where(eye, gram, 0.0)
    sig_row = 1.0 / (jnp.sum(square, axis=0, keepdims=True) + 1e-06)
    sig_col = 1.0 / (jnp.sum(square, axis=1, keepdims=True) + 1e-06)
    beta_row = 2.0 * jax.nn.sigmoid(logit_row)
    beta_col = to_col(beta_row, eye)
    return sig_row, sig_col, beta_row, beta_col


def inverses(lows, rows, cols, eye):
    invs = [jnp.where(eye, 1.0, jnp.where((rows ^ cols) == 1, -low, 0.0)) for low in lows]
    size = 2
    while size < rows.shape[0]:
        pair = (rows // size ^ cols // size) == 1
        parts = [split(inv) for inv in invs]
        offs = [split(jnp.where(pair, low, 0.0)) for low in lows]
        mids = [split(mm(off, part, 1, 0)) for off, part in zip(offs, parts)]
        invs = [inv - mm(part, mid, 1, 0) for inv, part, mid in zip(invs, parts, mids)]
        size *= 2
    return invs


def fwd_kernel(proj_ref, lg_ref, seg_ref, att_ref, pr_ref, qm_ref, x_ref, ft_ref, e_ref, kt_ref, p_ref, s_ref):
    length, width = att_ref.shape
    q_ref, k_ref, v_ref, r_ref = (proj_ref.at[:, n * width : (n + 1) * width] for n in range(4))
    blocks = length // width
    rows, cols = grids(width)
    eye = rows == cols
    lows, scales = [], []
    for c in range(blocks):
        r = r_ref[c * width : (c + 1) * width, :]
        gram = mm(r, r, 1, 1)
        sig_row, sig_col, beta_row, beta_col = strengths(gram, lg_ref[0, :, c * width : (c + 1) * width], eye)
        lows.append(jnp.where(rows > cols, gram * (beta_col * sig_col), 0.0))
        scales.append(beta_row * sig_row)
    invs = inverses(lows, rows, cols, eye)

    def chunk(c):
        at = pl.ds(pl.multiple_of(c * width, width), width)
        q, k, r = q_ref[at, :], k_ref[at, :], r_ref[at, :]
        prods = mm(jnp.concatenate([q, k], axis=0), r, 1, 1)
        qr, kr = prods[:width], prods[width : 2 * width]
        inv = invs[c]
        tri = split(inv * scales[c])
        qrl = split(jnp.where(rows >= cols, qr, 0.0))
        kru = split(jnp.where(rows < cols, kr, 0.0))
        ft = mm(kru, tri, 1, 1)
        e = mm(qrl, tri, 1, 0)
        fts, es = split(ft), split(e)
        moved = mm(cat([fts, es, tri]), r, 1, 0)
        s_ref[at, at] = mm(q, k, 1, 1) - mm(qrl, fts, 1, 1)
        kt_ref[0, at, :] = k.astype(F32) - moved[:width]
        qm_ref[0, c, at, :] = q.astype(F32) - moved[width : 2 * width]
        p_ref[0, at, :] = jnp.where(eye, 1.0, 0.0) - mm(r, split(moved[2 * width :]), 0, 0)
        x_ref[0, at, :] = inv
        ft_ref[0, at, :] = ft
        e_ref[0, at, :] = e

    for c in range(blocks):
        chunk(c)

    for j in range(blocks - 1, -1, -1):
        here = pl.ds(j * width, width)
        if j < blocks - 1:
            below = pl.ds((j + 1) * width, length - (j + 1) * width)
            moved = split(qm_ref[0, j, below, :])
            s_ref[below, here] = mm(moved, split(kt_ref[0, here, :]), 1, 1)
            if j:
                qm_ref[0, j - 1, below, :] = mm(moved, split(p_ref[0, here, :]), 1, 0)
        if j:
            qm_ref[0, j - 1, here, :] = qm_ref[0, j, here, :]

    seg_row = seg_ref[0:1, :].astype(F32)
    for i in range(blocks):
        here = pl.ds(i * width, width)
        upto = (i + 1) * width
        seg_col = to_col(seg_row[:, i * width : upto], eye)
        row = lax.broadcasted_iota(jnp.int32, (width, upto), 0) + i * width
        col = lax.broadcasted_iota(jnp.int32, (width, upto), 1)
        ok = (col <= row) & (seg_col == seg_row[:, :upto])
        score = jnp.where(ok, s_ref[here, :upto] * width ** (-0.5), -1e30)
        top = jnp.max(score, axis=1, keepdims=True)
        ex = jnp.exp(score - top)
        prob = ex / jnp.sum(ex, axis=1, keepdims=True)
        pr_ref[0, here, :upto] = prob
        att_ref[here, :] = mm(split(prob), v_ref[:upto, :], 1, 0).astype(att_ref.dtype)


def attend_fwd(proj, logits, seg):
    length, wide = proj.shape
    heads = wide // (4 * HD)
    blocks = length // HD
    part = pl.BlockSpec((length, 4 * HD), lambda h: (0, h))
    per = pl.BlockSpec((1, length, HD), lambda h: (h, 0, 0))
    st = jax.ShapeDtypeStruct
    return pl.pallas_call(
        fwd_kernel,
        grid=(heads,),
        in_specs=[part,
                  pl.BlockSpec((1, 1, length), lambda h: (h, 0, 0)),
                  pl.BlockSpec((1, length), lambda h: (0, 0))],
        out_specs=[pl.BlockSpec((length, HD), lambda h: (0, h)),
                   pl.BlockSpec((1, length, length), lambda h: (h, 0, 0)),
                   pl.BlockSpec((1, blocks, length, HD), lambda h: (h, 0, 0, 0)),
                   per, per, per, per, per],
        out_shape=[st((length, heads * HD), BF), st((heads, length, length), F32),
                   st((heads, blocks, length, HD), F32)] + [st((heads, length, HD), F32)] * 5,
        scratch_shapes=[pltpu.VMEM((length, length), F32)],
        compiler_params=pltpu.CompilerParams(vmem_limit_bytes=56 << 20, dimension_semantics=("arbitrary",)),
        name="attend_fwd",
    )(proj, logits.reshape(heads, 1, length), seg)


def bwd_kernel(proj_ref, lg_ref, do_ref, pr_ref, qm_ref, x_ref, ft_ref, e_ref, kt_ref, p_ref,
               dproj_ref, dl_ref, ds_ref, dkt_ref, dqt_ref, dp_ref):
    length, width = do_ref.shape
    q_ref, k_ref, v_ref, r_ref = (proj_ref.at[:, n * width : (n + 1) * width] for n in range(4))
    dq_ref, dk_ref, dv_ref, dr_ref = (dproj_ref.at[:, n * width : (n + 1) * width] for n in range(4))
    blocks = length // width
    rows, cols = grids(width)
    eye = rows == cols

    for i in range(blocks):
        here = pl.ds(i * width, width)
        upto = (i + 1) * width
        prob = pr_ref[0, here, :upto]
        dprob = mm(split(do_ref[here, :]), v_ref[:upto, :], 1, 1)
        delta = jnp.sum(prob * dprob, axis=1, keepdims=True)
        ds_ref[here, :upto] = prob * (dprob - delta) * width ** (-0.5)
    for j in range(blocks):
        here = pl.ds(j * width, width)
        below = pl.ds(j * width, length - j * width)
        dv_ref[here, :] = mm(split(pr_ref[0, below, here]), split(do_ref[below, :]), 0, 0).astype(dv_ref.dtype)

    zero = jnp.zeros((width, width), F32)
    dqt_ref[0:width, :] = zero
    dp_ref[0:width, :] = zero
    last = pl.ds((blocks - 1) * width, width)
    dkt_ref[last, :] = zero
    dp_ref[last, :] = zero
    grad = None
    for j in range(blocks - 1):
        here = pl.ds(j * width, width)
        below = pl.ds((j + 1) * width, length - (j + 1) * width)
        dsj = split(ds_ref[below, here])
        moved = split(qm_ref[0, j, below, :])
        dkt_ref[here, :] = mm(dsj, moved, 0, 0)
        fresh = mm(dsj, split(kt_ref[0, here, :]), 1, 0)
        if j:
            old = split(grad)
            dp_ref[here, :] = mm(moved, old, 0, 0)
            fresh = fresh + mm(old, split(p_ref[0, here, :]), 1, 1)
        dqt_ref[pl.ds((j + 1) * width, width), :] = fresh[:width]
        grad = fresh[width:]

    def chunk(c):
        at = pl.ds(pl.multiple_of(c * width, width), width)
        q, k, r = q_ref[at, :], k_ref[at, :], r_ref[at, :]
        prods = mm(jnp.concatenate([r, q, k], axis=0), r, 1, 1)
        gram, qr, kr = prods[:width], prods[width : 2 * width], prods[2 * width :]
        sig_row, sig_col, beta_row, beta_col = strengths(gram, lg_ref[0, :, at], eye)
        inv = x_ref[0, at, :]
        tri_full = inv * (beta_row * sig_row)
        tri = split(tri_full)
        qrl = split(jnp.where(rows >= cols, qr, 0.0))
        kru = split(jnp.where(rows < cols, kr, 0.0))
        ft, e = split(ft_ref[0, at, :]), split(e_ref[0, at, :])
        dsin = split(ds_ref[at, at])
        dkt_f, dqt_f = dkt_ref[at, :], dqt_ref[at, :]
        dkt, dqt = split(dkt_f), split(dqt_f)
        dp = split(dp_ref[at, :])
        y = split(mm(tri, r, 1, 0))
        dy = split(-mm(r, dp, 1, 0))
        both = mm(cat([dkt, dqt, dy]), r, 1, 1)
        dft = split(-both[:width] - mm(dsin, qrl, 0, 0))
        de = split(-both[width : 2 * width])
        dtri = both[2 * width :] + mm(cat([dft, qrl]), cat([kru, de]), 0, 0)
        dtris = split(dtri)
        dqr = split(jnp.where(rows >= cols, mm(de, tri, 1, 1) - mm(dsin, ft, 1, 0), 0.0))
        dkr = split(jnp.where(rows < cols, mm(dft, tri, 1, 0), 0.0))
        dlow = -mm(split(inv), split(mm(dtris, tri, 1, 1)), 0, 0)
        dlow = jnp.where(rows > cols, dlow, 0.0)
        b_col = beta_col * sig_col
        dgram = split(dlow * b_col)
        db = jnp.sum(dtri * inv, axis=0, keepdims=True)
        db_col = jnp.sum(dlow * gram, axis=1, keepdims=True)
        db = db + jnp.sum(jnp.where(eye, db_col, 0.0), axis=0, keepdims=True)
        dl_ref[0, :, at] = db * sig_row * beta_row * (1.0 - 0.5 * beta_row)
        dst = tuple(jnp.transpose(d) for d in dsin)
        dq = dqt_f + mm(beside([dsin, dqr]), jnp.concatenate([k, r], axis=0), 1, 0)
        dk = dkt_f + mm(beside([dst, dkr]), jnp.concatenate([q, r], axis=0), 1, 0)
        dr = mm(dgram, r, 1, 0) + mm(cat([dqr, dkr, dgram]), jnp.concatenate([q, k, r], axis=0), 0, 0)
        dr = dr - mm(cat([ft, e]), cat([dkt, dqt]), 0, 0) + mm(tri, dy, 0, 0) - mm(y, dp, 1, 1)
        dsig = to_col(db * beta_row, eye)
        dr = dr - (2.0 * dsig * sig_col * sig_col) * r.astype(F32)
        dq_ref[at, :] = dq.astype(dq_ref.dtype)
        dk_ref[at, :] = dk.astype(dk_ref.dtype)
        dr_ref[at, :] = dr.astype(dr_ref.dtype)

    for c in range(blocks):
        chunk(c)


def attend_bwd(proj, logits, saved, grad):
    length, wide = proj.shape
    heads = wide // (4 * HD)
    blocks = length // HD
    part = pl.BlockSpec((length, 4 * HD), lambda h: (0, h))
    per = pl.BlockSpec((1, length, HD), lambda h: (h, 0, 0))
    col = pl.BlockSpec((length, HD), lambda h: (0, h))
    lrow = pl.BlockSpec((1, 1, length), lambda h: (h, 0, 0))
    st = jax.ShapeDtypeStruct
    scr = pltpu.VMEM((length, HD), F32)
    return pl.pallas_call(
        bwd_kernel,
        grid=(heads,),
        in_specs=[part, lrow, col,
                  pl.BlockSpec((1, length, length), lambda h: (h, 0, 0)),
                  pl.BlockSpec((1, blocks, length, HD), lambda h: (h, 0, 0, 0)),
                  per, per, per, per, per],
        out_specs=[part, lrow],
        out_shape=[st((length, wide), BF), st((heads, 1, length), F32)],
        scratch_shapes=[pltpu.VMEM((length, length), F32), scr, scr, scr],
        compiler_params=pltpu.CompilerParams(vmem_limit_bytes=56 << 20, dimension_semantics=("arbitrary",)),
        name="attend_bwd",
    )(proj, logits.reshape(heads, 1, length), grad, *saved)


def after(value, *first):
    return lax.optimization_barrier((value,) + first)[0]


def shift(value, axis, size, by):
    return lax.ppermute(value, axis, [(i, (i + by) % size) for i in range(size)])


def swap(value, axis, size, bit):
    return lax.ppermute(value, axis, [(i, i ^ bit) for i in range(size)])


def norm_back(values, scale_row, gain, grad_out):
    weighted = grad_out * gain
    grad_gain = jnp.sum(grad_out * values * scale_row, axis=0)
    grad_values = scale_row * weighted - values * scale_row**3 * jnp.mean(
        weighted * values, axis=-1, keepdims=True
    )
    return (grad_gain, grad_values)


def make_body(sizes):
    dp, hid, wid = sizes["dp"], sizes["hid"], sizes["wid"]

    def body(
        hidden_in, cotangent, segments, gain_attn, gain_mlp,
        in_weight, beta_weight, out_weight, gate_weight, up_weight, down_weight,
    ):
        me_dp, me_hid, me_wid = (lax.axis_index(a) for a in ("dp", "hid", "wid"))
        tokens, slice_width = hidden_in.shape
        rows = tokens // wid
        quarter = rows // hid
        features = slice_width * wid
        heads = in_weight.shape[2] // HD
        shard = in_weight.shape[0]

        def dot(a, b, ca, cb, out=F32):
            return lax.dot_general(a, b, (((ca,), (cb,)), ((), ())), preferred_element_type=F32).astype(out)

        def to_tokens(array):
            mine = lax.dynamic_index_in_dim(array.reshape(wid, hid, quarter, slice_width), me_hid, 1, keepdims=False)
            return lax.all_to_all(mine.reshape(wid * quarter, slice_width), "wid", split_axis=0, concat_axis=1, tiled=True)

        def gather_hid(own):
            pieces = {0: own}
            bit = hid // 2
            while bit:
                for k in list(pieces):
                    pieces[k | bit] = swap(pieces[k], "hid", hid, bit)
                bit //= 2
            return [pieces[k] for k in range(hid)]

        def sum_hid(make):
            keep, bit = list(range(hid)), 1
            send = [k for k in keep if k & bit]
            keep = [k for k in keep if not k & bit]
            got = swap(make(send).astype(BF), "hid", hid, bit)
            total = make(keep) + got
            bit *= 2
            while bit < hid:
                half = total.shape[0] // 2
                low = [n for n, k in enumerate(keep) if not k & bit]
                high = [n for n, k in enumerate(keep) if k & bit]
                part = lambda ns: jnp.concatenate([total[n * quarter : (n + 1) * quarter] for n in ns], axis=0)
                got = swap(part(high).astype(BF), "hid", hid, bit)
                total = part(low) + got
                keep = [k for k in keep if not k & bit]
                bit *= 2
            return total

        def reorder(array, axis=0):
            size = array.shape[axis] // hid
            return jnp.concatenate(
                [lax.dynamic_slice_in_dim(array, (me_hid ^ j) * size, size, axis) for j in range(hid)], axis=axis
            )

        def gather_wid(own):
            return [own] + [shift(own, "wid", wid, k) for k in range(1, wid)]

        def gather_dp(pieces):
            got = [pieces] + [[shift(p, "dp", dp, k) for p in pieces] for k in range(1, dp)]
            cols = pieces[0].shape[1]
            whole = jnp.zeros((dp * wid, shard, cols), pieces[0].dtype)
            for i in range(dp):
                for k in range(wid):
                    place = ((me_dp + dp - i) % dp) * wid + (me_wid + wid - k) % wid
                    whole = lax.dynamic_update_slice(whole, got[i][k][None], (place, 0, 0))
            return whole.reshape(dp * wid * shard, cols)

        def scatter_grad(left, right):
            width = left.shape[1] // dp

            def part(k):
                cols = lax.dynamic_slice_in_dim(left, ((me_dp + k) % dp) * width, width, 1)
                return dot(cols, right, 0, 0)

            got = [shift(part(k).astype(BF), "dp", dp, k) for k in range(1, dp)]
            mine = part(0)
            for g in got:
                mine = mine + g
            parts = lax.all_to_all(mine.astype(BF), "wid", split_axis=0, concat_axis=0, tiled=True)
            return jnp.sum(parts.reshape(wid, shard, right.shape[1]).astype(F32), axis=0)

        def to_widths(own, dtype):
            mine = lax.all_to_all(own.astype(BF), "wid", split_axis=1, concat_axis=0, tiled=True)
            pieces = gather_hid(mine.reshape(wid, 1, quarter, slice_width))
            stacked = reorder(jnp.concatenate(pieces, axis=1), axis=1)
            return stacked.reshape(tokens, slice_width).astype(dtype)

        by_head = in_weight.reshape(shard, 4, heads, HD).transpose(0, 2, 1, 3).reshape(shard, 4 * heads * HD)
        small = jnp.concatenate([beta_weight, gain_attn[:, None], gain_mlp[:, None]], axis=1)
        small = jnp.pad(small, ((0, 0), (0, HD - small.shape[1])))
        own_in = jnp.concatenate([by_head, small], axis=1)
        own_mlp = jnp.concatenate([gate_weight, up_weight], axis=1)

        token_in = to_tokens(hidden_in)
        parts_in = gather_wid(own_in)
        inputs_all = jnp.concatenate(gather_hid(token_in), axis=0).astype(F32)
        parts_out = gather_wid(after(out_weight, *parts_in).T)
        weight_in = gather_dp(parts_in)
        parts_mlp = gather_wid(after(own_mlp, *parts_in))
        weight_out = gather_dp(parts_out)
        cotangent = after(cotangent, *parts_mlp)
        token_grad = to_tokens(cotangent)
        grad_all = jnp.concatenate(gather_hid(token_grad), axis=0)
        parts_down = gather_wid(after(down_weight, *parts_mlp).T)
        weight_mlp = gather_dp(parts_mlp)
        weight_down = gather_dp(parts_down)

        width_in = 4 * heads * HD
        weight_beta = weight_in[:, width_in : width_in + heads]
        gain_one = weight_in[:, width_in + heads].astype(F32)
        gain_two = weight_in[:, width_in + heads + 1].astype(F32)
        weight_in = weight_in[:, :width_in]

        scale_all = lax.rsqrt(jnp.mean(inputs_all * inputs_all, axis=-1, keepdims=True) + 1e-06)
        normed = (inputs_all * scale_all * gain_one).astype(BF)
        projected = reorder(dot(normed, weight_in, 1, 0, BF))
        logits = reorder(dot(normed, weight_beta, 1, 0)).T
        attended, *saved = attend_fwd(projected, logits, segments)
        attended = reorder(attended)

        def rows_of(array, ks):
            return jnp.concatenate([array[k * quarter : (k + 1) * quarter] for k in ks], axis=0)

        branch = sum_hid(lambda ks: dot(rows_of(attended, ks), weight_out, 1, 1))
        inputs = inputs_all[:quarter]
        scale_one = scale_all[:quarter]
        middle = inputs + branch
        scale_two = lax.rsqrt(jnp.mean(middle * middle, axis=-1, keepdims=True) + 1e-06)
        mixed = jnp.concatenate(gather_hid((middle * scale_two * gain_two).astype(BF)), axis=0)
        gate_up = dot(mixed, weight_mlp, 1, 0)
        hidden = gate_up.shape[1] // 2
        gate, upward = gate_up[:, :hidden], gate_up[:, hidden:]
        sigmoid_gate = jax.nn.sigmoid(gate)
        silu_gate = gate * sigmoid_gate
        product = (silu_gate * upward).astype(BF)

        grad_product = dot(grad_all, weight_down, 1, 0)
        grad_gate_pre = grad_product * upward * sigmoid_gate * (1.0 + gate * (1.0 - sigmoid_gate))
        grad_pre = jnp.concatenate([grad_gate_pre.astype(BF), (grad_product * silu_gate).astype(BF)], axis=1)
        grad_mixed = sum_hid(lambda ks: dot(rows_of(grad_pre, ks), weight_mlp, 1, 1))
        grad_down = scatter_grad(grad_all, product)
        grad_mlp = scatter_grad(mixed, grad_pre)

        grad_gain_two, grad_middle = norm_back(middle, scale_two, gain_two, grad_mixed)
        grad_middle = grad_middle + token_grad.astype(F32)
        grad_branch = jnp.concatenate(gather_hid(grad_middle.astype(BF)), axis=0)
        grad_attended = reorder(dot(grad_branch, weight_out, 1, 0))
        grad_proj, grad_logit = attend_bwd(projected, logits, saved, grad_attended)
        grad_out = scatter_grad(grad_branch, attended)

        feed = sum_hid(lambda ks: dot(rows_of(product, ks), weight_down, 1, 1))
        output = to_widths(middle + feed, BF)

        grad_proj = reorder(grad_proj)
        logit_parts = jnp.concatenate(split(reorder(grad_logit[:, 0, :].T)), axis=1)
        beta_twice = jnp.concatenate([weight_beta, weight_beta], axis=1)
        grad_normed = sum_hid(
            lambda ks: dot(rows_of(grad_proj, ks), weight_in, 1, 1) + dot(rows_of(logit_parts, ks), beta_twice, 1, 1)
        )
        grad_gain_one, grad_inputs = norm_back(inputs, scale_one, gain_one, grad_normed)
        grad_input = to_widths(grad_inputs + grad_middle, F32)
        grad_in = scatter_grad(normed, grad_proj)
        grad_beta = scatter_grad(normed, logit_parts)
        grad_beta = grad_beta[:, :heads] + grad_beta[:, heads:]
        grad_in = grad_in.reshape(shard, heads, 4, HD).transpose(0, 2, 1, 3).reshape(shard, 4, heads * HD)

        gains = lax.psum(jnp.stack([grad_gain_one, grad_gain_two]), ("dp", "hid", "wid"))
        gains = lax.dynamic_slice_in_dim(gains, (me_dp * wid + me_wid) * shard, shard, 1)
        return (
            output, grad_input, gains[0], gains[1], grad_in, grad_beta, grad_out.T,
            grad_mlp[:, :hidden], grad_mlp[:, hidden:], grad_down.T,
        )

    return body


def solution(mesh):
    by_rows, by_cols = P(("dp", "wid"), "hid"), P("hid", ("dp", "wid"))
    both = P(("dp", "wid"))
    deep = P(("dp", "wid"), None, "hid")
    wide = P("dp", "wid")
    return jax.shard_map(
        make_body(dict(mesh.shape)),
        mesh=mesh,
        in_specs=(wide, wide, P(("dp", "wid"), None), both, both, deep, by_rows, by_cols, by_rows, by_rows, by_cols),
        out_specs=(wide, wide, both, both, deep, by_rows, by_cols, by_rows, by_rows, by_cols),
        check_vma=False,
    )
```

time: 2550 us -> 847 us (0.33)
  waiting for transfers between devices: 1100 us -> 382 us
  matrix products: 573 us -> 87.1 us
  local copies, waits for them, and re-layouts: 386 us -> 75.3 us
  other arithmetic: 255 us -> 47.6 us
  starting transfers between devices: 20.7 us -> 126 us
  blocking collectives: 152 us -> 53.7 us
  Pallas kernels: 0 us -> 63.7 us
  loops' own time: 27.4 us -> 0 us
    reduce_scatter x5 -> x0, waiting for transfers between devices: 561 us -> none  [the longest x1 127 us: body(): lax.psum_scatter(grad_in, ('dp', 'wid'), scatter_dimension=0, tiled=True)]
    dot_general x264 -> x25, matrix products: 560 us -> 87.1 us  [dot(): lax.dot_general(a, b, (((ca,), (cb,)), ((), ())), preferred_element_type=...]
    ppermute x0 -> x59, waiting for transfers between devices: none -> 354 us  [the longest x33 269 us: shift(): lax.ppermute(value, axis, [(i, (i + by) % size) for i in range(size)])]
    psum x4 -> x0, waiting for transfers between devices: 219 us -> none  [the longest x1 78.6 us: body(): grad_mixed = lax.psum(grad_mixed_part, 'hid')]
    another operation x22 -> x1, other arithmetic: 195 us -> 0.01 us  [body(): jnp.stack([grad_gain_one, grad_gain_two])]
    all_gather x5 -> x0, waiting for transfers between devices: 163 us -> none  [the longest x1 54.2 us: body(): lax.all_gather(down_weight, ('dp', 'wid'), axis=1, tiled=True)]
    unnamed x2 -> x0, blocking collectives: 125 us -> none
    unnamed x16 -> x0, waiting for transfers between devices: 119 us -> none
  transfers between devices with their start and end apart: 19 -> 68, of which waited for: 14 -> 27; matrix products, arithmetic and copies ran while one was open for 26% -> 20% of each run, Pallas kernels for 0% -> 8%
where the time goes in v1:
time: 847 us; the launch traced here: 839 us
  waiting for transfers between devices  382 us (45%)
  starting transfers between devices  126 us (15%)
  matrix products  87.1 us (10%)
  local copies, waits for them, and re-layouts  75.3 us (9%)
  Pallas kernels  63.7 us (8%)
  blocking collectives  53.7 us (6%)
  other arithmetic  47.6 us (6%)
    ppermute x33, waiting for transfers between devices, shift(): lax.ppermute(value, axis, [(i, (i + by) % size) for i in range(size)])  269 us
    dot_general x25, matrix products, dot(): lax.dot_general(a, b, (((ca,), (cb,)), ((), ())), preferred_element_type=...  87.1 us
    ppermute x26, waiting for transfers between devices, swap(): return lax.ppermute(value, axis, [(i, i ^ bit) for i in range(size)])  84.7 us
    ppermute x33, starting transfers between devices, shift(): lax.ppermute(value, axis, [(i, (i + by) % size) for i in range(size)])  66.1 us
    psum x1, blocking collectives, body(): lax.psum(jnp.stack([grad_gain_one, grad_gain_two]), ('dp', 'hid', 'wid'))  53.7 us
    dynamic_update_slice x31, local copies, waits for them, and re-layouts, gather_dp(): whole = lax.dynamic_update_slice(whole, got[i][k][None], (place, 0, 0))  34.5 us
    pallas_call x1, Pallas kernels, attend_bwd(): pl.pallas_call(bwd_kernel, grid=(heads,), in_specs=[part, lrow, col, pl.B...  34.4 us
    pallas_call x1, Pallas kernels, attend_fwd(): pl.pallas_call(fwd_kernel, grid=(heads,), in_specs=[part, pl.BlockSpec((1...  29.4 us
  transfers between devices with their start and end apart: 68, of which 27 were waited for; matrix products, arithmetic and copies ran while one was open for 20% of the time, Pallas kernels for 8%

profile of v1, /device:TPU:0, one launch (start us, length us, event | category | flops | bytes accessed | tf_op | source)
XLA Modules:
  0.0 838.8 jit_solution(4304571246202130059)
XLA Ops:
  9.1 3.0 collective-permute-start.3
  12.1 2.6 collective-permute-start.4
  18.4 3.5 all-to-all-start
  24.4 5.3 collective-permute-done.3
  29.8 27.4 %collective-permute-done.4 = bf16[192,1664]{1,0:T(8,128)(2,1)} collective-permute-done((bf16[192,1664]{1,0:T(8,128)(2,1)}, bf16[192,1664]{1,0:T(8,128)(2,1)}, u32[]{:S(2)}, u32[]{:S(2)}) %collective-permute-start.4) | collective-permute-done | bytes 639008 | tf_op jit(solution)/shard_map/ppermute | solution.py:284
  57.2 19.7 %collective-permute-start.22 = (bf16[192,2048]{1,0:T(8,128)(2,1)}, bf16[192,2048]{1,0:T(8,128)(2,1)}, u32[]{:S(2)}, u32[]{:S(2)}) collective-permute-start(bf16[192,2048]{1,0:T(8,128)(2,1)} %pad_maximum_fusion.12), channel_id=1, source_target_pairs={{0,1},{1,2},{2,3},{3,0},{4,5},{5,6},{6,7},{7,4},{8,9},{9,10},{10,1... | collective-permute-start | bytes 2359304 | tf_op jit(solution)/shard_map/ppermute | solution.py:284
  76.9 2.6 collective-permute-start.23
  81.6 3.4 broadcast_in_dim.142
  92.3 41.0 %collective-permute-done.10 = bf16[192,384]{1,0:T(8,128)(2,1)S(1)} collective-permute-done((bf16[192,384]{1,0:T(8,128)(2,1)S(1)}, bf16[192,384]{1,0:T(8,128)(2,1)S(1)}, u32[]{:S(2)}, u32[]{:S(2)}) %collective-permute-start.10) | collective-permute-done | bytes 147488 | tf_op jit(solution)/shard_map/ppermute | solution.py:284
  133.4 26.1 %collective-permute-done.11 = bf16[192,384]{1,0:T(8,128)(2,1)S(1)} collective-permute-done((bf16[192,384]{1,0:T(8,128)(2,1)S(1)}, bf16[192,384]{1,0:T(8,128)(2,1)S(1)}, u32[]{:S(2)}, u32[]{:S(2)}) %collective-permute-start.11) | collective-permute-done | bytes 147488 | tf_op jit(solution)/shard_map/ppermute | solution.py:284
  167.9 14.1 %collective-permute-done.14 = bf16[192,384]{1,0:T(8,128)(2,1)S(1)} collective-permute-done((bf16[192,384]{1,0:T(8,128)(2,1)S(1)}, bf16[192,384]{1,0:T(8,128)(2,1)S(1)}, u32[]{:S(2)}, u32[]{:S(2)}) %collective-permute-start.14) | collective-permute-done | bytes 147488 | tf_op jit(solution)/shard_map/ppermute | solution.py:284
  183.6 3.6 collective-permute-done.15
  188.7 4.4 collective-permute-done.16
  196.2 14.5 %collective-permute-done.8 = bf16[192,1664]{1,0:T(8,128)(2,1)S(1)} collective-permute-done((bf16[192,1664]{1,0:T(8,128)(2,1)}, bf16[192,1664]{1,0:T(8,128)(2,1)S(1)}, u32[]{:S(2)}, u32[]{:S(2)}) %collective-permute-start.8) | collective-permute-done | bytes 639008 | tf_op jit(solution)/shard_map/ppermute | solution.py:284
  213.1 11.3 %collective-permute-done.9 = bf16[192,1664]{1,0:T(8,128)(2,1)S(1)} collective-permute-done((bf16[192,1664]{1,0:T(8,128)(2,1)}, bf16[192,1664]{1,0:T(8,128)(2,1)S(1)}, u32[]{:S(2)}, u32[]{:S(2)}) %collective-permute-start.9) | collective-permute-done | bytes 639008 | tf_op jit(solution)/shard_map/ppermute | solution.py:284
  228.6 2.8 collective-permute-start.29
  231.3 2.6 collective-permute-start.30
  235.9 4.2 all-to-all-start.2
  246.3 4.0 collective-permute-start.31
  259.3 7.2 collective-permute-done.30
  279.0 4.0 fusion.6
  285.5 29.4 %attend_fwd.1 = (bf16[768,384]{1,0:T(8,128)(2,1)}, f32[3,768,768]{2,1,0:T(8,128)}, f32[3,6,768,128]{3,2,1,0:T(8,128)}, f32[3,768,128]{2,1,0:T(8,128)}, f32[3,768...) custom-call(bf16[768,1536]{1,0:T(8,128)(2,1)} %pad_maximum_fusion.1.proj_ref, ...), custom_call_target="tpu_custom_call" | custom-call | tf_op jit(solution)/shard_map/attend_fwd/pallas_call | solution.py:146
  317.9 2.8 maximum_convert_fusion
  334.2 10.2 %collective-permute-done.18 = bf16[192,1536]{1,0:T(8,128)(2,1)} collective-permute-done((bf16[192,1536]{1,0:T(8,128)(2,1)S(1)}, bf16[192,1536]{1,0:T(8,128)(2,1)}, u32[]{:S(2)}, u32[]{:S(2)}) %collective-permute-start.18) | collective-permute-done | bytes 589856 | tf_op jit(solution)/shard_map/ppermute | solution.py:288
  351.5 5.5 collective-permute-done.42
  357.6 11.0 %collective-permute-done.20 = bf16[192,1536]{1,0:T(8,128)(2,1)S(1)} collective-permute-done((bf16[192,1536]{1,0:T(8,128)(2,1)S(1)}, bf16[192,1536]{1,0:T(8,128)(2,1)S(1)}, u32[]{:S(2)}, u32[]{:S(2)}) %collective-permute-start.20) | collective-permute-done | bytes 589856 | tf_op jit(solution)/shard_map/ppermute | solution.py:288
  370.6 7.4 fusion.119
  378.0 5.9 multiply_convert_fusion.1
  386.1 6.6 convolution_convert_fusion.2
  393.8 4.4 convolution_convert_fusion.3
  398.6 6.2 convolution_add_fusion.1
  405.6 3.8 convolution_add_fusion.2
  411.0 2.7 convolution_convert_fusion.5
  414.3 6.8 collective-permute-done.45
  422.3 10.7 %collective-permute-done.37 = bf16[192,1536]{1,0:T(8,128)(2,1)S(1)} collective-permute-done((bf16[192,1536]{1,0:T(8,128)(2,1)S(1)}, bf16[192,1536]{1,0:T(8,128)(2,1)S(1)}, u32[]{:S(2)}, u32[]{:S(2)}) %collective-permute-start.37) | collective-permute-done | bytes 589856 | tf_op jit(solution)/shard_map/ppermute | solution.py:288
  435.5 14.3 %collective-permute-done.47 = bf16[192,1536]{1,0:T(8,128)(2,1)S(1)} collective-permute-done((bf16[192,1536]{1,0:T(8,128)(2,1)}, bf16[192,1536]{1,0:T(8,128)(2,1)S(1)}, u32[]{:S(2)}, u32[]{:S(2)}) %collective-permute-start.47) | collective-permute-done | bytes 589856 | tf_op jit(solution)/shard_map/ppermute | solution.py:288
  451.7 4.9 add_convert_fusion.2
  457.4 14.2 %all-to-all-start.1 = ((bf16[192,4,384]{2,0,1:T(8,128)(2,1)}), bf16[192,4,384]{2,0,1:T(8,128)(2,1)S(1)}, u32[]{:S(2)}, u32[]{:S(2)}) async-start(bf16[192,4,384]{2,0,1:T(8,128)(2,1)} %bitcast.156), calls=%async_computation.1 | async-start | bytes 1179648 | tf_op jit(solution)/shard_map/all_to_all | solution.py:383
  476.1 34.4 %attend_bwd.1 = (bf16[768,1536]{1,0:T(8,128)(2,1)}, f32[3,1,768]{2,1,0:T(1,128)}) custom-call(bf16[768,1536]{1,0:T(8,128)(2,1)} %pad_maximum_fusion.1.proj_ref, f32[3,1,768]{2,1,0:T(1,128)} %reshape.181.lg_ref, f32[768,384]{1,0:T(8,128)} %pad_maximum_fusion.11.do_ref, f32[3,768,768]{2,1,0:T(8,128)} %get-tuple-element.29.pr_ref, ...), custom_call_target="tpu_custom_call" | custom-call | tf_op jit(solution)/shard_map/attend_bwd/pallas_call | solution.py:264
  512.6 2.9 constant_dynamic-slice_fusion.12
  521.0 5.3 all-to-all-start.5
  526.3 6.3 fusion.19
  532.7 5.2 all-to-all-start.8
  539.6 6.9 convolution_convert_fusion
  550.1 3.3 fusion.16
  556.2 73.2 %collective-permute-done.56 = bf16[768,384]{1,0:T(8,128)(2,1)S(1)} collective-permute-done((bf16[768,384]{1,0:T(8,128)(2,1)S(1)}, bf16[768,384]{1,0:T(8,128)(2,1)S(1)}, u32[]{:S(2)}, u32[]{:S(2)}) %collective-permute-start.56) | collective-permute-done | bytes 589856 | tf_op jit(solution)/shard_map/ppermute | solution.py:284
  631.1 5.0 all-to-all-start.6
  636.0 2.4 multiply_reduce_fusion.2
  641.3 9.8 %all-to-all-done.6 = bf16[4,192,384]{2,1,0:T(8,128)(2,1)} async-done(((bf16[4,192,384]{2,1,0:T(8,128)(2,1)}), bf16[4,192,384]{2,1,0:T(8,128)(2,1)}, u32[]{:S(2)}, u32[]{:S(2)}) %all-to-all-start.6) | async-done | bytes 589856 | tf_op jit(solution)/shard_map/all_to_all | solution.py:379
  651.1 3.5 all-to-all-start.3
  654.6 7.5 add_convert_fusion
  662.1 7.8 all-to-all-done.3
  669.9 4.9 all-to-all-start.7
  674.9 3.8 convolution_convert_fusion.1
  680.6 13.6 %collective-permute-done.39 = bf16[4,1,192,384]{3,2,1,0:T(8,128)(2,1)} collective-permute-done((bf16[4,1,192,384]{3,2,1,0:T(8,128)(2,1)S(1)}, bf16[4,1,192,384]{3,2,1,0:T(8,128)(2,1)}, u32[]{:S(2)}, u32[]{:S(2)}) %collective-permute-start.39) | collective-permute-done | bytes 589856 | tf_op jit(solution)/shard_map/ppermute | solution.py:288
  694.2 36.7 %collective-permute-done.54 = bf16[768,1536]{1,0:T(8,128)(2,1)S(1)} collective-permute-done((bf16[768,1536]{1,0:T(8,128)(2,1)S(1)}, bf16[768,1536]{1,0:T(8,128)(2,1)S(1)}, u32[]{:S(2)}, u32[]{:S(2)}) %collective-permute-start.54) | collective-permute-done | bytes 2359328 | tf_op jit(solution)/shard_map/ppermute | solution.py:284
  731.0 3.4 add_convert_fusion.1
  734.4 10.7 %all-to-all-done.7 = bf16[4,192,2048]{2,1,0:T(8,128)(2,1)} async-done(((bf16[4,192,2048]{2,1,0:T(8,128)(2,1)}), bf16[4,192,2048]{2,1,0:T(8,128)(2,1)}, u32[]{:S(2)}, u32[]{:S(2)}) %all-to-all-start.7) | async-done | bytes 3145760 | tf_op jit(solution)/shard_map/all_to_all | solution.py:379
  745.0 4.7 all-to-all-start.4
  753.5 10.6 %collective-permute-done.52 = bf16[4,1,192,384]{3,2,1,0:T(8,128)(2,1)} collective-permute-done((bf16[4,1,192,384]{3,2,1,0:T(8,128)(2,1)S(1)}, bf16[4,1,192,384]{3,2,1,0:T(8,128)(2,1)}, u32[]{:S(2)}, u32[]{:S(2)}) %collective-permute-start.52) | collective-permute-done | bytes 589856 | tf_op jit(solution)/shard_map/ppermute | solution.py:288
  764.2 2.6 convert_reduce_fusion.2
  768.7 53.7 %psum.7 = f32[2,1536]{1,0:T(2,128)} all-reduce(f32[2,1536]{1,0:T(2,128)S(1)} %pad_maximum_fusion.23), channel_id=1, replica_groups=mesh['dp'=2,'hid'=4,'wid'=4] {'dp','hid','wid'}, use_global_device_ids=true, to_apply=%region_6.7 | all-reduce | flops 3072 | bytes 24576 | tf_op jit(solution)/shard_map/psum | solution.py:467
  828.1 2.7 bitcast_convert_fusion
  830.8 2.7 convert_reduce_fusion
  (365 shorter events, 158.4 us)
Async XLA Ops:
  9.1 20.7 %collective-permute-start.3 = (bf16[192,1664]{1,0:T(8,128)(2,1)}, bf16[192,1664]{1,0:T(8,128)(2,1)}, u32[]{:S(2)}, u32[]{:S(2)}) collective-permute-start(bf16[192,1664]{1,0:T(8,128)(2,1)} %fusion.69), channel_id=1, source_target_pairs={{0,1},{1,2},{2,3},{3,0},{4,5},{5,6},{6,7},{7,4},{8,9},{9,10},{10,1... | collective-permute-start | bytes 1916936 | tf_op jit(solution)/shard_map/ppermute | solution.py:284
  12.1 45.1 %collective-permute-start.4 = (bf16[192,1664]{1,0:T(8,128)(2,1)}, bf16[192,1664]{1,0:T(8,128)(2,1)}, u32[]{:S(2)}, u32[]{:S(2)}) collective-permute-start(bf16[192,1664]{1,0:T(8,128)(2,1)} %fusion.69), channel_id=1, source_target_pairs={{0,2},{1,3},{2,0},{3,1},{4,6},{5,7},{6,4},{7,5},{8,10},{9,11},{10,... | collective-permute-start | bytes 1916936 | tf_op jit(solution)/shard_map/ppermute | solution.py:284
  14.7 42.5 %collective-permute-start.5 = (bf16[192,1664]{1,0:T(8,128)(2,1)}, bf16[192,1664]{1,0:T(8,128)(2,1)}, u32[]{:S(2)}, u32[]{:S(2)}) collective-permute-start(bf16[192,1664]{1,0:T(8,128)(2,1)} %fusion.69), channel_id=1, source_target_pairs={{0,3},{1,0},{2,1},{3,2},{4,7},{5,4},{6,5},{7,6},{8,11},{9,8},{10,9... | collective-permute-start | bytes 1916936 | tf_op jit(solution)/shard_map/ppermute | solution.py:284
  16.0 74.6 %collective-permute-start.6 = (bf16[192,1664]{1,0:T(8,128)(2,1)}, bf16[192,1664]{1,0:T(8,128)(2,1)}, u32[]{:S(2)}, u32[]{:S(2)}) collective-permute-start(bf16[192,1664]{1,0:T(8,128)(2,1)} %fusion.69), channel_id=1, source_target_pairs={{0,16},{16,0},{1,17},{17,1},{2,18},{18,2},{3,19},{19,3},{4,20},{20... | collective-permute-start | bytes 1916936 | tf_op jit(solution)/shard_map/ppermute | solution.py:284
  18.4 149.4 %all-to-all-start = ((bf16[4,192,384]{2,1,0:T(8,128)(2,1)}), bf16[4,192,384]{2,1,0:T(8,128)(2,1)S(1)}, u32[]{:S(2)}, u32[]{:S(2)}) async-start(bf16[4,192,384]{2,1,0:T(8,128)(2,1)} %dynamic-slice_bitcast_fusion.1), calls=%async_computation | async-start | bytes 1179648 | tf_op jit(solution)/shard_map/all_to_all | solution.py:320
  57.2 171.3 %collective-permute-start.22 = (bf16[192,2048]{1,0:T(8,128)(2,1)}, bf16[192,2048]{1,0:T(8,128)(2,1)}, u32[]{:S(2)}, u32[]{:S(2)}) collective-permute-start(bf16[192,2048]{1,0:T(8,128)(2,1)} %pad_maximum_fusion.12), channel_id=1, source_target_pairs={{0,1},{1,2},{2,3},{3,0},{4,5},{5,6},{6,7},{7,4},{8,9},{9,10},{10,1... | collective-permute-start | bytes 2359304 | tf_op jit(solution)/shard_map/ppermute | solution.py:284
  76.9 151.6 %collective-permute-start.23 = (bf16[192,2048]{1,0:T(8,128)(2,1)}, bf16[192,2048]{1,0:T(8,128)(2,1)}, u32[]{:S(2)}, u32[]{:S(2)}) collective-permute-start(bf16[192,2048]{1,0:T(8,128)(2,1)} %pad_maximum_fusion.12), channel_id=1, source_target_pairs={{0,2},{1,3},{2,0},{3,1},{4,6},{5,7},{6,4},{7,5},{8,10},{9,11},{10,... | collective-permute-start | bytes 2359304 | tf_op jit(solution)/shard_map/ppermute | solution.py:284
  79.5 149.0 %collective-permute-start.24 = (bf16[192,2048]{1,0:T(8,128)(2,1)}, bf16[192,2048]{1,0:T(8,128)(2,1)}, u32[]{:S(2)}, u32[]{:S(2)}) collective-permute-start(bf16[192,2048]{1,0:T(8,128)(2,1)} %pad_maximum_fusion.12), channel_id=1, source_target_pairs={{0,3},{1,0},{2,1},{3,2},{4,7},{5,4},{6,5},{7,6},{8,11},{9,8},{10,9... | collective-permute-start | bytes 2359304 | tf_op jit(solution)/shard_map/ppermute | solution.py:284
  79.5 53.8 %collective-permute-start.10 = (bf16[192,384]{1,0:T(8,128)(2,1)S(1)}, bf16[192,384]{1,0:T(8,128)(2,1)S(1)}, u32[]{:S(2)}, u32[]{:S(2)}) collective-permute-start(bf16[192,384]{1,0:T(8,128)(2,1)S(1)} %bitcast.207), channel_id=1, source_target_pairs={{0,1},{1,2},{2,3},{3,0},{4,5},{5,6},{6,7},{7,4},{8,9},{9,10},{10,1... | collective-permute-start | bytes 442376 | tf_op jit(solution)/shard_map/ppermute | solution.py:284
  90.6 68.9 %collective-permute-start.11 = (bf16[192,384]{1,0:T(8,128)(2,1)S(1)}, bf16[192,384]{1,0:T(8,128)(2,1)S(1)}, u32[]{:S(2)}, u32[]{:S(2)}) collective-permute-start(bf16[192,384]{1,0:T(8,128)(2,1)S(1)} %bitcast.208), channel_id=1, source_target_pairs={{0,2},{1,3},{2,0},{3,1},{4,6},{5,7},{6,4},{7,5},{8,10},{9,11},{10,... | collective-permute-start | bytes 442376 | tf_op jit(solution)/shard_map/ppermute | solution.py:284
  133.3 29.2 %collective-permute-start.12 = (bf16[192,384]{1,0:T(8,128)(2,1)S(1)}, bf16[192,384]{1,0:T(8,128)(2,1)S(1)}, u32[]{:S(2)}, u32[]{:S(2)}) collective-permute-start(bf16[192,384]{1,0:T(8,128)(2,1)S(1)} %bitcast.209), channel_id=1, source_target_pairs={{0,3},{1,0},{2,1},{3,2},{4,7},{5,4},{6,5},{7,6},{8,11},{9,8},{10,9... | collective-permute-start | bytes 442376 | tf_op jit(solution)/shard_map/ppermute | solution.py:284
  159.5 6.7 collective-permute-start.13
  162.6 32.1 %collective-permute-start.7 = (bf16[192,1664]{1,0:T(8,128)(2,1)}, bf16[192,1664]{1,0:T(8,128)(2,1)S(1)}, u32[]{:S(2)}, u32[]{:S(2)}) collective-permute-start(bf16[192,1664]{1,0:T(8,128)(2,1)} %collective-permute-done.3), channel_id=1, source_target_pairs={{0,16},{16,0},{1,17},{17,1},{2,18},{18,2},{3,19},{19,3},{4,20},{20... | collective-permute-start | bytes 1916936 | tf_op jit(solution)/shard_map/ppermute | solution.py:284
  166.2 15.8 %collective-permute-start.14 = (bf16[192,384]{1,0:T(8,128)(2,1)S(1)}, bf16[192,384]{1,0:T(8,128)(2,1)S(1)}, u32[]{:S(2)}, u32[]{:S(2)}) collective-permute-start(bf16[192,384]{1,0:T(8,128)(2,1)S(1)} %collective-permute-done.10), channel_id=1, source_target_pairs={{0,16},{16,0},{1,17},{17,1},{2,18},{18,2},{3,19},{19,3},{4,20},{20... | collective-permute-start | bytes 442376 | tf_op jit(solution)/shard_map/ppermute | solution.py:284
  193.1 17.5 %collective-permute-start.8 = (bf16[192,1664]{1,0:T(8,128)(2,1)}, bf16[192,1664]{1,0:T(8,128)(2,1)S(1)}, u32[]{:S(2)}, u32[]{:S(2)}) collective-permute-start(bf16[192,1664]{1,0:T(8,128)(2,1)} %collective-permute-done.4), channel_id=1, source_target_pairs={{0,16},{16,0},{1,17},{17,1},{2,18},{18,2},{3,19},{19,3},{4,20},{20... | collective-permute-start | bytes 1916936 | tf_op jit(solution)/shard_map/ppermute | solution.py:284
  194.7 29.6 %collective-permute-start.9 = (bf16[192,1664]{1,0:T(8,128)(2,1)}, bf16[192,1664]{1,0:T(8,128)(2,1)S(1)}, u32[]{:S(2)}, u32[]{:S(2)}) collective-permute-start(bf16[192,1664]{1,0:T(8,128)(2,1)} %collective-permute-done.5), channel_id=1, source_target_pairs={{0,16},{16,0},{1,17},{17,1},{2,18},{18,2},{3,19},{19,3},{4,20},{20... | collective-permute-start | bytes 1916936 | tf_op jit(solution)/shard_map/ppermute | solution.py:284
  210.7 35.7 %collective-permute-start.25 = (bf16[192,2048]{1,0:T(8,128)(2,1)}, bf16[192,2048]{1,0:T(8,128)(2,1)}, u32[]{:S(2)}, u32[]{:S(2)}) collective-permute-start(bf16[192,2048]{1,0:T(8,128)(2,1)} %pad_maximum_fusion.12), channel_id=1, source_target_pairs={{0,16},{16,0},{1,17},{17,1},{2,18},{18,2},{3,19},{19,3},{4,20},{20... | collective-permute-start | bytes 2359304 | tf_op jit(solution)/shard_map/ppermute | solution.py:284
  224.4 34.4 %collective-permute-start.1 = (bf16[192,1536]{1,0:T(8,128)(2,1)S(1)}, bf16[192,1536]{1,0:T(8,128)(2,1)S(1)}, u32[]{:S(2)}, u32[]{:S(2)}) collective-permute-start(bf16[192,1536]{1,0:T(8,128)(2,1)S(1)} %bitcast.165), channel_id=1, source_target_pairs={{0,8},{4,12},{8,0},{12,4},{1,9},{5,13},{9,1},{13,5},{2,10},{6,14},... | collective-permute-start | bytes 1769480 | tf_op jit(solution)/shard_map/ppermute | solution.py:288
  228.5 45.2 %collective-permute-start = (bf16[192,1536]{1,0:T(8,128)(2,1)S(1)}, bf16[192,1536]{1,0:T(8,128)(2,1)S(1)}, u32[]{:S(2)}, u32[]{:S(2)}) collective-permute-start(bf16[192,1536]{1,0:T(8,128)(2,1)S(1)} %bitcast.166), channel_id=1, source_target_pairs={{0,4},{4,0},{8,12},{12,8},{1,5},{5,1},{9,13},{13,9},{2,6},{6,2},{1... | collective-permute-start | bytes 1769480 | tf_op jit(solution)/shard_map/ppermute | solution.py:288
  228.6 26.9 %collective-permute-start.29 = (bf16[192,1024]{1,0:T(8,128)(2,1)S(1)}, bf16[192,1024]{1,0:T(8,128)(2,1)}, u32[]{:S(2)}, u32[]{:S(2)}) collective-permute-start(bf16[192,1024]{1,0:T(8,128)(2,1)S(1)} %bitcast.201), channel_id=1, source_target_pairs={{0,1},{1,2},{2,3},{3,0},{4,5},{5,6},{6,7},{7,4},{8,9},{9,10},{10,1... | collective-permute-start | bytes 1179656 | tf_op jit(solution)/shard_map/ppermute | solution.py:284
  231.3 35.2 %collective-permute-start.30 = (bf16[192,1024]{1,0:T(8,128)(2,1)S(1)}, bf16[192,1024]{1,0:T(8,128)(2,1)}, u32[]{:S(2)}, u32[]{:S(2)}) collective-permute-start(bf16[192,1024]{1,0:T(8,128)(2,1)S(1)} %bitcast.202), channel_id=1, source_target_pairs={{0,2},{1,3},{2,0},{3,1},{4,6},{5,7},{6,4},{7,5},{8,10},{9,11},{10,... | collective-permute-start | bytes 1179656 | tf_op jit(solution)/shard_map/ppermute | solution.py:284
  235.9 95.6 %all-to-all-start.2 = ((bf16[4,192,384]{2,1,0:T(8,128)(2,1)}), bf16[4,192,384]{2,1,0:T(8,128)(2,1)}, u32[]{:S(2)}, u32[]{:S(2)}) async-start(bf16[4,192,384]{2,1,0:T(8,128)(2,1)} %dynamic-slice_bitcast_fusion), calls=%async_computation.2 | async-start | bytes 1179648 | tf_op jit(solution)/shard_map/all_to_all | solution.py:320
  246.3 22.7 %collective-permute-start.31 = (bf16[192,1024]{1,0:T(8,128)(2,1)S(1)}, bf16[192,1024]{1,0:T(8,128)(2,1)}, u32[]{:S(2)}, u32[]{:S(2)}) collective-permute-start(bf16[192,1024]{1,0:T(8,128)(2,1)S(1)} %bitcast.203), channel_id=1, source_target_pairs={{0,3},{1,0},{2,1},{3,2},{4,7},{5,4},{6,5},{7,6},{8,11},{9,8},{10,9... | collective-permute-start | bytes 1179656 | tf_op jit(solution)/shard_map/ppermute | solution.py:284
  255.5 16.8 %collective-permute-start.32 = (bf16[192,1024]{1,0:T(8,128)(2,1)S(1)}, bf16[192,1024]{1,0:T(8,128)(2,1)S(1)}, u32[]{:S(2)}, u32[]{:S(2)}) collective-permute-start(bf16[192,1024]{1,0:T(8,128)(2,1)S(1)} %bitcast.204), channel_id=1, source_target_pairs={{0,16},{16,0},{1,17},{17,1},{2,18},{18,2},{3,19},{19,3},{4,20},{20... | collective-permute-start | bytes 1179656 | tf_op jit(solution)/shard_map/ppermute | solution.py:284
  258.8 61.9 %collective-permute-start.26 = (bf16[192,2048]{1,0:T(8,128)(2,1)}, bf16[192,2048]{1,0:T(8,128)(2,1)S(1)}, u32[]{:S(2)}, u32[]{:S(2)}) collective-permute-start(bf16[192,2048]{1,0:T(8,128)(2,1)} %collective-permute-done.22), channel_id=1, source_target_pairs={{0,16},{16,0},{1,17},{17,1},{2,18},{18,2},{3,19},{19,3},{4,20},{20... | collective-permute-start | bytes 2359304 | tf_op jit(solution)/shard_map/ppermute | solution.py:284
  266.5 8.6 %collective-permute-start.2 = (bf16[192,1536]{1,0:T(8,128)(2,1)S(1)}, bf16[192,1536]{1,0:T(8,128)(2,1)S(1)}, u32[]{:S(2)}, u32[]{:S(2)}) collective-permute-start(bf16[192,1536]{1,0:T(8,128)(2,1)S(1)} %collective-permute-done.1), channel_id=1, source_target_pairs={{0,4},{4,0},{8,12},{12,8},{1,5},{5,1},{9,13},{13,9},{2,6},{6,2},{1... | collective-permute-start | bytes 1769480 | tf_op jit(solution)/shard_map/ppermute | solution.py:288
  269.1 53.2 %collective-permute-start.27 = (bf16[192,2048]{1,0:T(8,128)(2,1)}, bf16[192,2048]{1,0:T(8,128)(2,1)}, u32[]{:S(2)}, u32[]{:S(2)}) collective-permute-start(bf16[192,2048]{1,0:T(8,128)(2,1)} %collective-permute-done.23), channel_id=1, source_target_pairs={{0,16},{16,0},{1,17},{17,1},{2,18},{18,2},{3,19},{19,3},{4,20},{20... | collective-permute-start | bytes 2359304 | tf_op jit(solution)/shard_map/ppermute | solution.py:284
  272.3 58.1 %collective-permute-start.28 = (bf16[192,2048]{1,0:T(8,128)(2,1)}, bf16[192,2048]{1,0:T(8,128)(2,1)S(1)}, u32[]{:S(2)}, u32[]{:S(2)}) collective-permute-start(bf16[192,2048]{1,0:T(8,128)(2,1)} %collective-permute-done.24), channel_id=1, source_target_pairs={{0,16},{16,0},{1,17},{17,1},{2,18},{18,2},{3,19},{19,3},{4,20},{20... | collective-permute-start | bytes 2359304 | tf_op jit(solution)/shard_map/ppermute | solution.py:284
  273.7 55.0 %collective-permute-start.33 = (bf16[192,1024]{1,0:T(8,128)(2,1)}, bf16[192,1024]{1,0:T(8,128)(2,1)}, u32[]{:S(2)}, u32[]{:S(2)}) collective-permute-start(bf16[192,1024]{1,0:T(8,128)(2,1)} %collective-permute-done.29), channel_id=1, source_target_pairs={{0,16},{16,0},{1,17},{17,1},{2,18},{18,2},{3,19},{19,3},{4,20},{20... | collective-permute-start | bytes 1179656 | tf_op jit(solution)/shard_map/ppermute | solution.py:284
  317.8 8.0 collective-permute-start.17
  320.7 27.2 %collective-permute-start.34 = (bf16[192,1024]{1,0:T(8,128)(2,1)}, bf16[192,1024]{1,0:T(8,128)(2,1)}, u32[]{:S(2)}, u32[]{:S(2)}) collective-permute-start(bf16[192,1024]{1,0:T(8,128)(2,1)} %collective-permute-done.30), channel_id=1, source_target_pairs={{0,16},{16,0},{1,17},{17,1},{2,18},{18,2},{3,19},{19,3},{4,20},{20... | collective-permute-start | bytes 1179656 | tf_op jit(solution)/shard_map/ppermute | solution.py:284
  322.3 27.4 %collective-permute-start.35 = (bf16[192,1024]{1,0:T(8,128)(2,1)}, bf16[192,1024]{1,0:T(8,128)(2,1)}, u32[]{:S(2)}, u32[]{:S(2)}) collective-permute-start(bf16[192,1024]{1,0:T(8,128)(2,1)} %collective-permute-done.31), channel_id=1, source_target_pairs={{0,16},{16,0},{1,17},{17,1},{2,18},{18,2},{3,19},{19,3},{4,20},{20... | collective-permute-start | bytes 1179656 | tf_op jit(solution)/shard_map/ppermute | solution.py:284
  328.1 16.4 %collective-permute-start.18 = (bf16[192,1536]{1,0:T(8,128)(2,1)S(1)}, bf16[192,1536]{1,0:T(8,128)(2,1)}, u32[]{:S(2)}, u32[]{:S(2)}) collective-permute-start(bf16[192,1536]{1,0:T(8,128)(2,1)S(1)} %slice.294), channel_id=1, source_target_pairs={{0,8},{4,12},{8,0},{12,4},{1,9},{5,13},{9,1},{13,5},{2,10},{6,14},... | collective-permute-start | bytes 1769480 | tf_op jit(solution)/shard_map/ppermute | solution.py:288
  332.6 36.0 %collective-permute-start.41 = (bf16[192,1536]{1,0:T(8,128)(2,1)S(1)}, bf16[192,1536]{1,0:T(8,128)(2,1)S(1)}, u32[]{:S(2)}, u32[]{:S(2)}) collective-permute-start(bf16[192,1536]{1,0:T(8,128)(2,1)S(1)} %bitcast.180), channel_id=1, source_target_pairs={{0,4},{4,0},{8,12},{12,8},{1,5},{5,1},{9,13},{13,9},{2,6},{6,2},{1... | collective-permute-start | bytes 1769480 | tf_op jit(solution)/shard_map/ppermute | solution.py:288
  332.6 24.3 %collective-permute-start.42 = (bf16[192,1536]{1,0:T(8,128)(2,1)S(1)}, bf16[192,1536]{1,0:T(8,128)(2,1)S(1)}, u32[]{:S(2)}, u32[]{:S(2)}) collective-permute-start(bf16[192,1536]{1,0:T(8,128)(2,1)S(1)} %bitcast.181), channel_id=1, source_target_pairs={{0,8},{4,12},{8,0},{12,4},{1,9},{5,13},{9,1},{13,5},{2,10},{6,14},... | collective-permute-start | bytes 1769480 | tf_op jit(solution)/shard_map/ppermute | solution.py:288
  347.3 21.3 %collective-permute-start.20 = (bf16[192,1536]{1,0:T(8,128)(2,1)S(1)}, bf16[192,1536]{1,0:T(8,128)(2,1)S(1)}, u32[]{:S(2)}, u32[]{:S(2)}) collective-permute-start(bf16[192,1536]{1,0:T(8,128)(2,1)S(1)} %multiply_convert_fusion.4), channel_id=1, source_target_pairs={{0,8},{4,12},{8,0},{12,4},{1,9},{5,13},{9,1},{13,5},{2,10},{6,14},... | collective-permute-start | bytes 1769480 | tf_op jit(solution)/shard_map/ppermute | solution.py:288
  357.0 11.7 %collective-permute-start.43 = (bf16[192,1536]{1,0:T(8,128)(2,1)S(1)}, bf16[192,1536]{1,0:T(8,128)(2,1)S(1)}, u32[]{:S(2)}, u32[]{:S(2)}) collective-permute-start(bf16[192,1536]{1,0:T(8,128)(2,1)S(1)} %collective-permute-done.42), channel_id=1, source_target_pairs={{0,4},{4,0},{8,12},{12,8},{1,5},{5,1},{9,13},{13,9},{2,6},{6,2},{1... | collective-permute-start | bytes 1769480 | tf_op jit(solution)/shard_map/ppermute | solution.py:288
  357.0 11.7 %collective-permute-start.19 = (bf16[192,1536]{1,0:T(8,128)(2,1)S(1)}, bf16[192,1536]{1,0:T(8,128)(2,1)S(1)}, u32[]{:S(2)}, u32[]{:S(2)}) collective-permute-start(bf16[192,1536]{1,0:T(8,128)(2,1)S(1)} %multiply_convert_fusion.4), channel_id=1, source_target_pairs={{0,4},{4,0},{8,12},{12,8},{1,5},{5,1},{9,13},{13,9},{2,6},{6,2},{1... | collective-permute-start | bytes 1769480 | tf_op jit(solution)/shard_map/ppermute | solution.py:288
  392.6 6.0 collective-permute-start.44
  398.2 7.3 collective-permute-start.36
  404.9 16.2 %collective-permute-start.45 = (bf16[192,1536]{1,0:T(8,128)(2,1)S(1)}, bf16[192,1536]{1,0:T(8,128)(2,1)S(1)}, u32[]{:S(2)}, u32[]{:S(2)}) collective-permute-start(bf16[192,1536]{1,0:T(8,128)(2,1)S(1)} %slice.292), channel_id=1, source_target_pairs={{0,8},{4,12},{8,0},{12,4},{1,9},{5,13},{9,1},{13,5},{2,10},{6,14},... | collective-permute-start | bytes 1769480 | tf_op jit(solution)/shard_map/ppermute | solution.py:288
  409.5 23.5 %collective-permute-start.37 = (bf16[192,1536]{1,0:T(8,128)(2,1)S(1)}, bf16[192,1536]{1,0:T(8,128)(2,1)S(1)}, u32[]{:S(2)}, u32[]{:S(2)}) collective-permute-start(bf16[192,1536]{1,0:T(8,128)(2,1)S(1)} %slice.293), channel_id=1, source_target_pairs={{0,8},{4,12},{8,0},{12,4},{1,9},{5,13},{9,1},{13,5},{2,10},{6,14},... | collective-permute-start | bytes 1769480 | tf_op jit(solution)/shard_map/ppermute | solution.py:288
  413.7 38.0 %collective-permute-start.58 = (bf16[768,1024]{1,0:T(8,128)(2,1)}, bf16[768,1024]{1,0:T(8,128)(2,1)}, u32[]{:S(2)}, u32[]{:S(2)}) collective-permute-start(bf16[768,1024]{1,0:T(8,128)(2,1)} %convolution_convert_fusion.5), channel_id=1, source_target_pairs={{0,16},{16,0},{1,17},{17,1},{2,18},{18,2},{3,19},{19,3},{4,20},{20... | collective-permute-start | bytes 4718600 | tf_op jit(solution)/shard_map/ppermute | solution.py:284
  435.0 14.9 %collective-permute-start.47 = (bf16[192,1536]{1,0:T(8,128)(2,1)}, bf16[192,1536]{1,0:T(8,128)(2,1)S(1)}, u32[]{:S(2)}, u32[]{:S(2)}) collective-permute-start(bf16[192,1536]{1,0:T(8,128)(2,1)} %get-tuple-element.84), channel_id=1, source_target_pairs={{0,8},{4,12},{8,0},{12,4},{1,9},{5,13},{9,1},{13,5},{2,10},{6,14},... | collective-permute-start | bytes 1769480 | tf_op jit(solution)/shard_map/ppermute | solution.py:288
  435.5 36.1 %collective-permute-start.46 = (bf16[192,1536]{1,0:T(8,128)(2,1)}, bf16[192,1536]{1,0:T(8,128)(2,1)}, u32[]{:S(2)}, u32[]{:S(2)}) collective-permute-start(bf16[192,1536]{1,0:T(8,128)(2,1)} %get-tuple-element.84), channel_id=1, source_target_pairs={{0,4},{4,0},{8,12},{12,8},{1,5},{5,1},{9,13},{13,9},{2,6},{6,2},{1... | collective-permute-start | bytes 1769480 | tf_op jit(solution)/shard_map/ppermute | solution.py:288
  449.9 21.8 %collective-permute-start.48 = (bf16[192,1536]{1,0:T(8,128)(2,1)S(1)}, bf16[192,1536]{1,0:T(8,128)(2,1)}, u32[]{:S(2)}, u32[]{:S(2)}) collective-permute-start(bf16[192,1536]{1,0:T(8,128)(2,1)S(1)} %collective-permute-done.47), channel_id=1, source_target_pairs={{0,4},{4,0},{8,12},{12,8},{1,5},{5,1},{9,13},{13,9},{2,6},{6,2},{1... | collective-permute-start | bytes 1769480 | tf_op jit(solution)/shard_map/ppermute | solution.py:288
  457.4 63.6 %all-to-all-start.1 = ((bf16[192,4,384]{2,0,1:T(8,128)(2,1)}), bf16[192,4,384]{2,0,1:T(8,128)(2,1)S(1)}, u32[]{:S(2)}, u32[]{:S(2)}) async-start(bf16[192,4,384]{2,0,1:T(8,128)(2,1)} %bitcast.156), calls=%async_computation.1 | async-start | bytes 1179648 | tf_op jit(solution)/shard_map/all_to_all | solution.py:383
  521.0 11.7 %all-to-all-start.5 = ((bf16[4,192,6]{1,2,0:T(8,128)(2,1)}), bf16[4,192,6]{1,2,0:T(8,128)(2,1)}, u32[]{:S(2)}, u32[]{:S(2)}) async-start(bf16[4,192,6]{1,2,0:T(8,128)(2,1)} %copy.77), calls=%async_computation.5 | async-start | bytes 32768 | tf_op jit(solution)/shard_map/all_to_all | solution.py:379
  532.7 17.4 %collective-permute-start.49 = (bf16[384,1536]{1,0:T(8,128)(2,1)}, bf16[384,1536]{1,0:T(8,128)(2,1)}, u32[]{:S(2)}, u32[]{:S(2)}) collective-permute-start(bf16[384,1536]{1,0:T(8,128)(2,1)} %fusion.19), channel_id=1, source_target_pairs={{0,4},{4,0},{8,12},{12,8},{1,5},{5,1},{9,13},{13,9},{2,6},{6,2},{1... | collective-permute-start | bytes 3538952 | tf_op jit(solution)/shard_map/ppermute | solution.py:288
  532.7 98.4 %all-to-all-start.8 = ((bf16[4,192,1024]{2,1,0:T(8,128)(2,1)}), bf16[4,192,1024]{2,1,0:T(8,128)(2,1)}, u32[]{:S(2)}, u32[]{:S(2)}) async-start(bf16[4,192,1024]{2,1,0:T(8,128)(2,1)} %bitcast.197), calls=%async_computation.8 | async-start | bytes 3145728 | tf_op jit(solution)/shard_map/all_to_all | solution.py:379
  546.5 108.1 %collective-permute-start.57 = (bf16[768,2048]{1,0:T(8,128)(2,1)}, bf16[768,2048]{1,0:T(8,128)(2,1)}, u32[]{:S(2)}, u32[]{:S(2)}) collective-permute-start(bf16[768,2048]{1,0:T(8,128)(2,1)} %convolution_convert_fusion), channel_id=1, source_target_pairs={{0,16},{16,0},{1,17},{17,1},{2,18},{18,2},{3,19},{19,3},{4,20},{20... | collective-permute-start | bytes 9437192 | tf_op jit(solution)/shard_map/ppermute | solution.py:284
  548.7 80.7 %collective-permute-start.56 = (bf16[768,384]{1,0:T(8,128)(2,1)S(1)}, bf16[768,384]{1,0:T(8,128)(2,1)S(1)}, u32[]{:S(2)}, u32[]{:S(2)}) collective-permute-start(bf16[768,384]{1,0:T(8,128)(2,1)S(1)} %convolution_convert_fusion.6), channel_id=1, source_target_pairs={{0,16},{16,0},{1,17},{17,1},{2,18},{18,2},{3,19},{19,3},{4,20},{20... | collective-permute-start | bytes 1769480 | tf_op jit(solution)/shard_map/ppermute | solution.py:284
  554.4 81.6 %collective-permute-start.50 = (bf16[192,1536]{1,0:T(8,128)(2,1)}, bf16[192,1536]{1,0:T(8,128)(2,1)}, u32[]{:S(2)}, u32[]{:S(2)}) collective-permute-start(bf16[192,1536]{1,0:T(8,128)(2,1)} %slice.291), channel_id=1, source_target_pairs={{0,8},{4,12},{8,0},{12,4},{1,9},{5,13},{9,1},{13,5},{2,10},{6,14},... | collective-permute-start | bytes 1769480 | tf_op jit(solution)/shard_map/ppermute | solution.py:288
  631.1 20.0 %all-to-all-start.6 = ((bf16[4,192,384]{2,1,0:T(8,128)(2,1)}), bf16[4,192,384]{2,1,0:T(8,128)(2,1)}, u32[]{:S(2)}, u32[]{:S(2)}) async-start(bf16[4,192,384]{2,1,0:T(8,128)(2,1)} %bitcast.200), calls=%async_computation.6 | async-start | bytes 1179648 | tf_op jit(solution)/shard_map/all_to_all | solution.py:379
  651.1 18.8 %all-to-all-start.3 = ((bf16[192,4,384]{2,0,1:T(8,128)(2,1)}), bf16[192,4,384]{2,0,1:T(8,128)(2,1)S(1)}, u32[]{:S(2)}, u32[]{:S(2)}) async-start(bf16[192,4,384]{2,0,1:T(8,128)(2,1)} %bitcast.155), calls=%async_computation.3 | async-start | bytes 1179648 | tf_op jit(solution)/shard_map/all_to_all | solution.py:383
  669.9 75.1 %all-to-all-start.7 = ((bf16[4,192,2048]{2,1,0:T(8,128)(2,1)}), bf16[4,192,2048]{2,1,0:T(8,128)(2,1)}, u32[]{:S(2)}, u32[]{:S(2)}) async-start(bf16[4,192,2048]{2,1,0:T(8,128)(2,1)} %bitcast.184), calls=%async_computation.7 | async-start | bytes 6291456 | tf_op jit(solution)/shard_map/all_to_all | solution.py:379
  678.7 52.3 %collective-permute-start.54 = (bf16[768,1536]{1,0:T(8,128)(2,1)S(1)}, bf16[768,1536]{1,0:T(8,128)(2,1)S(1)}, u32[]{:S(2)}, u32[]{:S(2)}) collective-permute-start(bf16[768,1536]{1,0:T(8,128)(2,1)S(1)} %convolution_convert_fusion.1), channel_id=1, source_target_pairs={{0,16},{16,0},{1,17},{17,1},{2,18},{18,2},{3,19},{19,3},{4,20},{20... | collective-permute-start | bytes 7077896 | tf_op jit(solution)/shard_map/ppermute | solution.py:284
  680.1 14.1 %collective-permute-start.39 = (bf16[4,1,192,384]{3,2,1,0:T(8,128)(2,1)S(1)}, bf16[4,1,192,384]{3,2,1,0:T(8,128)(2,1)}, u32[]{:S(2)}, u32[]{:S(2)}) collective-permute-start(bf16[4,1,192,384]{3,2,1,0:T(8,128)(2,1)S(1)} %bitcast.186), channel_id=1, source_target_pairs={{0,8},{4,12},{8,0},{12,4},{1,9},{5,13},{9,1},{13,5},{2,10},{6,14},... | collective-permute-start | bytes 1769480 | tf_op jit(solution)/shard_map/ppermute | solution.py:288
  680.6 71.0 %collective-permute-start.38 = (bf16[4,1,192,384]{3,2,1,0:T(8,128)(2,1)S(1)}, bf16[4,1,192,384]{3,2,1,0:T(8,128)(2,1)}, u32[]{:S(2)}, u32[]{:S(2)}) collective-permute-start(bf16[4,1,192,384]{3,2,1,0:T(8,128)(2,1)S(1)} %bitcast.187), channel_id=1, source_target_pairs={{0,4},{4,0},{8,12},{12,8},{1,5},{5,1},{9,13},{13,9},{2,6},{6,2},{1... | collective-permute-start | bytes 1769480 | tf_op jit(solution)/shard_map/ppermute | solution.py:288
  694.2 57.5 %collective-permute-start.40 = (bf16[4,1,192,384]{3,2,1,0:T(8,128)(2,1)}, bf16[4,1,192,384]{3,2,1,0:T(8,128)(2,1)}, u32[]{:S(2)}, u32[]{:S(2)}) collective-permute-start(bf16[4,1,192,384]{3,2,1,0:T(8,128)(2,1)} %collective-permute-done.39), channel_id=1, source_target_pairs={{0,4},{4,0},{8,12},{12,8},{1,5},{5,1},{9,13},{13,9},{2,6},{6,2},{1... | collective-permute-start | bytes 1769480 | tf_op jit(solution)/shard_map/ppermute | solution.py:288
  745.0 89.8 %all-to-all-start.4 = ((bf16[4,192,1536]{2,1,0:T(8,128)(2,1)}), bf16[4,192,1536]{2,1,0:T(8,128)(2,1)}, u32[]{:S(2)}, u32[]{:S(2)}) async-start(bf16[4,192,1536]{2,1,0:T(8,128)(2,1)} %bitcast.193), calls=%async_computation.4 | async-start | bytes 4718592 | tf_op jit(solution)/shard_map/all_to_all | solution.py:379
  749.7 14.5 %collective-permute-start.52 = (bf16[4,1,192,384]{3,2,1,0:T(8,128)(2,1)S(1)}, bf16[4,1,192,384]{3,2,1,0:T(8,128)(2,1)}, u32[]{:S(2)}, u32[]{:S(2)}) collective-permute-start(bf16[4,1,192,384]{3,2,1,0:T(8,128)(2,1)S(1)} %bitcast.189), channel_id=1, source_target_pairs={{0,8},{4,12},{8,0},{12,4},{1,9},{5,13},{9,1},{13,5},{2,10},{6,14},... | collective-permute-start | bytes 1769480 | tf_op jit(solution)/shard_map/ppermute | solution.py:288
  753.4 70.4 %collective-permute-start.51 = (bf16[4,1,192,384]{3,2,1,0:T(8,128)(2,1)S(1)}, bf16[4,1,192,384]{3,2,1,0:T(8,128)(2,1)S(1)}, u32[]{:S(2)}, u32[]{:S(2)}) collective-permute-start(bf16[4,1,192,384]{3,2,1,0:T(8,128)(2,1)S(1)} %bitcast.190), channel_id=1, source_target_pairs={{0,4},{4,0},{8,12},{12,8},{1,5},{5,1},{9,13},{13,9},{2,6},{6,2},{1... | collective-permute-start | bytes 1769480 | tf_op jit(solution)/shard_map/ppermute | solution.py:288
  764.2 59.6 %collective-permute-start.53 = (bf16[4,1,192,384]{3,2,1,0:T(8,128)(2,1)}, bf16[4,1,192,384]{3,2,1,0:T(8,128)(2,1)}, u32[]{:S(2)}, u32[]{:S(2)}) collective-permute-start(bf16[4,1,192,384]{3,2,1,0:T(8,128)(2,1)} %collective-permute-done.52), channel_id=1, source_target_pairs={{0,4},{4,0},{8,12},{12,8},{1,5},{5,1},{9,13},{13,9},{2,6},{6,2},{1... | collective-permute-start | bytes 1769480 | tf_op jit(solution)/shard_map/ppermute | solution.py:288
  (76 other events, 1273.8 us)

commit v2 on v1

--- a/solution.py
+++ b/solution.py
@@ -1,3 +1,4 @@
+import functools
 import jax, jax.numpy as jnp
 from jax import lax
 from jax.experimental import pallas as pl
@@ -5,6 +6,7 @@
 from jax.sharding import PartitionSpec as P
 
 HD = 128
+STEP = 64
 F32 = jnp.float32
 BF = jnp.bfloat16
 
@@ -70,9 +72,15 @@
     return invs
 
 
-def fwd_kernel(proj_ref, lg_ref, seg_ref, att_ref, pr_ref, qm_ref, x_ref, ft_ref, e_ref, kt_ref, p_ref, s_ref):
+def place_of(order_ref, block, per):
+    return pl.ds(pl.multiple_of((((block // per) ^ order_ref[0]) * per + block % per) * STEP, STEP), STEP)
+
+
+def fwd_kernel(per, order_ref, proj_ref, lg_ref, seg_ref, att_ref, pr_ref, qm_ref, x_ref, ft_ref, e_ref, kt_ref, p_ref, s_ref, own_ref):
     length, width = att_ref.shape
-    q_ref, k_ref, v_ref, r_ref = (proj_ref.at[:, n * width : (n + 1) * width] for n in range(4))
+    for b in range(length // STEP):
+        own_ref[b * STEP : (b + 1) * STEP, :] = proj_ref[place_of(order_ref, b, per), :]
+    q_ref, k_ref, v_ref, r_ref = (own_ref.at[:, n * width : (n + 1) * width] for n in range(4))
     blocks = length // width
     rows, cols = grids(width)
     eye = rows == cols
@@ -133,20 +141,23 @@
         ex = jnp.exp(score - top)
         prob = ex / jnp.sum(ex, axis=1, keepdims=True)
         pr_ref[0, here, :upto] = prob
-        att_ref[here, :] = mm(split(prob), v_ref[:upto, :], 1, 0).astype(att_ref.dtype)
-
-
-def attend_fwd(proj, logits, seg):
+        att = mm(split(prob), v_ref[:upto, :], 1, 0).astype(att_ref.dtype)
+        for b in range(width // STEP):
+            att_ref[place_of(order_ref, i * width // STEP + b, per), :] = att[b * STEP : (b + 1) * STEP]
+
+
+def attend_fwd(order, proj, logits, seg, quarter):
     length, wide = proj.shape
     heads = wide // (4 * HD)
     blocks = length // HD
     part = pl.BlockSpec((length, 4 * HD), lambda h: (0, h))
+    smem = pl.BlockSpec(memory_space=pltpu.SMEM)
     per = pl.BlockSpec((1, length, HD), lambda h: (h, 0, 0))
     st = jax.ShapeDtypeStruct
     return pl.pallas_call(
-        fwd_kernel,
+        functools.partial(fwd_kernel, quarter // STEP),
         grid=(heads,),
-        in_specs=[part,
+        in_specs=[smem, part,
                   pl.BlockSpec((1, 1, length), lambda h: (h, 0, 0)),
                   pl.BlockSpec((1, length), lambda h: (0, 0))],
         out_specs=[pl.BlockSpec((length, HD), lambda h: (0, h)),
@@ -155,17 +166,21 @@
                    per, per, per, per, per],
         out_shape=[st((length, heads * HD), BF), st((heads, length, length), F32),
                    st((heads, blocks, length, HD), F32)] + [st((heads, length, HD), F32)] * 5,
-        scratch_shapes=[pltpu.VMEM((length, length), F32)],
+        scratch_shapes=[pltpu.VMEM((length, length), F32), pltpu.VMEM((length, 4 * HD), BF)],
         compiler_params=pltpu.CompilerParams(vmem_limit_bytes=56 << 20, dimension_semantics=("arbitrary",)),
+        cost_estimate=pl.CostEstimate(flops=heads * 11 * 10**9, bytes_accessed=heads * 10**7, transcendentals=heads * length * length),
         name="attend_fwd",
-    )(proj, logits.reshape(heads, 1, length), seg)
-
-
-def bwd_kernel(proj_ref, lg_ref, do_ref, pr_ref, qm_ref, x_ref, ft_ref, e_ref, kt_ref, p_ref,
-               dproj_ref, dl_ref, ds_ref, dkt_ref, dqt_ref, dp_ref):
-    length, width = do_ref.shape
-    q_ref, k_ref, v_ref, r_ref = (proj_ref.at[:, n * width : (n + 1) * width] for n in range(4))
-    dq_ref, dk_ref, dv_ref, dr_ref = (dproj_ref.at[:, n * width : (n + 1) * width] for n in range(4))
+    )(order, proj, logits.reshape(heads, 1, length), seg)
+
+
+def bwd_kernel(per, order_ref, proj_ref, lg_ref, dog_ref, pr_ref, qm_ref, x_ref, ft_ref, e_ref, kt_ref, p_ref,
+               dproj_ref, dl_ref, ds_ref, dkt_ref, dqt_ref, dp_ref, own_ref, do_ref, dv_ref):
+    length, width = dog_ref.shape
+    for b in range(length // STEP):
+        rows = slice(b * STEP, (b + 1) * STEP)
+        own_ref[rows, :] = proj_ref[place_of(order_ref, b, per), :]
+        do_ref[rows, :] = dog_ref[place_of(order_ref, b, per), :]
+    q_ref, k_ref, v_ref, r_ref = (own_ref.at[:, n * width : (n + 1) * width] for n in range(4))
     blocks = length // width
     rows, cols = grids(width)
     eye = rows == cols
@@ -180,7 +195,7 @@
     for j in range(blocks):
         here = pl.ds(j * width, width)
         below = pl.ds(j * width, length - j * width)
-        dv_ref[here, :] = mm(split(pr_ref[0, below, here]), split(do_ref[below, :]), 0, 0).astype(dv_ref.dtype)
+        dv_ref[here, :] = mm(split(pr_ref[0, below, here]), split(do_ref[below, :]), 0, 0)
 
     zero = jnp.zeros((width, width), F32)
     dqt_ref[0:width, :] = zero
@@ -243,49 +258,96 @@
         dr = dr - mm(cat([ft, e]), cat([dkt, dqt]), 0, 0) + mm(tri, dy, 0, 0) - mm(y, dp, 1, 1)
         dsig = to_col(db * beta_row, eye)
         dr = dr - (2.0 * dsig * sig_col * sig_col) * r.astype(F32)
-        dq_ref[at, :] = dq.astype(dq_ref.dtype)
-        dk_ref[at, :] = dk.astype(dk_ref.dtype)
-        dr_ref[at, :] = dr.astype(dr_ref.dtype)
+        whole = jnp.concatenate([dq, dk, dv_ref[at, :], dr], axis=1).astype(dproj_ref.dtype)
+        for b in range(width // STEP):
+            dproj_ref[place_of(order_ref, c * width // STEP + b, per), :] = whole[b * STEP : (b + 1) * STEP]
 
     for c in range(blocks):
         chunk(c)
 
 
-def attend_bwd(proj, logits, saved, grad):
+def attend_bwd(order, proj, logits, saved, grad, quarter):
     length, wide = proj.shape
     heads = wide // (4 * HD)
     blocks = length // HD
     part = pl.BlockSpec((length, 4 * HD), lambda h: (0, h))
+    smem = pl.BlockSpec(memory_space=pltpu.SMEM)
     per = pl.BlockSpec((1, length, HD), lambda h: (h, 0, 0))
     col = pl.BlockSpec((length, HD), lambda h: (0, h))
     lrow = pl.BlockSpec((1, 1, length), lambda h: (h, 0, 0))
     st = jax.ShapeDtypeStruct
     scr = pltpu.VMEM((length, HD), F32)
     return pl.pallas_call(
-        bwd_kernel,
+        functools.partial(bwd_kernel, quarter // STEP),
         grid=(heads,),
-        in_specs=[part, lrow, col,
+        in_specs=[smem, part, lrow, col,
                   pl.BlockSpec((1, length, length), lambda h: (h, 0, 0)),
                   pl.BlockSpec((1, blocks, length, HD), lambda h: (h, 0, 0, 0)),
                   per, per, per, per, per],
         out_specs=[part, lrow],
         out_shape=[st((length, wide), BF), st((heads, 1, length), F32)],
-        scratch_shapes=[pltpu.VMEM((length, length), F32), scr, scr, scr],
+        scratch_shapes=[pltpu.VMEM((length, length), F32), scr, scr, scr, pltpu.VMEM((length, 4 * HD), BF), scr, scr],
         compiler_params=pltpu.CompilerParams(vmem_limit_bytes=56 << 20, dimension_semantics=("arbitrary",)),
+        cost_estimate=pl.CostEstimate(flops=15 * 10**9, bytes_accessed=10**7, transcendentals=length),
         name="attend_bwd",
-    )(proj, logits.reshape(heads, 1, length), grad, *saved)
+    )(order, proj, logits.reshape(heads, 1, length), grad, *saved)
+
+
+def assemble(pieces, places, widths):
+    size, count = pieces[0].shape[0], len(pieces)
+
+    def kernel(place_ref, *refs):
+        for n in range(count):
+            rows = pl.ds(pl.multiple_of(place_ref[n] * size, size), size)
+            start = 0
+            for out, width in zip(refs[count:], widths):
+                out[rows, :] = refs[n][:, start : start + width]
+                start += width
+
+    vmem = pl.BlockSpec(memory_space=pltpu.VMEM)
+    return pl.pallas_call(
+        kernel,
+        in_specs=[pl.BlockSpec(memory_space=pltpu.SMEM)] + [vmem] * count,
+        out_specs=[vmem] * len(widths),
+        out_shape=[jax.ShapeDtypeStruct((count * size, w), BF) for w in widths],
+        compiler_params=pltpu.CompilerParams(vmem_limit_bytes=56 << 20),
+        cost_estimate=pl.CostEstimate(flops=0, bytes_accessed=4 * count * size * sum(widths), transcendentals=0),
+        name="assemble",
+    )(jnp.stack(places), *pieces)
 
 
 def after(value, *first):
     return lax.optimization_barrier((value,) + first)[0]
 
 
-def shift(value, axis, size, by):
-    return lax.ppermute(value, axis, [(i, (i + by) % size) for i in range(size)])
-
-
-def swap(value, axis, size, bit):
-    return lax.ppermute(value, axis, [(i, i ^ bit) for i in range(size)])
+class Lane:
+    def __init__(self, depth):
+        self.depth, self.done = depth, []
+
+    def send(self, value, axis, pairs, *first):
+        if len(self.done) >= self.depth:
+            first = first + (self.done[-self.depth],)
+        if first:
+            value = after(value, *first)
+        self.done.append(lax.ppermute(value, axis, pairs))
+        return self.done[-1]
+
+
+class Flow:
+    def __init__(self, make):
+        self.make, self.got, self.sent, self.out = make, None, None, None
+
+    def step(self, *first):
+        try:
+            self.sent, self.got = self.make.send(first) if self.got is not None else next(self.make)
+        except StopIteration as end:
+            self.out = end.value
+        return self.got
+
+    def finish(self, *first):
+        while self.out is None:
+            self.step(*first)
+        return self.out
 
 
 def norm_back(values, scale_row, gain, grad_out):
@@ -308,12 +370,15 @@
         tokens, slice_width = hidden_in.shape
         rows = tokens // wid
         quarter = rows // hid
-        features = slice_width * wid
         heads = in_weight.shape[2] // HD
         shard = in_weight.shape[0]
+        lane_x, lane_y, lane_z = Lane(4), Lane(6), Lane(4)
 
         def dot(a, b, ca, cb, out=F32):
             return lax.dot_general(a, b, (((ca,), (cb,)), ((), ())), preferred_element_type=F32).astype(out)
+
+        def swap(value, bit, *first):
+            return lane_x.send(value, "hid", [(i, i ^ bit) for i in range(hid)], *first)
 
         def to_tokens(array):
             mine = lax.dynamic_index_in_dim(array.reshape(wid, hid, quarter, slice_width), me_hid, 1, keepdims=False)
@@ -324,27 +389,33 @@
             bit = hid // 2
             while bit:
                 for k in list(pieces):
-                    pieces[k | bit] = swap(pieces[k], "hid", hid, bit)
+                    pieces[k | bit] = swap(pieces[k], bit)
                 bit //= 2
             return [pieces[k] for k in range(hid)]
 
-        def sum_hid(make):
+        def summing_hid(make, first=()):
             keep, bit = list(range(hid)), 1
             send = [k for k in keep if k & bit]
             keep = [k for k in keep if not k & bit]
-            got = swap(make(send).astype(BF), "hid", hid, bit)
-            total = make(keep) + got
+            sent = make(send).astype(BF)
+            got = swap(sent, bit, *first)
+            wait = yield sent, got
+            total = make(keep) + (after(got, *wait) if wait else got)
             bit *= 2
             while bit < hid:
-                half = total.shape[0] // 2
                 low = [n for n, k in enumerate(keep) if not k & bit]
                 high = [n for n, k in enumerate(keep) if k & bit]
                 part = lambda ns: jnp.concatenate([total[n * quarter : (n + 1) * quarter] for n in ns], axis=0)
-                got = swap(part(high).astype(BF), "hid", hid, bit)
-                total = part(low) + got
+                sent = part(high).astype(BF)
+                got = swap(sent, bit)
+                wait = yield sent, got
+                total = part(low) + (after(got, *wait) if wait else got)
                 keep = [k for k in keep if not k & bit]
                 bit *= 2
             return total
+
+        def sum_hid(make):
+            return Flow(summing_hid(make)).finish()
 
         def reorder(array, axis=0):
             size = array.shape[axis] // hid
@@ -352,123 +423,213 @@
                 [lax.dynamic_slice_in_dim(array, (me_hid ^ j) * size, size, axis) for j in range(hid)], axis=axis
             )
 
-        def gather_wid(own):
-            return [own] + [shift(own, "wid", wid, k) for k in range(1, wid)]
-
-        def gather_dp(pieces):
-            got = [pieces] + [[shift(p, "dp", dp, k) for p in pieces] for k in range(1, dp)]
-            cols = pieces[0].shape[1]
-            whole = jnp.zeros((dp * wid, shard, cols), pieces[0].dtype)
-            for i in range(dp):
-                for k in range(wid):
-                    place = ((me_dp + dp - i) % dp) * wid + (me_wid + wid - k) % wid
-                    whole = lax.dynamic_update_slice(whole, got[i][k][None], (place, 0, 0))
-            return whole.reshape(dp * wid * shard, cols)
-
-        def scatter_grad(left, right):
+        def rows_of(array, ks):
+            return jnp.concatenate([array[k * quarter : (k + 1) * quarter] for k in ks], axis=0)
+
+        def scattering(make, kept, wid_first=False, first=()):
+            def bits(size):
+                return [1 << n for n in range(size.bit_length() - 1)]
+
+            def over(axis, lane, parts, bit, first):
+                high = [j for j in parts if j & bit]
+                sent = jnp.concatenate([parts[j].astype(BF) for j in high], axis=0)
+                got = lane.send(sent, axis, [(i, i ^ bit) for i in range(sizes[axis])], *first)
+                wait = yield sent, got
+                got = after(got, *wait) if wait else got
+                low = [j for j in parts if not j & bit]
+                size = sent.shape[0] // len(high)
+                return {j: parts[j] + got[n * size : (n + 1) * size] for n, j in enumerate(low)}, ()
+
+            parts = {j: make(j) for j in range(dp)}
+            kept.append(parts[0])
+            if not wid_first:
+                for bit in reversed(bits(dp)):
+                    parts, first = yield from over("dp", lane_y, parts, bit, first)
+            width = parts[0].shape[-1]
+            blocks = {j: part.reshape(wid, shard, width) for j, part in parts.items()}
+            parts = {
+                n: jnp.concatenate([lax.dynamic_index_in_dim(b, me_wid ^ n, 0, keepdims=False) for b in blocks.values()], axis=0)
+                for n in range(wid)
+            }
+            for bit in bits(wid):
+                parts, first = yield from over("wid", lane_z, parts, bit, first)
+            if wid_first:
+                parts = dict(enumerate(jnp.split(parts[0], dp, axis=0)))
+                for bit in reversed(bits(dp)):
+                    parts, first = yield from over("dp", lane_y, parts, bit, first)
+            return parts[0]
+
+        def scatter_grad(left, right, first=(), kept=None):
+            kept = [] if kept is None else kept
+            return Flow(scattering(lambda by: dot(half(left, by), right, 0, 0), kept, False, first))
+
+        def half(left, by):
             width = left.shape[1] // dp
-
-            def part(k):
-                cols = lax.dynamic_slice_in_dim(left, ((me_dp + k) % dp) * width, width, 1)
-                return dot(cols, right, 0, 0)
-
-            got = [shift(part(k).astype(BF), "dp", dp, k) for k in range(1, dp)]
-            mine = part(0)
-            for g in got:
-                mine = mine + g
-            parts = lax.all_to_all(mine.astype(BF), "wid", split_axis=0, concat_axis=0, tiled=True)
-            return jnp.sum(parts.reshape(wid, shard, right.shape[1]).astype(F32), axis=0)
-
-        def to_widths(own, dtype):
-            mine = lax.all_to_all(own.astype(BF), "wid", split_axis=1, concat_axis=0, tiled=True)
-            pieces = gather_hid(mine.reshape(wid, 1, quarter, slice_width))
-            stacked = reorder(jnp.concatenate(pieces, axis=1), axis=1)
+            return lax.dynamic_slice_in_dim(left, (me_dp ^ by) * width, width, 1)
+
+        def to_widths(own, *first):
+            mine = lax.all_to_all(after(own.astype(BF), *first), "wid", split_axis=1, concat_axis=0, tiled=True)
+            return mine.reshape(wid, 1, own.shape[0], slice_width)
+
+        def placed(pieces, dtype):
+            stacked = reorder(jnp.concatenate([p[:, :, :quarter] for p in pieces], axis=1), axis=1)
             return stacked.reshape(tokens, slice_width).astype(dtype)
 
-        by_head = in_weight.reshape(shard, 4, heads, HD).transpose(0, 2, 1, 3).reshape(shard, 4 * heads * HD)
-        small = jnp.concatenate([beta_weight, gain_attn[:, None], gain_mlp[:, None]], axis=1)
-        small = jnp.pad(small, ((0, 0), (0, HD - small.shape[1])))
-        own_in = jnp.concatenate([by_head, small], axis=1)
-        own_mlp = jnp.concatenate([gate_weight, up_weight], axis=1)
+        inner, hidden = out_weight.shape[0], gate_weight.shape[1]
+
+        def gather_rows(own):
+            return lax.all_gather(own, ("dp", "wid"), axis=0, tiled=True)
+
+        weight_out = gather_rows(out_weight.T)
+
+        hops = list(range(wid))
+        hops = [0, 1] + hops[:1:-1] if wid > 2 else hops
+
+        def along_wid(own, *first):
+            if first:
+                own = after(own, *first)
+            made = [own]
+            for k in hops[1:]:
+                sent = own if k in (1, wid - 1) else after(own, *made[1:])
+                made.append(lax.ppermute(sent, "wid", [(i, (i + k) % wid) for i in range(wid)]))
+            return made
+
+        def over_dp(piece, *first):
+            return [piece] + [lane_y.send(piece, "dp", [(i, (i + by) % dp) for i in range(dp)], *first) for by in range(1, dp)]
+
+        def whole(pieces, widths):
+            places = [
+                (me_dp + dp - by) % dp * wid + (me_wid + wid - k) % wid for k in hops for by in range(dp)
+            ]
+            return assemble([p for ps in pieces for p in ps], places, widths)
 
         token_in = to_tokens(hidden_in)
-        parts_in = gather_wid(own_in)
+        width_in = 4 * heads * HD
+        columns = [in_weight[:, c, h * HD : (h + 1) * HD] for h in range(heads) for c in range(4)]
+        small = [beta_weight, gain_attn[:, None], gain_mlp[:, None], jnp.zeros((shard, HD - heads - 2), BF)]
+        along = along_wid(jnp.concatenate(columns + small, axis=1))
+        own_late = jnp.concatenate([gate_weight, up_weight, down_weight.T], axis=1)
         inputs_all = jnp.concatenate(gather_hid(token_in), axis=0).astype(F32)
-        parts_out = gather_wid(after(out_weight, *parts_in).T)
-        weight_in = gather_dp(parts_in)
-        parts_mlp = gather_wid(after(own_mlp, *parts_in))
-        weight_out = gather_dp(parts_out)
-        cotangent = after(cotangent, *parts_mlp)
-        token_grad = to_tokens(cotangent)
-        grad_all = jnp.concatenate(gather_hid(token_grad), axis=0)
-        parts_down = gather_wid(after(down_weight, *parts_mlp).T)
-        weight_mlp = gather_dp(parts_mlp)
-        weight_down = gather_dp(parts_down)
-
-        width_in = 4 * heads * HD
-        weight_beta = weight_in[:, width_in : width_in + heads]
-        gain_one = weight_in[:, width_in + heads].astype(F32)
-        gain_two = weight_in[:, width_in + heads + 1].astype(F32)
-        weight_in = weight_in[:, :width_in]
+        pieces = [over_dp(a) for a in along]
+        late_along = along_wid(own_late, along[-1])
+        late = [over_dp(own_late)]
+        weight_in, small = whole(pieces, (width_in, HD))
+        weight_beta = small[:, :heads]
+        gain_one = small[:, heads].astype(F32)
+        gain_two = small[:, heads + 1].astype(F32)
 
         scale_all = lax.rsqrt(jnp.mean(inputs_all * inputs_all, axis=-1, keepdims=True) + 1e-06)
         normed = (inputs_all * scale_all * gain_one).astype(BF)
-        projected = reorder(dot(normed, weight_in, 1, 0, BF))
+        projected = dot(normed, weight_in, 1, 0, BF)
+        order = me_hid.reshape(1)
         logits = reorder(dot(normed, weight_beta, 1, 0)).T
-        attended, *saved = attend_fwd(projected, logits, segments)
-        attended = reorder(attended)
-
-        def rows_of(array, ks):
-            return jnp.concatenate([array[k * quarter : (k + 1) * quarter] for k in ks], axis=0)
-
-        branch = sum_hid(lambda ks: dot(rows_of(attended, ks), weight_out, 1, 1))
+        late += [over_dp(a) for a in late_along[1:]]
+        attended, *saved = attend_fwd(order, after(projected, *late_along[1:3]), logits, segments, quarter)
+        attended = after(attended, late[1][-1])
+        token_grad = to_tokens(after(cotangent, attended))
+
+        branch_flow = Flow(summing_hid(lambda ks: dot(rows_of(attended, ks), weight_out, 1, 1)))
+        branch_flow.step()
+        branch_flow.step(late_along[-1])
+        branch = branch_flow.finish(late[2][-1])
         inputs = inputs_all[:quarter]
         scale_one = scale_all[:quarter]
         middle = inputs + branch
         scale_two = lax.rsqrt(jnp.mean(middle * middle, axis=-1, keepdims=True) + 1e-06)
         mixed = jnp.concatenate(gather_hid((middle * scale_two * gain_two).astype(BF)), axis=0)
+        grad_all = jnp.concatenate(gather_hid(after(token_grad, mixed)), axis=0)
+        weight_mlp, weight_down = whole(late, (2 * hidden, hidden))
         gate_up = dot(mixed, weight_mlp, 1, 0)
-        hidden = gate_up.shape[1] // 2
         gate, upward = gate_up[:, :hidden], gate_up[:, hidden:]
         sigmoid_gate = jax.nn.sigmoid(gate)
         silu_gate = gate * sigmoid_gate
         product = (silu_gate * upward).astype(BF)
-
+        def scatter_plain(full):
+            return lax.psum_scatter(full, ("dp", "wid"), scatter_dimension=0, tiled=True).astype(F32)
+
+        down_full = dot(grad_all, product, 0, 0, BF)
+        grad_down = scatter_plain(down_full)
         grad_product = dot(grad_all, weight_down, 1, 0)
         grad_gate_pre = grad_product * upward * sigmoid_gate * (1.0 + gate * (1.0 - sigmoid_gate))
-        grad_pre = jnp.concatenate([grad_gate_pre.astype(BF), (grad_product * silu_gate).astype(BF)], axis=1)
-        grad_mixed = sum_hid(lambda ks: dot(rows_of(grad_pre, ks), weight_mlp, 1, 1))
-        grad_down = scatter_grad(grad_all, product)
-        grad_mlp = scatter_grad(mixed, grad_pre)
-
+        grad_gate_pre, grad_up_pre = grad_gate_pre.astype(BF), (grad_product * silu_gate).astype(BF)
+        kept = [down_full]
+        gate_flow, up_flow = (scatter_grad(mixed, g, kept=kept) for g in (grad_gate_pre, grad_up_pre))
+        grad_pre = jnp.concatenate([grad_gate_pre, grad_up_pre], axis=1)
+        mixed_flow = Flow(summing_hid(lambda ks: dot(rows_of(grad_pre, ks), weight_mlp, 1, 1)))
+        mixed_flow.step()
+        gate_flow.step()
+        mixed_flow.step()
+        feed_flow = Flow(summing_hid(lambda ks: dot(rows_of(product, ks), weight_down, 1, 1)))
+        feed_flow.step()
+        grad_mixed = mixed_flow.finish()
+        up_flow.step()
         grad_gain_two, grad_middle = norm_back(middle, scale_two, gain_two, grad_mixed)
         grad_middle = grad_middle + token_grad.astype(F32)
-        grad_branch = jnp.concatenate(gather_hid(grad_middle.astype(BF)), axis=0)
-        grad_attended = reorder(dot(grad_branch, weight_out, 1, 0))
-        grad_proj, grad_logit = attend_bwd(projected, logits, saved, grad_attended)
-        grad_out = scatter_grad(grad_branch, attended)
-
-        feed = sum_hid(lambda ks: dot(rows_of(product, ks), weight_down, 1, 1))
-        output = to_widths(middle + feed, BF)
-
-        grad_proj = reorder(grad_proj)
-        logit_parts = jnp.concatenate(split(reorder(grad_logit[:, 0, :].T)), axis=1)
+        quarters = gather_hid(grad_middle.astype(BF))
+        grad_branch = after(jnp.concatenate(quarters, axis=0), gate_flow.got, *kept)
+        grad_attended = dot(grad_branch, weight_out, 1, 0)
+        gate_flow.step(grad_branch)
+        feed_flow.step(grad_branch)
+
+        grad_proj, grad_logit = attend_bwd(order, projected, logits, saved, grad_attended, quarter)
+        grad_proj = after(grad_proj, up_flow.got, feed_flow.got)
+        grad_logit = grad_logit[:, 0, :]
+        logit_parts = jnp.concatenate(split(reorder(grad_logit, axis=1)), axis=0)
         beta_twice = jnp.concatenate([weight_beta, weight_beta], axis=1)
-        grad_normed = sum_hid(
-            lambda ks: dot(rows_of(grad_proj, ks), weight_in, 1, 1) + dot(rows_of(logit_parts, ks), beta_twice, 1, 1)
-        )
+
+        def back(ks):
+            lower = jnp.concatenate([logit_parts[:, k * quarter : (k + 1) * quarter] for k in ks], axis=1)
+            return dot(rows_of(grad_proj, ks), weight_in, 1, 1) + dot(lower, beta_twice, 0, 1)
+
+        back_flow = Flow(summing_hid(back))
+        back_flow.step()
+        begun = back_flow.sent
+        in_flow = scatter_grad(normed, after(grad_proj, begun))
+        in_flow.step()
+        up_flow.step(begun)
+        feed_widths = to_widths(middle + feed_flow.finish(begun))
+        back_flow.step()
+        handed = back_flow.sent
+        grad_normed = back_flow.finish()
+        gate_flow.step(handed)
         grad_gain_one, grad_inputs = norm_back(inputs, scale_one, gain_one, grad_normed)
-        grad_input = to_widths(grad_inputs + grad_middle, F32)
-        grad_in = scatter_grad(normed, grad_proj)
-        grad_beta = scatter_grad(normed, logit_parts)
-        grad_beta = grad_beta[:, :heads] + grad_beta[:, heads:]
-        grad_in = grad_in.reshape(shard, heads, 4, HD).transpose(0, 2, 1, 3).reshape(shard, 4, heads * HD)
-
-        gains = lax.psum(jnp.stack([grad_gain_one, grad_gain_two]), ("dp", "hid", "wid"))
-        gains = lax.dynamic_slice_in_dim(gains, (me_dp * wid + me_wid) * shard, shard, 1)
+        grad_beta = dot(after(logit_parts, handed), normed, 1, 0)
+        grad_beta = grad_beta[:heads] + grad_beta[heads:]
+        vectors = jnp.concatenate([grad_gain_one[None], grad_gain_two[None], grad_beta], axis=0)
+        count = vectors.shape[0]
+        vectors = vectors.reshape(count, dp, wid, shard).transpose(0, 2, 1, 3).reshape(count, wid * dp * shard)
+        extra = jnp.concatenate(split(vectors), axis=0)
+        extra = jnp.pad(extra, ((0, -(2 * count) % 16), (0, 0)))
+        ended = jnp.concatenate([(grad_inputs + grad_middle).astype(BF), extra], axis=0)
+        grad_widths = to_widths(ended)
+        in_flow.step(ended)
+        up_flow.step(grad_widths)
+        grad_out = scatter_plain(dot(grad_branch, after(attended, handed), 0, 0, BF))
+        out_pieces = gather_hid(after(feed_widths, ended))
+        in_pieces = gather_hid(grad_widths)
+        arrived = in_pieces[hid // 2]
+        in_flow.step(grad_widths)
+        passed = in_flow.sent
+        grad_gate, grad_up = gate_flow.finish(arrived), up_flow.finish(passed)
+
+        def row_sums(piece):
+            both = jnp.sum(piece[:, 0, quarter : quarter + 2 * count].astype(F32), axis=0)
+            return (both[:count] + both[count:]).reshape(count, dp, shard)
+
+        sums = [row_sums(p) for p in in_pieces]
+        gains = functools.reduce(jnp.add, [one[:2] for one in sums])
+        sums = jnp.concatenate([gains, sums[0][2:]], axis=0)
+        vectors = lax.dynamic_index_in_dim(sums, me_dp, 1, keepdims=False)
+        for by in range(1, dp):
+            theirs = lax.dynamic_index_in_dim(sums, (me_dp + by) % dp, 1, keepdims=False)
+            vectors = vectors + lax.ppermute(theirs, "dp", [(i, (i + by) % dp) for i in range(dp)])
+        in_pieces = [after(p, passed) for p in in_pieces]
+        output, grad_input = placed(out_pieces, BF), placed(in_pieces, F32)
+        grad_in = in_flow.finish().reshape(shard, heads, 4, HD).transpose(0, 2, 1, 3).reshape(shard, 4, heads * HD)
+
         return (
-            output, grad_input, gains[0], gains[1], grad_in, grad_beta, grad_out.T,
-            grad_mlp[:, :hidden], grad_mlp[:, hidden:], grad_down.T,
+            output, grad_input, vectors[0], vectors[1], grad_in, vectors[2:].T, grad_out.T,
+            grad_gate, grad_up, grad_down.T,
         )
 
     return body

time: 847 us -> 615 us (0.73)
  waiting for transfers between devices: 382 us -> 247 us
  starting transfers between devices: 126 us -> 66.8 us
  blocking collectives: 53.7 us -> 0 us
  local copies, waits for them, and re-layouts: 75.3 us -> 54.3 us
  other arithmetic: 47.6 us -> 63.5 us
  Pallas kernels: 63.7 us -> 76.9 us
  between operations: 2.56 us -> 15.6 us
    ppermute x59 -> x50, waiting for transfers between devices: 354 us -> 224 us  [the longest x43 124 us: send(): self.done.append(lax.ppermute(value, axis, pairs))]
    psum x1 -> x0, blocking collectives: 53.7 us -> none  [body(): lax.psum(jnp.stack([grad_gain_one, grad_gain_two]), ('dp', 'hid', 'wid'))]
    dynamic_update_slice x31 -> x0, local copies, waits for them, and re-layouts: 34.5 us -> none  [gather_dp(): whole = lax.dynamic_update_slice(whole, got[i][k][None], (place, 0, 0))]
    all_to_all x7 -> x2, starting transfers between devices: 42.7 us -> 8.46 us  [to_widths(): lax.all_to_all(after(own.astype(BF), *first), 'wid', split_axis=1, concat...]
    ppermute x59 -> x50, starting transfers between devices: 76.1 us -> 47.2 us  [the longest x43 35.3 us: send(): self.done.append(lax.ppermute(value, axis, pairs))]
    all_to_all x7 -> x2, waiting for transfers between devices: 28.2 us -> 15 us  [to_widths(): lax.all_to_all(after(own.astype(BF), *first), 'wid', split_axis=1, concat...]
    pallas_call x2 -> x4, Pallas kernels: 63.7 us -> 76.9 us  [the longest x1 34.7 us: attend_bwd(): pl.pallas_call(functools.partial(bwd_kernel, quarter // STEP), grid=(head...]
    add x1 -> x9, other arithmetic: 0.6 us -> 11.9 us  [the longest x5 10.5 us: over(): parts[j] + got[n * size:(n + 1) * size]]
  transfers between devices with their start and end apart: 68 -> 57, of which waited for: 27 -> 21; matrix products, arithmetic and copies ran while one was open for 20% -> 28% of each run, Pallas kernels for 8% -> 13%
where the time goes in v2:
time: 615 us; the launch traced here: 610 us
  waiting for transfers between devices  247 us (40%)
  matrix products  85.7 us (14%)
  Pallas kernels  76.9 us (13%)
  starting transfers between devices  66.8 us (11%)
  other arithmetic  63.5 us (10%)
  local copies, waits for them, and re-layouts  54.3 us (9%)
  between operations  15.6 us (3%)
    ppermute x43, waiting for transfers between devices, send(): self.done.append(lax.ppermute(value, axis, pairs))  124 us
    ppermute x6, waiting for transfers between devices, along_wid(): lax.ppermute(sent, 'wid', [(i, (i + k) % wid) for i in range(wid)])  99.2 us
    dot_general x24, matrix products, dot(): lax.dot_general(a, b, (((ca,), (cb,)), ((), ())), preferred_element_type=...  85.7 us
    ppermute x43, starting transfers between devices, send(): self.done.append(lax.ppermute(value, axis, pairs))  35.3 us
    pallas_call x1, Pallas kernels, attend_bwd(): pl.pallas_call(functools.partial(bwd_kernel, quarter // STEP), grid=(head...  34.7 us
    pallas_call x1, Pallas kernels, attend_fwd(): pl.pallas_call(functools.partial(fwd_kernel, quarter // STEP), grid=(head...  29.2 us
    unnamed x161, local copies, waits for them, and re-layouts  16.5 us
    all_to_all x2, waiting for transfers between devices, to_widths(): lax.all_to_all(after(own.astype(BF), *first), 'wid', split_axis=1, concat...  15 us
  transfers between devices with their start and end apart: 57, of which 21 were waited for; matrix products, arithmetic and copies ran while one was open for 28% of the time, Pallas kernels for 13%

profile of v2, /device:TPU:0, one launch (start us, length us, event | category | flops | bytes accessed | tf_op | source)
XLA Modules:
  0.0 610.1 jit_solution(14736970852909050485)
XLA Ops:
  9.7 6.3 %all-to-all-start = ((bf16[4,192,384]{2,1,0:T(8,128)(2,1)}), bf16[4,192,384]{2,1,0:T(8,128)(2,1)S(1)}, u32[]{:S(2)}, u32[]{:S(2)}) async-start(bf16[4,192,384]{2,1,0:T(8,128)(2,1)} %dynamic-slice_bitcast_fusion.1), calls=%async_computation | async-start | bytes 1179648 | tf_op jit(solution)/shard_map/all_to_all | solution.py:385
  18.1 2.1 collective-permute-start.4
  22.1 22.8 %collective-permute-done.4.refs_2_ = bf16[192,1664]{1,0:T(8,128)(2,1)S(1)} collective-permute-done((bf16[192,1664]{1,0:T(8,128)(2,1)S(1)}, bf16[192,1664]{1,0:T(8,128)(2,1)S(1)}, u32[]{:S(2)}, u32[]{:S(2)}) %collective-permute-start.4) | collective-permute-done | bytes 639008 | tf_op jit(solution)/shard_map/ppermute | solution.py:494
  44.8 10.4 %collective-permute-done.6.refs_4_ = bf16[192,1664]{1,0:T(8,128)(2,1)S(1)} collective-permute-done((bf16[192,1664]{1,0:T(8,128)(2,1)S(1)}, bf16[192,1664]{1,0:T(8,128)(2,1)S(1)}, u32[]{:S(2)}, u32[]{:S(2)}) %collective-permute-start.6) | collective-permute-done | bytes 639008 | tf_op jit(solution)/shard_map/ppermute | solution.py:494
  55.3 4.7 collective-permute-start.8
  65.1 21.8 %collective-permute-done.8.refs_6_ = bf16[192,1664]{1,0:T(8,128)(2,1)} collective-permute-done((bf16[192,1664]{1,0:T(8,128)(2,1)S(1)}, bf16[192,1664]{1,0:T(8,128)(2,1)}, u32[]{:S(2)}, u32[]{:S(2)}) %collective-permute-start.8) | collective-permute-done | bytes 639008 | tf_op jit(solution)/shard_map/ppermute | solution.py:494
  89.7 2.2 pad_maximum_fusion.5.refs_0_
  91.9 14.4 %collective-permute-done.7.refs_5_ = bf16[192,1664]{1,0:T(8,128)(2,1)} collective-permute-done((bf16[192,1664]{1,0:T(8,128)(2,1)}, bf16[192,1664]{1,0:T(8,128)(2,1)}, u32[]{:S(2)}, u32[]{:S(2)}) %collective-permute-start.7) | collective-permute-done | bytes 639008 | tf_op jit(solution)/shard_map/ppermute | solution.py:332
  106.4 2.3 collective-permute-start.11
  108.6 8.7 %collective-permute-done.9.refs_7_ = bf16[192,1664]{1,0:T(8,128)(2,1)} collective-permute-done((bf16[192,1664]{1,0:T(8,128)(2,1)}, bf16[192,1664]{1,0:T(8,128)(2,1)}, u32[]{:S(2)}, u32[]{:S(2)}) %collective-permute-start.9) | collective-permute-done | bytes 639008 | tf_op jit(solution)/shard_map/ppermute | solution.py:332
  117.4 5.1 assemble.2
  128.7 5.0 convolution_convert_fusion.2.proj_ref
  133.7 27.7 %collective-permute-done.11.refs_4_ = bf16[192,3072]{1,0:T(8,128)(2,1)S(1)} collective-permute-done((bf16[192,3072]{1,0:T(8,128)(2,1)}, bf16[192,3072]{1,0:T(8,128)(2,1)S(1)}, u32[]{:S(2)}, u32[]{:S(2)}) %collective-permute-start.11) | collective-permute-done | bytes 1179680 | tf_op jit(solution)/shard_map/ppermute | solution.py:494
  162.4 29.2 %attend_fwd.1 = (bf16[768,384]{1,0:T(8,128)(2,1)}, f32[3,768,768]{2,1,0:T(8,128)}, f32[3,6,768,128]{3,2,1,0:T(8,128)}, f32[3,768,128]{2,1,0:T(8,128)}, f32[3,768...) custom-call(s32[1]{0:T(128)} %bitcast.3.order_ref, ...), custom_call_target="tpu_custom_call" | custom-call | flops 32999999488 | bytes 30000000 | tf_op jit(solution)/shard_map/attend_fwd/pallas_call | solution.py:157
  194.7 2.4 convolution_convert_fusion.6
  198.7 16.5 %collective-permute-done.14.refs_6_ = bf16[192,3072]{1,0:T(8,128)(2,1)} collective-permute-done((bf16[192,3072]{1,0:T(8,128)(2,1)}, bf16[192,3072]{1,0:T(8,128)(2,1)}, u32[]{:S(2)}, u32[]{:S(2)}) %collective-permute-start.14) | collective-permute-done | bytes 1179680 | tf_op jit(solution)/shard_map/ppermute | solution.py:494
  218.9 7.0 %collective-permute-done.16.refs_5_ = bf16[192,3072]{1,0:T(8,128)(2,1)S(1)} collective-permute-done((bf16[192,3072]{1,0:T(8,128)(2,1)S(1)}, bf16[192,3072]{1,0:T(8,128)(2,1)S(1)}, u32[]{:S(2)}, u32[]{:S(2)}) %collective-permute-start.16) | collective-permute-done | bytes 1179680 | tf_op jit(solution)/shard_map/ppermute | solution.py:332
  226.0 5.3 collective-permute-done.15
  237.1 4.2 all-to-all-start.1
  241.8 5.8 collective-permute-done.18
  247.6 8.5 %all-to-all-done.1 = bf16[4,192,384]{2,1,0:T(8,128)(2,1)} async-done(((bf16[4,192,384]{2,1,0:T(8,128)(2,1)}), bf16[4,192,384]{2,1,0:T(8,128)(2,1)}, u32[]{:S(2)}, u32[]{:S(2)}) %all-to-all-start.1) | async-done | bytes 589856 | tf_op jit(solution)/shard_map/all_to_all | solution.py:385
  257.2 18.9 %collective-permute-done.21.refs_7_ = bf16[192,3072]{1,0:T(8,128)(2,1)} collective-permute-done((bf16[192,3072]{1,0:T(8,128)(2,1)}, bf16[192,3072]{1,0:T(8,128)(2,1)}, u32[]{:S(2)}, u32[]{:S(2)}) %collective-permute-start.21) | collective-permute-done | bytes 1179680 | tf_op jit(solution)/shard_map/ppermute | solution.py:332
  276.2 8.0 %assemble.3 = (bf16[1536,2048]{1,0:T(8,128)(2,1)}, bf16[1536,1024]{1,0:T(8,128)(2,1)}) custom-call(s32[8]{0:T(128)} %stack.44.place_ref, bf16[192,3072]{1,0:T(8,128)(2,1)} %pad_maximum_fusion.5.refs_0_, bf16[192,3072]{1,0:T(8,128)(2,1)} %collective-permute-done.20.refs_1_, bf16[192,3072]{1,0:T(8,128)(2,1)} %copy-done.38, bf16[192,3072]{1,0:T(8,128)(2,1)} %copy-done.41, ...), custom_call_target="tpu_custom_call" | custom-call | bytes 18874368 | tf_op jit(solution)/shard_map/assemble/pallas_call | solution.py:308
  284.1 3.1 pad_maximum_fusion
  288.8 7.8 %fusion.105 = f32[768,2048]{1,0:T(8,128)S(1)} fusion(bf16[1536,2048]{1,0:T(8,128)(2,1)} %get-tuple-element.98, bf16[192,1536]{1,0:T(8,128)(2,1)} %collective-permute-done.19, bf16[192,1536]{1,0:T(8,128)(2,1)} %collective-permute-done.18, bf16[192,1536]{1,0:T(8,128)(2,1)} %collective-permute-done.17, bf16[192,1536]{1,0:T(8,128)(2,1)} %multiply_convert_fusion.4), kind=kOutput, calls=%fused_computation.255 | convolution fusion | flops 4841275392 | bytes 14942208 | tf_op jit(solution)/shard_map/dot_general | solution.py:378
  296.6 6.4 %collective-permute-done.24 = bf16[192,1536]{1,0:T(8,128)(2,1)S(1)} collective-permute-done((bf16[192,1536]{1,0:T(8,128)(2,1)S(1)}, bf16[192,1536]{1,0:T(8,128)(2,1)S(1)}, u32[]{:S(2)}, u32[]{:S(2)}) %collective-permute-start.24) | collective-permute-done | bytes 589856 | tf_op jit(solution)/shard_map/ppermute | solution.py:332
  305.1 5.0 multiply_convert_fusion.2
  312.3 3.7 convolution_convert_fusion.4
  319.0 4.4 convolution_convert_fusion.8
  323.5 5.9 convolution_add_fusion.2
  335.9 4.3 convolution_convert_fusion
  340.2 7.4 %collective-permute-done.27 = bf16[192,1536]{1,0:T(8,128)(2,1)} collective-permute-done((bf16[192,1536]{1,0:T(8,128)(2,1)}, bf16[192,1536]{1,0:T(8,128)(2,1)}, u32[]{:S(2)}, u32[]{:S(2)}) %collective-permute-start.27) | collective-permute-done | bytes 589856 | tf_op jit(solution)/shard_map/ppermute | solution.py:332
  349.6 2.9 fusion.106
  354.0 2.4 convolution_convert_fusion.5
  356.5 2.6 convolution_convert_fusion.7
  360.9 6.7 %collective-permute-done.29 = bf16[192,1536]{1,0:T(8,128)(2,1)} collective-permute-done((bf16[192,1536]{1,0:T(8,128)(2,1)}, bf16[192,1536]{1,0:T(8,128)(2,1)}, u32[]{:S(2)}, u32[]{:S(2)}) %collective-permute-start.29) | collective-permute-done | bytes 589856 | tf_op jit(solution)/shard_map/ppermute | solution.py:332
  367.6 4.8 fusion.34
  372.4 3.0 fusion.32
  379.1 2.8 convolution_add_fusion.3
  383.5 2.4 fusion.116.dog_ref
  385.9 34.7 %attend_bwd.1 = (bf16[768,1536]{1,0:T(8,128)(2,1)}, f32[3,1,768]{2,1,0:T(1,128)}) custom-call(s32[1]{0:T(128)} %bitcast.3.order_ref, bf16[768,1536]{1,0:T(8,128)(2,1)} %convolution_convert_fusion.2.proj_ref, f32[3,1,768]{2,1,0:T(1,128)} %reshape.176.lg_ref, f32[768,384]{1,0:T(8,128)} %fusion.116.dog_ref, f32[3,768,768]{2,1,0:T(8,128)} %get-tuple-element.115.pr_ref, ...), custom_call_target="tpu_custom_call" | custom-call | flops 15000000512 | bytes 10000000 | tf_op jit(solution)/shard_map/attend_bwd/pallas_call | solution.py:280
  429.8 5.8 fusion.4
  436.8 4.7 all-to-all-start.2
  441.7 5.3 convolution_convert_fusion.1
  448.6 2.2 convert_add_fusion.2
  453.6 2.0 collective-permute-start.45
  455.6 4.8 fusion.3
  465.8 10.5 %collective-permute-done.35 = bf16[192,1536]{1,0:T(8,128)(2,1)} collective-permute-done((bf16[192,1536]{1,0:T(8,128)(2,1)}, bf16[192,1536]{1,0:T(8,128)(2,1)}, u32[]{:S(2)}, u32[]{:S(2)}) %collective-permute-start.35) | collective-permute-done | bytes 589856 | tf_op jit(solution)/shard_map/ppermute | solution.py:332
  476.3 2.7 multiply_reduce_fusion.3
  484.9 2.2 add_convert_fusion
  487.8 2.1 fusion.50
  489.8 2.4 collective-permute-start.48
  492.2 4.2 convolution_convert_fusion.3
  497.4 3.8 all-to-all-start.3
  503.6 4.4 convert_add_fusion
  516.2 15.0 %all-to-all-done.3 = bf16[208,4,384]{2,0,1:T(8,128)(2,1)S(1)} async-done(((bf16[208,4,384]{2,0,1:T(8,128)(2,1)}), bf16[208,4,384]{2,0,1:T(8,128)(2,1)S(1)}, u32[]{:S(2)}, u32[]{:S(2)}) %all-to-all-start.3) | async-done | bytes 639008 | tf_op jit(solution)/shard_map/all_to_all | solution.py:471
  533.4 2.1 fusion.48
  543.1 3.6 collective-permute-done.42
  548.8 2.3 fusion.51
  551.1 14.4 %collective-permute-done.40 = bf16[384,1536]{1,0:T(8,128)(2,1)} collective-permute-done((bf16[384,1536]{1,0:T(8,128)(2,1)}, bf16[384,1536]{1,0:T(8,128)(2,1)}, u32[]{:S(2)}, u32[]{:S(2)}) %collective-permute-start.40) | collective-permute-done | bytes 1179680 | tf_op jit(solution)/shard_map/ppermute | solution.py:332
  565.5 2.3 fusion.26
  573.4 2.3 fusion.49
  582.7 2.7 bitcast_convert_fusion
  586.6 13.3 %collective-permute-done.46 = bf16[192,1536]{1,0:T(8,128)(2,1)} collective-permute-done((bf16[192,1536]{1,0:T(8,128)(2,1)}, bf16[192,1536]{1,0:T(8,128)(2,1)}, u32[]{:S(2)}, u32[]{:S(2)}) %collective-permute-start.46) | collective-permute-done | bytes 589856 | tf_op jit(solution)/shard_map/ppermute | solution.py:332
  (357 shorter events, 129.6 us)
Async XLA Ops:
  9.7 51.8 %all-to-all-start = ((bf16[4,192,384]{2,1,0:T(8,128)(2,1)}), bf16[4,192,384]{2,1,0:T(8,128)(2,1)S(1)}, u32[]{:S(2)}, u32[]{:S(2)}) async-start(bf16[4,192,384]{2,1,0:T(8,128)(2,1)} %dynamic-slice_bitcast_fusion.1), calls=%async_computation | async-start | bytes 1179648 | tf_op jit(solution)/shard_map/all_to_all | solution.py:385
  16.1 178.6 %all-gather.2.cloned.1.call-start = ((), (), s32[]{:S(2)}) async-start(), calls=%async_computation.6 | async-start | bytes 1327104 | tf_op jit(solution)/shard_map/all_gather | solution.py:481
  17.3 72.4 %copy-start.52 = (bf16[1024,192]{0,1:T(8,128)(2,1)S(1)}, bf16[1024,192]{0,1:T(8,128)(2,1)}, u32[]{:S(2)}) copy-start(bf16[1024,192]{0,1:T(8,128)(2,1)} %param.21) | copy-start | bytes 1179652
  18.1 99.2 %copy-start.21 = (bf16[192,1664]{1,0:T(8,128)(2,1)}, bf16[192,1664]{1,0:T(8,128)(2,1)S(1)}, u32[]{:S(2)}) copy-start(bf16[192,1664]{1,0:T(8,128)(2,1)S(1)} %concatenate.104.refs_0_) | copy-start | bytes 1916932
  18.1 26.7 %collective-permute-start.4 = (bf16[192,1664]{1,0:T(8,128)(2,1)S(1)}, bf16[192,1664]{1,0:T(8,128)(2,1)S(1)}, u32[]{:S(2)}, u32[]{:S(2)}) collective-permute-start(bf16[192,1664]{1,0:T(8,128)(2,1)S(1)} %concatenate.104.refs_0_), channel_id=1, source_target_pairs={{0,1},{1,2},{2,3},{3,0},{4,5},{5,6},{6,7},{7,4},{8,9},{9,10},{10,1... | collective-permute-start | bytes 1916936 | tf_op jit(solution)/shard_map/ppermute | solution.py:494
  20.2 35.1 %collective-permute-start.6 = (bf16[192,1664]{1,0:T(8,128)(2,1)S(1)}, bf16[192,1664]{1,0:T(8,128)(2,1)S(1)}, u32[]{:S(2)}, u32[]{:S(2)}) collective-permute-start(bf16[192,1664]{1,0:T(8,128)(2,1)S(1)} %concatenate.104.refs_0_), channel_id=1, source_target_pairs={{0,3},{1,0},{2,1},{3,2},{4,7},{5,4},{6,5},{7,6},{8,11},{9,8},{10,9... | collective-permute-start | bytes 1916936 | tf_op jit(solution)/shard_map/ppermute | solution.py:494
  55.3 31.7 %collective-permute-start.8 = (bf16[192,1664]{1,0:T(8,128)(2,1)S(1)}, bf16[192,1664]{1,0:T(8,128)(2,1)}, u32[]{:S(2)}, u32[]{:S(2)}) collective-permute-start(bf16[192,1664]{1,0:T(8,128)(2,1)S(1)} %concatenate.104.refs_0_), channel_id=1, source_target_pairs={{0,2},{1,3},{2,0},{3,1},{4,6},{5,7},{6,4},{7,5},{8,10},{9,11},{10,... | collective-permute-start | bytes 1916936 | tf_op jit(solution)/shard_map/ppermute | solution.py:494
  60.0 28.5 %collective-permute-start.3 = (bf16[192,1664]{1,0:T(8,128)(2,1)S(1)}, bf16[192,1664]{1,0:T(8,128)(2,1)}, u32[]{:S(2)}, u32[]{:S(2)}) collective-permute-start(bf16[192,1664]{1,0:T(8,128)(2,1)S(1)} %concatenate.104.refs_0_), channel_id=1, source_target_pairs={{0,16},{16,0},{1,17},{17,1},{2,18},{18,2},{3,19},{19,3},{4,20},{20... | collective-permute-start | bytes 1916936 | tf_op jit(solution)/shard_map/ppermute | solution.py:332
  61.5 26.9 %collective-permute-start.1 = (bf16[192,1536]{1,0:T(8,128)(2,1)S(1)}, bf16[192,1536]{1,0:T(8,128)(2,1)S(1)}, u32[]{:S(2)}, u32[]{:S(2)}) collective-permute-start(bf16[192,1536]{1,0:T(8,128)(2,1)S(1)} %bitcast.178), channel_id=1, source_target_pairs={{0,8},{4,12},{8,0},{12,4},{1,9},{5,13},{9,1},{13,5},{2,10},{6,14},... | collective-permute-start | bytes 1769480 | tf_op jit(solution)/shard_map/ppermute | solution.py:332
  63.1 28.8 %collective-permute-start.5 = (bf16[192,1664]{1,0:T(8,128)(2,1)}, bf16[192,1664]{1,0:T(8,128)(2,1)}, u32[]{:S(2)}, u32[]{:S(2)}) collective-permute-start(bf16[192,1664]{1,0:T(8,128)(2,1)} %copy-done.46), channel_id=1, source_target_pairs={{0,16},{16,0},{1,17},{17,1},{2,18},{18,2},{3,19},{19,3},{4,20},{20... | collective-permute-start | bytes 1916936 | tf_op jit(solution)/shard_map/ppermute | solution.py:332
  63.6 42.7 %collective-permute-start.7 = (bf16[192,1664]{1,0:T(8,128)(2,1)}, bf16[192,1664]{1,0:T(8,128)(2,1)}, u32[]{:S(2)}, u32[]{:S(2)}) collective-permute-start(bf16[192,1664]{1,0:T(8,128)(2,1)} %copy-done.47), channel_id=1, source_target_pairs={{0,16},{16,0},{1,17},{17,1},{2,18},{18,2},{3,19},{19,3},{4,20},{20... | collective-permute-start | bytes 1916936 | tf_op jit(solution)/shard_map/ppermute | solution.py:332
  86.9 30.4 %collective-permute-start.9 = (bf16[192,1664]{1,0:T(8,128)(2,1)}, bf16[192,1664]{1,0:T(8,128)(2,1)}, u32[]{:S(2)}, u32[]{:S(2)}) collective-permute-start(bf16[192,1664]{1,0:T(8,128)(2,1)} %collective-permute-done.8.refs_6_), channel_id=1, source_target_pairs={{0,16},{16,0},{1,17},{17,1},{2,18},{18,2},{3,19},{19,3},{4,20},{20... | collective-permute-start | bytes 1916936 | tf_op jit(solution)/shard_map/ppermute | solution.py:332
  88.5 35.7 %collective-permute-start = (bf16[192,1536]{1,0:T(8,128)(2,1)S(1)}, bf16[192,1536]{1,0:T(8,128)(2,1)S(1)}, u32[]{:S(2)}, u32[]{:S(2)}) collective-permute-start(bf16[192,1536]{1,0:T(8,128)(2,1)S(1)} %bitcast.179), channel_id=1, source_target_pairs={{0,4},{4,0},{8,12},{12,8},{1,5},{5,1},{9,13},{13,9},{2,6},{6,2},{1... | collective-permute-start | bytes 1769480 | tf_op jit(solution)/shard_map/ppermute | solution.py:332
  88.5 35.7 %collective-permute-start.2 = (bf16[192,1536]{1,0:T(8,128)(2,1)S(1)}, bf16[192,1536]{1,0:T(8,128)(2,1)S(1)}, u32[]{:S(2)}, u32[]{:S(2)}) collective-permute-start(bf16[192,1536]{1,0:T(8,128)(2,1)S(1)} %collective-permute-done.1), channel_id=1, source_target_pairs={{0,4},{4,0},{8,12},{12,8},{1,5},{5,1},{9,13},{13,9},{2,6},{6,2},{1... | collective-permute-start | bytes 1769480 | tf_op jit(solution)/shard_map/ppermute | solution.py:332
  91.9 41.8 %collective-permute-start.10 = (bf16[192,3072]{1,0:T(8,128)(2,1)}, bf16[192,3072]{1,0:T(8,128)(2,1)S(1)}, u32[]{:S(2)}, u32[]{:S(2)}) collective-permute-start(bf16[192,3072]{1,0:T(8,128)(2,1)} %pad_maximum_fusion.5.refs_0_), channel_id=1, source_target_pairs={{0,1},{1,2},{2,3},{3,0},{4,5},{5,6},{6,7},{7,4},{8,9},{9,10},{10,1... | collective-permute-start | bytes 3538952 | tf_op jit(solution)/shard_map/ppermute | solution.py:494
  106.4 55.0 %collective-permute-start.11 = (bf16[192,3072]{1,0:T(8,128)(2,1)}, bf16[192,3072]{1,0:T(8,128)(2,1)S(1)}, u32[]{:S(2)}, u32[]{:S(2)}) collective-permute-start(bf16[192,3072]{1,0:T(8,128)(2,1)} %pad_maximum_fusion.5.refs_0_), channel_id=1, source_target_pairs={{0,3},{1,0},{2,1},{3,2},{4,7},{5,4},{6,5},{7,6},{8,11},{9,8},{10,9... | collective-permute-start | bytes 3538952 | tf_op jit(solution)/shard_map/ppermute | solution.py:494
  133.7 57.9 %copy-start.38 = (bf16[192,3072]{1,0:T(8,128)(2,1)}, bf16[192,3072]{1,0:T(8,128)(2,1)S(1)}, u32[]{:S(2)}) copy-start(bf16[192,3072]{1,0:T(8,128)(2,1)S(1)} %collective-permute-done.10.refs_2_) | copy-start | bytes 3538948
  161.4 30.3 %copy-start.39 = (bf16[192,3072]{1,0:T(8,128)(2,1)}, bf16[192,3072]{1,0:T(8,128)(2,1)S(1)}, u32[]{:S(2)}) copy-start(bf16[192,3072]{1,0:T(8,128)(2,1)S(1)} %collective-permute-done.11.refs_4_) | copy-start | bytes 3538948
  161.4 53.9 %collective-permute-start.14 = (bf16[192,3072]{1,0:T(8,128)(2,1)}, bf16[192,3072]{1,0:T(8,128)(2,1)}, u32[]{:S(2)}, u32[]{:S(2)}) collective-permute-start(bf16[192,3072]{1,0:T(8,128)(2,1)} %pad_maximum_fusion.5.refs_0_), channel_id=1, source_target_pairs={{0,2},{1,3},{2,0},{3,1},{4,6},{5,7},{6,4},{7,5},{8,10},{9,11},{10,... | collective-permute-start | bytes 3538952 | tf_op jit(solution)/shard_map/ppermute | solution.py:494
  161.9 29.7 %collective-permute-start.12 = (bf16[192,3072]{1,0:T(8,128)(2,1)S(1)}, bf16[192,3072]{1,0:T(8,128)(2,1)S(1)}, u32[]{:S(2)}, u32[]{:S(2)}) collective-permute-start(bf16[192,3072]{1,0:T(8,128)(2,1)S(1)} %collective-permute-done.10.refs_2_), channel_id=1, source_target_pairs={{0,16},{16,0},{1,17},{17,1},{2,18},{18,2},{3,19},{19,3},{4,20},{20... | collective-permute-start | bytes 3538952 | tf_op jit(solution)/shard_map/ppermute | solution.py:332
  197.0 18.2 %collective-permute-start.13 = (bf16[384,1536]{1,0:T(8,128)(2,1)S(1)}, bf16[384,1536]{1,0:T(8,128)(2,1)S(1)}, u32[]{:S(2)}, u32[]{:S(2)}) collective-permute-start(bf16[384,1536]{1,0:T(8,128)(2,1)S(1)} %convolution_convert_fusion.6), channel_id=1, source_target_pairs={{0,4},{4,0},{8,12},{12,8},{1,5},{5,1},{9,13},{13,9},{2,6},{6,2},{1... | collective-permute-start | bytes 3538952 | tf_op jit(solution)/shard_map/ppermute | solution.py:332
  197.1 28.8 %collective-permute-start.16 = (bf16[192,3072]{1,0:T(8,128)(2,1)S(1)}, bf16[192,3072]{1,0:T(8,128)(2,1)S(1)}, u32[]{:S(2)}, u32[]{:S(2)}) collective-permute-start(bf16[192,3072]{1,0:T(8,128)(2,1)S(1)} %copy-done.40), channel_id=1, source_target_pairs={{0,16},{16,0},{1,17},{17,1},{2,18},{18,2},{3,19},{19,3},{4,20},{20... | collective-permute-start | bytes 3538952 | tf_op jit(solution)/shard_map/ppermute | solution.py:332
  216.2 15.1 %collective-permute-start.15 = (bf16[192,1536]{1,0:T(8,128)(2,1)S(1)}, bf16[192,1536]{1,0:T(8,128)(2,1)S(1)}, u32[]{:S(2)}, u32[]{:S(2)}) collective-permute-start(bf16[192,1536]{1,0:T(8,128)(2,1)S(1)} %slice.505), channel_id=1, source_target_pairs={{0,8},{4,12},{8,0},{12,4},{1,9},{5,13},{9,1},{13,5},{2,10},{6,14},... | collective-permute-start | bytes 1769480 | tf_op jit(solution)/shard_map/ppermute | solution.py:332
  217.7 39.5 %collective-permute-start.20 = (bf16[192,3072]{1,0:T(8,128)(2,1)}, bf16[192,3072]{1,0:T(8,128)(2,1)}, u32[]{:S(2)}, u32[]{:S(2)}) collective-permute-start(bf16[192,3072]{1,0:T(8,128)(2,1)} %pad_maximum_fusion.5.refs_0_), channel_id=1, source_target_pairs={{0,16},{16,0},{1,17},{17,1},{2,18},{18,2},{3,19},{19,3},{4,20},{20... | collective-permute-start | bytes 3538952 | tf_op jit(solution)/shard_map/ppermute | solution.py:332
  233.1 14.5 %collective-permute-start.18 = (bf16[192,1536]{1,0:T(8,128)(2,1)}, bf16[192,1536]{1,0:T(8,128)(2,1)}, u32[]{:S(2)}, u32[]{:S(2)}) collective-permute-start(bf16[192,1536]{1,0:T(8,128)(2,1)} %multiply_convert_fusion.4), channel_id=1, source_target_pairs={{0,8},{4,12},{8,0},{12,4},{1,9},{5,13},{9,1},{13,5},{2,10},{6,14},... | collective-permute-start | bytes 1769480 | tf_op jit(solution)/shard_map/ppermute | solution.py:332
  234.5 41.7 %collective-permute-start.21 = (bf16[192,3072]{1,0:T(8,128)(2,1)}, bf16[192,3072]{1,0:T(8,128)(2,1)}, u32[]{:S(2)}, u32[]{:S(2)}) collective-permute-start(bf16[192,3072]{1,0:T(8,128)(2,1)} %collective-permute-done.14.refs_6_), channel_id=1, source_target_pairs={{0,16},{16,0},{1,17},{17,1},{2,18},{18,2},{3,19},{19,3},{4,20},{20... | collective-permute-start | bytes 3538952 | tf_op jit(solution)/shard_map/ppermute | solution.py:332
  237.1 19.0 %all-to-all-start.1 = ((bf16[4,192,384]{2,1,0:T(8,128)(2,1)}), bf16[4,192,384]{2,1,0:T(8,128)(2,1)}, u32[]{:S(2)}, u32[]{:S(2)}) async-start(bf16[4,192,384]{2,1,0:T(8,128)(2,1)} %dynamic-slice_bitcast_fusion), calls=%async_computation.1 | async-start | bytes 1179648 | tf_op jit(solution)/shard_map/all_to_all | solution.py:385
  241.2 294.3 %reduce-scatter.5.cloned.1.call-start = ((), (), s32[]{:S(2)}) async-start(), calls=%async_computation.8 | async-start | bytes 3538944 | tf_op jit(solution)/shard_map/reduce_scatter | solution.py:548
  241.7 42.4 %collective-permute-start.17 = (bf16[192,1536]{1,0:T(8,128)(2,1)}, bf16[192,1536]{1,0:T(8,128)(2,1)}, u32[]{:S(2)}, u32[]{:S(2)}) collective-permute-start(bf16[192,1536]{1,0:T(8,128)(2,1)} %multiply_convert_fusion.4), channel_id=1, source_target_pairs={{0,4},{4,0},{8,12},{12,8},{1,5},{5,1},{9,13},{13,9},{2,6},{6,2},{1... | collective-permute-start | bytes 1769480 | tf_op jit(solution)/shard_map/ppermute | solution.py:332
  247.6 36.5 %collective-permute-start.19 = (bf16[192,1536]{1,0:T(8,128)(2,1)}, bf16[192,1536]{1,0:T(8,128)(2,1)}, u32[]{:S(2)}, u32[]{:S(2)}) collective-permute-start(bf16[192,1536]{1,0:T(8,128)(2,1)} %collective-permute-done.18), channel_id=1, source_target_pairs={{0,4},{4,0},{8,12},{12,8},{1,5},{5,1},{9,13},{13,9},{2,6},{6,2},{1... | collective-permute-start | bytes 1769480 | tf_op jit(solution)/shard_map/ppermute | solution.py:332
  257.2 45.8 %copy-start.10 = (bf16[4,24,8,384]{3,2,0,1:T(8,128)(2,1)}, bf16[4,24,8,384]{3,2,0,1:T(8,128)(2,1)S(1)}, u32[]{:S(2)}) copy-start(bf16[4,24,8,384]{3,2,0,1:T(8,128)(2,1)S(1)} %copy.166) | copy-start | bytes 1769476
  287.3 15.8 %collective-permute-start.22 = (bf16[192,1536]{1,0:T(8,128)(2,1)S(1)}, bf16[192,1536]{1,0:T(8,128)(2,1)S(1)}, u32[]{:S(2)}, u32[]{:S(2)}) collective-permute-start(bf16[192,1536]{1,0:T(8,128)(2,1)S(1)} %bitcast.184), channel_id=1, source_target_pairs={{0,4},{4,0},{8,12},{12,8},{1,5},{5,1},{9,13},{13,9},{2,6},{6,2},{1... | collective-permute-start | bytes 1769480 | tf_op jit(solution)/shard_map/ppermute | solution.py:332
  287.3 15.7 %collective-permute-start.24 = (bf16[192,1536]{1,0:T(8,128)(2,1)S(1)}, bf16[192,1536]{1,0:T(8,128)(2,1)S(1)}, u32[]{:S(2)}, u32[]{:S(2)}) collective-permute-start(bf16[192,1536]{1,0:T(8,128)(2,1)S(1)} %bitcast.185), channel_id=1, source_target_pairs={{0,8},{4,12},{8,0},{12,4},{1,9},{5,13},{9,1},{13,5},{2,10},{6,14},... | collective-permute-start | bytes 1769480 | tf_op jit(solution)/shard_map/ppermute | solution.py:332
  303.0 2.0 collective-permute-start.25
  316.0 7.4 %collective-permute-start.26 = (bf16[384,1536]{1,0:T(8,128)(2,1)}, bf16[384,1536]{1,0:T(8,128)(2,1)}, u32[]{:S(2)}, u32[]{:S(2)}) collective-permute-start(bf16[384,1536]{1,0:T(8,128)(2,1)} %convolution_convert_fusion.4), channel_id=1, source_target_pairs={{0,4},{4,0},{8,12},{12,8},{1,5},{5,1},{9,13},{13,9},{2,6},{6,2},{1... | collective-permute-start | bytes 3538952 | tf_op jit(solution)/shard_map/ppermute | solution.py:332
  331.7 15.9 %collective-permute-start.27 = (bf16[192,1536]{1,0:T(8,128)(2,1)}, bf16[192,1536]{1,0:T(8,128)(2,1)}, u32[]{:S(2)}, u32[]{:S(2)}) collective-permute-start(bf16[192,1536]{1,0:T(8,128)(2,1)} %slice.504), channel_id=1, source_target_pairs={{0,8},{4,12},{8,0},{12,4},{1,9},{5,13},{9,1},{13,5},{2,10},{6,14},... | collective-permute-start | bytes 1769480 | tf_op jit(solution)/shard_map/ppermute | solution.py:332
  334.4 43.7 %collective-permute-start.31 = (bf16[768,1024]{1,0:T(8,128)(2,1)}, bf16[768,1024]{1,0:T(8,128)(2,1)}, u32[]{:S(2)}, u32[]{:S(2)}) collective-permute-start(bf16[768,1024]{1,0:T(8,128)(2,1)} %convolution_convert_fusion.8), channel_id=1, source_target_pairs={{0,16},{16,0},{1,17},{17,1},{2,18},{18,2},{3,19},{19,3},{4,20},{20... | collective-permute-start | bytes 4718600 | tf_op jit(solution)/shard_map/ppermute | solution.py:332
  352.5 15.1 %collective-permute-start.29 = (bf16[192,1536]{1,0:T(8,128)(2,1)}, bf16[192,1536]{1,0:T(8,128)(2,1)}, u32[]{:S(2)}, u32[]{:S(2)}) collective-permute-start(bf16[192,1536]{1,0:T(8,128)(2,1)} %get-tuple-element.108), channel_id=1, source_target_pairs={{0,8},{4,12},{8,0},{12,4},{1,9},{5,13},{9,1},{13,5},{2,10},{6,14},... | collective-permute-start | bytes 1769480 | tf_op jit(solution)/shard_map/ppermute | solution.py:332
  356.4 21.7 %collective-permute-start.23 = (bf16[384,1536]{1,0:T(8,128)(2,1)}, bf16[384,1536]{1,0:T(8,128)(2,1)}, u32[]{:S(2)}, u32[]{:S(2)}) collective-permute-start(bf16[384,1536]{1,0:T(8,128)(2,1)} %convolution_convert_fusion.5), channel_id=1, source_target_pairs={{0,4},{4,0},{8,12},{12,8},{1,5},{5,1},{9,13},{13,9},{2,6},{6,2},{1... | collective-permute-start | bytes 3538952 | tf_op jit(solution)/shard_map/ppermute | solution.py:332
  359.1 69.5 %collective-permute-start.33 = (bf16[768,1024]{1,0:T(8,128)(2,1)}, bf16[768,1024]{1,0:T(8,128)(2,1)}, u32[]{:S(2)}, u32[]{:S(2)}) collective-permute-start(bf16[768,1024]{1,0:T(8,128)(2,1)} %convolution_convert_fusion.7), channel_id=1, source_target_pairs={{0,16},{16,0},{1,17},{17,1},{2,18},{18,2},{3,19},{19,3},{4,20},{20... | collective-permute-start | bytes 4718600 | tf_op jit(solution)/shard_map/ppermute | solution.py:332
  360.6 15.5 %collective-permute-start.28 = (bf16[192,1536]{1,0:T(8,128)(2,1)}, bf16[192,1536]{1,0:T(8,128)(2,1)}, u32[]{:S(2)}, u32[]{:S(2)}) collective-permute-start(bf16[192,1536]{1,0:T(8,128)(2,1)} %get-tuple-element.108), channel_id=1, source_target_pairs={{0,4},{4,0},{8,12},{12,8},{1,5},{5,1},{9,13},{13,9},{2,6},{6,2},{1... | collective-permute-start | bytes 1769480 | tf_op jit(solution)/shard_map/ppermute | solution.py:332
  367.6 8.6 %collective-permute-start.30 = (bf16[192,1536]{1,0:T(8,128)(2,1)}, bf16[192,1536]{1,0:T(8,128)(2,1)}, u32[]{:S(2)}, u32[]{:S(2)}) collective-permute-start(bf16[192,1536]{1,0:T(8,128)(2,1)} %collective-permute-done.29), channel_id=1, source_target_pairs={{0,4},{4,0},{8,12},{12,8},{1,5},{5,1},{9,13},{13,9},{2,6},{6,2},{1... | collective-permute-start | bytes 1769480 | tf_op jit(solution)/shard_map/ppermute | solution.py:332
  382.0 46.6 %collective-permute-start.32 = (bf16[192,1536]{1,0:T(8,128)(2,1)S(1)}, bf16[192,1536]{1,0:T(8,128)(2,1)S(1)}, u32[]{:S(2)}, u32[]{:S(2)}) collective-permute-start(bf16[192,1536]{1,0:T(8,128)(2,1)S(1)} %slice.503), channel_id=1, source_target_pairs={{0,8},{4,12},{8,0},{12,4},{1,9},{5,13},{9,1},{13,5},{2,10},{6,14},... | collective-permute-start | bytes 1769480 | tf_op jit(solution)/shard_map/ppermute | solution.py:332
  385.9 35.7 %copy-start.19 = (f32[768,1024]{1,0:T(8,128)S(1)}, f32[768,1024]{1,0:T(8,128)}, u32[]{:S(2)}) copy-start(f32[768,1024]{1,0:T(8,128)} %fusion.34) | copy-start | bytes 9437188
  424.9 40.9 %collective-permute-start.47 = (bf16[384,1024]{1,0:T(8,128)(2,1)}, bf16[384,1024]{1,0:T(8,128)(2,1)}, u32[]{:S(2)}, u32[]{:S(2)}) collective-permute-start(bf16[384,1024]{1,0:T(8,128)(2,1)} %pad_maximum_fusion.8), channel_id=1, source_target_pairs={{0,1},{1,0},{2,3},{3,2},{4,5},{5,4},{6,7},{7,6},{8,9},{9,8},{10,11... | collective-permute-start | bytes 2359304 | tf_op jit(solution)/shard_map/ppermute | solution.py:332
  435.6 19.9 %collective-permute-start.34 = (bf16[384,1536]{1,0:T(8,128)(2,1)}, bf16[384,1536]{1,0:T(8,128)(2,1)}, u32[]{:S(2)}, u32[]{:S(2)}) collective-permute-start(bf16[384,1536]{1,0:T(8,128)(2,1)} %fusion.4), channel_id=1, source_target_pairs={{0,4},{4,0},{8,12},{12,8},{1,5},{5,1},{9,13},{13,9},{2,6},{6,2},{1... | collective-permute-start | bytes 3538952 | tf_op jit(solution)/shard_map/ppermute | solution.py:332
  436.8 50.4 %all-to-all-start.2 = ((bf16[192,4,384]{2,0,1:T(8,128)(2,1)}), bf16[192,4,384]{2,0,1:T(8,128)(2,1)}, u32[]{:S(2)}, u32[]{:S(2)}) async-start(bf16[192,4,384]{2,0,1:T(8,128)(2,1)} %bitcast.164), calls=%async_computation.2 | async-start | bytes 1179648 | tf_op jit(solution)/shard_map/all_to_all | solution.py:471
  441.5 130.2 %reduce-scatter.3.cloned.1.call-start = ((), (), s32[]{:S(2)}) async-start(), calls=%async_computation.7 | async-start | bytes 1327104 | tf_op jit(solution)/shard_map/reduce_scatter | solution.py:548
  447.0 56.6 %collective-permute-start.39 = (bf16[768,1536]{1,0:T(8,128)(2,1)}, bf16[768,1536]{1,0:T(8,128)(2,1)}, u32[]{:S(2)}, u32[]{:S(2)}) collective-permute-start(bf16[768,1536]{1,0:T(8,128)(2,1)} %convolution_convert_fusion.1), channel_id=1, source_target_pairs={{0,16},{16,0},{1,17},{17,1},{2,18},{18,2},{3,19},{19,3},{4,20},{20... | collective-permute-start | bytes 7077896 | tf_op jit(solution)/shard_map/ppermute | solution.py:332
  453.6 79.9 %collective-permute-start.45 = (bf16[384,1024]{1,0:T(8,128)(2,1)}, bf16[384,1024]{1,0:T(8,128)(2,1)}, u32[]{:S(2)}, u32[]{:S(2)}) collective-permute-start(bf16[384,1024]{1,0:T(8,128)(2,1)} %pad_maximum_fusion.7), channel_id=1, source_target_pairs={{0,1},{1,0},{2,3},{3,2},{4,5},{5,4},{6,7},{7,6},{8,9},{9,8},{10,11... | collective-permute-start | bytes 2359304 | tf_op jit(solution)/shard_map/ppermute | solution.py:332
  461.4 14.9 %collective-permute-start.35 = (bf16[192,1536]{1,0:T(8,128)(2,1)}, bf16[192,1536]{1,0:T(8,128)(2,1)}, u32[]{:S(2)}, u32[]{:S(2)}) collective-permute-start(bf16[192,1536]{1,0:T(8,128)(2,1)} %slice.502), channel_id=1, source_target_pairs={{0,8},{4,12},{8,0},{12,4},{1,9},{5,13},{9,1},{13,5},{2,10},{6,14},... | collective-permute-start | bytes 1769480 | tf_op jit(solution)/shard_map/ppermute | solution.py:332
  462.4 22.5 %copy-start.14 = (f32[192,1536]{1,0:T(8,128)S(1)}, f32[192,1536]{1,0:T(8,128)}, u32[]{:S(2)}) copy-start(f32[192,1536]{1,0:T(8,128)} %get-tuple-element.203) | copy-start | bytes 3538948
  487.2 15.9 %collective-permute-start.37 = (bf16[4,1,192,384]{3,2,1,0:T(8,128)(2,1)}, bf16[4,1,192,384]{3,2,1,0:T(8,128)(2,1)}, u32[]{:S(2)}, u32[]{:S(2)}) collective-permute-start(bf16[4,1,192,384]{3,2,1,0:T(8,128)(2,1)} %bitcast.31), channel_id=1, source_target_pairs={{0,8},{4,12},{8,0},{12,4},{1,9},{5,13},{9,1},{13,5},{2,10},{6,14},... | collective-permute-start | bytes 1769480 | tf_op jit(solution)/shard_map/ppermute | solution.py:332
  489.8 56.8 %collective-permute-start.48 = (bf16[192,1024]{1,0:T(8,128)(2,1)}, bf16[192,1024]{1,0:T(8,128)(2,1)S(1)}, u32[]{:S(2)}, u32[]{:S(2)}) collective-permute-start(bf16[192,1024]{1,0:T(8,128)(2,1)} %fusion.50), channel_id=1, source_target_pairs={{0,2},{1,3},{2,0},{3,1},{4,6},{5,7},{6,4},{7,5},{8,10},{9,11},{10,... | collective-permute-start | bytes 1179656 | tf_op jit(solution)/shard_map/ppermute | solution.py:332
  496.4 15.9 %collective-permute-start.36 = (bf16[4,1,192,384]{3,2,1,0:T(8,128)(2,1)}, bf16[4,1,192,384]{3,2,1,0:T(8,128)(2,1)}, u32[]{:S(2)}, u32[]{:S(2)}) collective-permute-start(bf16[4,1,192,384]{3,2,1,0:T(8,128)(2,1)} %bitcast.31), channel_id=1, source_target_pairs={{0,4},{4,0},{8,12},{12,8},{1,5},{5,1},{9,13},{13,9},{2,6},{6,2},{1... | collective-permute-start | bytes 1769480 | tf_op jit(solution)/shard_map/ppermute | solution.py:332
  497.4 33.8 %all-to-all-start.3 = ((bf16[208,4,384]{2,0,1:T(8,128)(2,1)}), bf16[208,4,384]{2,0,1:T(8,128)(2,1)S(1)}, u32[]{:S(2)}, u32[]{:S(2)}) async-start(bf16[208,4,384]{2,0,1:T(8,128)(2,1)} %bitcast.195), calls=%async_computation.3 | async-start | bytes 1277952 | tf_op jit(solution)/shard_map/all_to_all | solution.py:471
  503.1 34.4 %collective-permute-start.38 = (bf16[4,1,192,384]{3,2,1,0:T(8,128)(2,1)}, bf16[4,1,192,384]{3,2,1,0:T(8,128)(2,1)}, u32[]{:S(2)}, u32[]{:S(2)}) collective-permute-start(bf16[4,1,192,384]{3,2,1,0:T(8,128)(2,1)} %collective-permute-done.37), channel_id=1, source_target_pairs={{0,4},{4,0},{8,12},{12,8},{1,5},{5,1},{9,13},{13,9},{2,6},{6,2},{1... | collective-permute-start | bytes 1769480 | tf_op jit(solution)/shard_map/ppermute | solution.py:332
  510.6 54.9 %collective-permute-start.40 = (bf16[384,1536]{1,0:T(8,128)(2,1)}, bf16[384,1536]{1,0:T(8,128)(2,1)}, u32[]{:S(2)}, u32[]{:S(2)}) collective-permute-start(bf16[384,1536]{1,0:T(8,128)(2,1)} %pad_maximum_fusion.6), channel_id=1, source_target_pairs={{0,1},{1,0},{2,3},{3,2},{4,5},{5,4},{6,7},{7,6},{8,9},{9,8},{10,11... | collective-permute-start | bytes 3538952 | tf_op jit(solution)/shard_map/ppermute | solution.py:332
  531.2 15.5 %collective-permute-start.42 = (bf16[4,1,208,384]{3,2,1,0:T(8,128)(2,1)S(1)}, bf16[4,1,208,384]{3,2,1,0:T(8,128)(2,1)}, u32[]{:S(2)}, u32[]{:S(2)}) collective-permute-start(bf16[4,1,208,384]{3,2,1,0:T(8,128)(2,1)S(1)} %bitcast.191), channel_id=1, source_target_pairs={{0,8},{4,12},{8,0},{12,4},{1,9},{5,13},{9,1},{13,5},{2,10},{6,14},... | collective-permute-start | bytes 1916936 | tf_op jit(solution)/shard_map/ppermute | solution.py:332
  533.4 14.0 %collective-permute-start.41 = (bf16[4,1,208,384]{3,2,1,0:T(8,128)(2,1)S(1)}, bf16[4,1,208,384]{3,2,1,0:T(8,128)(2,1)S(1)}, u32[]{:S(2)}, u32[]{:S(2)}) collective-permute-start(bf16[4,1,208,384]{3,2,1,0:T(8,128)(2,1)S(1)} %bitcast.193), channel_id=1, source_target_pairs={{0,4},{4,0},{8,12},{12,8},{1,5},{5,1},{9,13},{13,9},{2,6},{6,2},{1... | collective-permute-start | bytes 1916936 | tf_op jit(solution)/shard_map/ppermute | solution.py:332
  537.5 34.2 %collective-permute-start.49 = (bf16[192,1024]{1,0:T(8,128)(2,1)}, bf16[192,1024]{1,0:T(8,128)(2,1)S(1)}, u32[]{:S(2)}, u32[]{:S(2)}) collective-permute-start(bf16[192,1024]{1,0:T(8,128)(2,1)} %fusion.48), channel_id=1, source_target_pairs={{0,2},{1,3},{2,0},{3,1},{4,6},{5,7},{6,4},{7,5},{8,10},{9,11},{10,... | collective-permute-start | bytes 1179656 | tf_op jit(solution)/shard_map/ppermute | solution.py:332
  546.6 29.0 %collective-permute-start.43 = (bf16[4,1,208,384]{3,2,1,0:T(8,128)(2,1)}, bf16[4,1,208,384]{3,2,1,0:T(8,128)(2,1)S(1)}, u32[]{:S(2)}, u32[]{:S(2)}) collective-permute-start(bf16[4,1,208,384]{3,2,1,0:T(8,128)(2,1)} %collective-permute-done.42), channel_id=1, source_target_pairs={{0,4},{4,0},{8,12},{12,8},{1,5},{5,1},{9,13},{13,9},{2,6},{6,2},{1... | collective-permute-start | bytes 1916936 | tf_op jit(solution)/shard_map/ppermute | solution.py:332
  570.7 29.2 %collective-permute-start.46 = (bf16[192,1536]{1,0:T(8,128)(2,1)}, bf16[192,1536]{1,0:T(8,128)(2,1)}, u32[]{:S(2)}, u32[]{:S(2)}) collective-permute-start(bf16[192,1536]{1,0:T(8,128)(2,1)} %fusion.26), channel_id=1, source_target_pairs={{0,2},{1,3},{2,0},{3,1},{4,6},{5,7},{6,4},{7,5},{8,10},{9,11},{10,... | collective-permute-start | bytes 1769480 | tf_op jit(solution)/shard_map/ppermute | solution.py:332
  580.7 4.7 collective-permute-start.44
  (68 other events, 401.6 us)
Sparse Core Ops, SparseCore 0:
  89.1 61.9 all-gather.1
  360.7 97.0 reduce-scatter.4
  496.5 73.1 reduce-scatter.2

commit v3 on v2

--- a/solution.py
+++ b/solution.py
@@ -485,14 +485,8 @@
         hops = list(range(wid))
         hops = [0, 1] + hops[:1:-1] if wid > 2 else hops
 
-        def along_wid(own, *first):
-            if first:
-                own = after(own, *first)
-            made = [own]
-            for k in hops[1:]:
-                sent = own if k in (1, wid - 1) else after(own, *made[1:])
-                made.append(lax.ppermute(sent, "wid", [(i, (i + k) % wid) for i in range(wid)]))
-            return made
+        def hop(own, k, *first):
+            return lax.ppermute(after(own, *first) if first else own, "wid", [(i, (i + k) % wid) for i in range(wid)])
 
         def over_dp(piece, *first):
             return [piece] + [lane_y.send(piece, "dp", [(i, (i + by) % dp) for i in range(dp)], *first) for by in range(1, dp)]
@@ -507,11 +501,17 @@
         width_in = 4 * heads * HD
         columns = [in_weight[:, c, h * HD : (h + 1) * HD] for h in range(heads) for c in range(4)]
         small = [beta_weight, gain_attn[:, None], gain_mlp[:, None], jnp.zeros((shard, HD - heads - 2), BF)]
-        along = along_wid(jnp.concatenate(columns + small, axis=1))
+        own_in = jnp.concatenate(columns + small, axis=1)
         own_late = jnp.concatenate([gate_weight, up_weight, down_weight.T], axis=1)
-        inputs_all = jnp.concatenate(gather_hid(token_in), axis=0).astype(F32)
-        pieces = [over_dp(a) for a in along]
-        late_along = along_wid(own_late, along[-1])
+        along = [own_in] + [hop(own_in, k) for k in hops[1:3]]
+        pieces = [over_dp(own_in)]
+        tokens_hid = gather_hid(token_in)
+        along = along[:1] + [after(a, token_in) for a in along[1:]]
+        for k in hops[3:]:
+            along.append(hop(own_in, k, *along[1:], pieces[0][-1], tokens_hid[hid // 2]))
+        inputs_all = jnp.concatenate(tokens_hid, axis=0).astype(F32)
+        pieces += [over_dp(a) for a in along[1:]]
+        late_along = [own_late] + [hop(own_late, k, along[-1]) for k in hops[1:3]]
         late = [over_dp(own_late)]
         weight_in, small = whole(pieces, (width_in, HD))
         weight_beta = small[:, :heads]
@@ -520,24 +520,29 @@
 
         scale_all = lax.rsqrt(jnp.mean(inputs_all * inputs_all, axis=-1, keepdims=True) + 1e-06)
         normed = (inputs_all * scale_all * gain_one).astype(BF)
-        projected = dot(normed, weight_in, 1, 0, BF)
+        projected = dot(after(normed, late[0][-1]), weight_in, 1, 0, BF)
         order = me_hid.reshape(1)
         logits = reorder(dot(normed, weight_beta, 1, 0)).T
-        late += [over_dp(a) for a in late_along[1:]]
+        for k in hops[3:]:
+            late_along.append(hop(own_late, k, *late_along[1:]))
+        late += [over_dp(a) for a in late_along[1:3]]
+        token_grad = to_tokens(after(cotangent, projected))
         attended, *saved = attend_fwd(order, after(projected, *late_along[1:3]), logits, segments, quarter)
-        attended = after(attended, late[1][-1])
-        token_grad = to_tokens(after(cotangent, attended))
+        attended = after(attended, late[1][-1], token_grad)
 
         branch_flow = Flow(summing_hid(lambda ks: dot(rows_of(attended, ks), weight_out, 1, 1)))
         branch_flow.step()
-        branch_flow.step(late_along[-1])
+        branch_flow.step(*late_along[3:])
         branch = branch_flow.finish(late[2][-1])
+        late += [over_dp(a) for a in late_along[3:]]
         inputs = inputs_all[:quarter]
         scale_one = scale_all[:quarter]
         middle = inputs + branch
         scale_two = lax.rsqrt(jnp.mean(middle * middle, axis=-1, keepdims=True) + 1e-06)
-        mixed = jnp.concatenate(gather_hid((middle * scale_two * gain_two).astype(BF)), axis=0)
-        grad_all = jnp.concatenate(gather_hid(after(token_grad, mixed)), axis=0)
+        mixed_own = (middle * scale_two * gain_two).astype(BF)
+        mixed = gather_hid(mixed_own)
+        mixed = jnp.concatenate(mixed[:-1] + [after(mixed[-1], late[-1][-1])], axis=0)
+        grad_all = jnp.concatenate(gather_hid(after(token_grad, mixed_own)), axis=0)
         weight_mlp, weight_down = whole(late, (2 * hidden, hidden))
         gate_up = dot(mixed, weight_mlp, 1, 0)
         gate, upward = gate_up[:, :hidden], gate_up[:, hidden:]

time: 615 us -> 591 us (0.961)
  waiting for transfers between devices: 247 us -> 222 us
    ppermute x6, waiting for transfers between devices: 99.2 us -> 64.7 us  [hop(): lax.ppermute(after(own, *first) if first else own, 'wid', [(i, (i + k) %...]
    all_to_all x2, waiting for transfers between devices: 8.49 us -> 27.8 us  [to_tokens(): lax.all_to_all(mine.reshape(wid * quarter, slice_width), 'wid', split_axi...]
    ppermute x43, waiting for transfers between devices: 124 us -> 115 us  [send(): self.done.append(lax.ppermute(value, axis, pairs))]
    unnamed x161 -> x165, local copies, waits for them, and re-layouts: 16.5 us -> 19.5 us
  transfers between devices with their start and end apart: 57 -> 57, of which waited for: 21 -> 20; matrix products, arithmetic and copies ran while one was open for 28% -> 29% of each run, Pallas kernels for 13% -> 13%
where the time goes in v3:
time: 591 us; the launch traced here: 584 us
  waiting for transfers between devices  222 us (38%)
  matrix products  83.6 us (14%)
  Pallas kernels  76.8 us (13%)
  starting transfers between devices  65.8 us (11%)
  other arithmetic  61.3 us (10%)
  local copies, waits for them, and re-layouts  58.4 us (10%)
  between operations  15.5 us (3%)
    ppermute x43, waiting for transfers between devices, send(): self.done.append(lax.ppermute(value, axis, pairs))  115 us
    dot_general x24, matrix products, dot(): lax.dot_general(a, b, (((ca,), (cb,)), ((), ())), preferred_element_type=...  83.6 us
    ppermute x6, waiting for transfers between devices, hop(): lax.ppermute(after(own, *first) if first else own, 'wid', [(i, (i + k) %...  64.7 us
    ppermute x43, starting transfers between devices, send(): self.done.append(lax.ppermute(value, axis, pairs))  37.4 us
    pallas_call x1, Pallas kernels, attend_bwd(): pl.pallas_call(functools.partial(bwd_kernel, quarter // STEP), grid=(head...  34.6 us
    pallas_call x1, Pallas kernels, attend_fwd(): pl.pallas_call(functools.partial(fwd_kernel, quarter // STEP), grid=(head...  29.2 us
    all_to_all x2, waiting for transfers between devices, to_tokens(): lax.all_to_all(mine.reshape(wid * quarter, slice_width), 'wid', split_axi...  27.8 us
    unnamed x165, local copies, waits for them, and re-layouts  19.5 us
  transfers between devices with their start and end apart: 57, of which 20 were waited for; matrix products, arithmetic and copies ran while one was open for 29% of the time, Pallas kernels for 13%

profile of v3, /device:TPU:0, one launch (start us, length us, event | category | flops | bytes accessed | tf_op | source)
XLA Modules:
  0.0 583.9 jit_solution(16424213461310369110)
XLA Ops:
  9.7 6.3 %all-to-all-start = ((bf16[4,192,384]{2,1,0:T(8,128)(2,1)}), bf16[4,192,384]{2,1,0:T(8,128)(2,1)S(1)}, u32[]{:S(2)}, u32[]{:S(2)}) async-start(bf16[4,192,384]{2,1,0:T(8,128)(2,1)} %dynamic-slice_bitcast_fusion.1), calls=%async_computation | async-start | bytes 1179648 | tf_op jit(solution)/shard_map/all_to_all | solution.py:385
  18.1 2.1 collective-permute-start.4
  23.5 23.1 %all-to-all-done = bf16[4,192,384]{2,1,0:T(8,128)(2,1)S(1)} async-done(((bf16[4,192,384]{2,1,0:T(8,128)(2,1)}), bf16[4,192,384]{2,1,0:T(8,128)(2,1)S(1)}, u32[]{:S(2)}, u32[]{:S(2)}) %all-to-all-start) | async-done | bytes 589856 | tf_op jit(solution)/shard_map/all_to_all | solution.py:385
  48.3 7.1 %collective-permute-done.6.refs_4_ = bf16[192,1664]{1,0:T(8,128)(2,1)} collective-permute-done((bf16[192,1664]{1,0:T(8,128)(2,1)S(1)}, bf16[192,1664]{1,0:T(8,128)(2,1)}, u32[]{:S(2)}, u32[]{:S(2)}) %collective-permute-start.6) | collective-permute-done | bytes 639008 | tf_op jit(solution)/shard_map/ppermute | solution.py:489
  55.4 4.5 collective-permute-done.1
  62.7 29.8 %collective-permute-done.8.refs_6_ = bf16[192,1664]{1,0:T(8,128)(2,1)} collective-permute-done((bf16[192,1664]{1,0:T(8,128)(2,1)S(1)}, bf16[192,1664]{1,0:T(8,128)(2,1)}, u32[]{:S(2)}, u32[]{:S(2)}) %collective-permute-start.8) | collective-permute-done | bytes 639008 | tf_op jit(solution)/shard_map/ppermute | solution.py:489
  94.1 2.2 pad_maximum_fusion.5.refs_0_
  98.2 3.8 collective-permute-start.12
  102.0 14.5 %collective-permute-done.9.refs_7_ = bf16[192,1664]{1,0:T(8,128)(2,1)} collective-permute-done((bf16[192,1664]{1,0:T(8,128)(2,1)}, bf16[192,1664]{1,0:T(8,128)(2,1)}, u32[]{:S(2)}, u32[]{:S(2)}) %collective-permute-start.9) | collective-permute-done | bytes 639008 | tf_op jit(solution)/shard_map/ppermute | solution.py:332
  116.5 5.1 assemble.2
  126.1 12.8 %collective-permute-done.10.refs_1_ = bf16[192,3072]{1,0:T(8,128)(2,1)S(1)} collective-permute-done((bf16[192,3072]{1,0:T(8,128)(2,1)}, bf16[192,3072]{1,0:T(8,128)(2,1)S(1)}, u32[]{:S(2)}, u32[]{:S(2)}) %collective-permute-start.10) | collective-permute-done | bytes 1179680 | tf_op jit(solution)/shard_map/ppermute | solution.py:332
  139.7 5.0 convolution_convert_fusion.2.proj_ref
  146.7 4.2 all-to-all-start.1
  151.1 10.8 %collective-permute-done.12.refs_4_ = bf16[192,3072]{1,0:T(8,128)(2,1)} collective-permute-done((bf16[192,3072]{1,0:T(8,128)(2,1)}, bf16[192,3072]{1,0:T(8,128)(2,1)}, u32[]{:S(2)}, u32[]{:S(2)}) %collective-permute-start.12) | collective-permute-done | bytes 1179680 | tf_op jit(solution)/shard_map/ppermute | solution.py:489
  164.7 29.2 %attend_fwd.1 = (bf16[768,384]{1,0:T(8,128)(2,1)}, f32[3,768,768]{2,1,0:T(8,128)}, f32[3,6,768,128]{3,2,1,0:T(8,128)}, f32[3,768,128]{2,1,0:T(8,128)}, f32[3,768...) custom-call(s32[1]{0:T(128)} %bitcast.3.order_ref, ...), custom_call_target="tpu_custom_call" | custom-call | flops 32999999488 | bytes 30000000 | tf_op jit(solution)/shard_map/attend_fwd/pallas_call | solution.py:157
  193.9 4.7 all-to-all-done.1
  202.5 2.3 convolution_convert_fusion.6
  206.5 17.0 %collective-permute-done.15.refs_6_ = bf16[192,3072]{1,0:T(8,128)(2,1)} collective-permute-done((bf16[192,3072]{1,0:T(8,128)(2,1)}, bf16[192,3072]{1,0:T(8,128)(2,1)}, u32[]{:S(2)}, u32[]{:S(2)}) %collective-permute-start.15) | collective-permute-done | bytes 1179680 | tf_op jit(solution)/shard_map/ppermute | solution.py:489
  228.1 5.8 collective-permute-done.17.refs_5_
  233.9 5.4 collective-permute-done.16
  243.1 14.2 %collective-permute-done.19 = bf16[192,1536]{1,0:T(8,128)(2,1)S(1)} collective-permute-done((bf16[192,1536]{1,0:T(8,128)(2,1)S(1)}, bf16[192,1536]{1,0:T(8,128)(2,1)S(1)}, u32[]{:S(2)}, u32[]{:S(2)}) %collective-permute-start.19) | collective-permute-done | bytes 589856 | tf_op jit(solution)/shard_map/ppermute | solution.py:332
  259.7 8.0 %assemble.3 = (bf16[1536,2048]{1,0:T(8,128)(2,1)}, bf16[1536,1024]{1,0:T(8,128)(2,1)}) custom-call(s32[8]{0:T(128)} %stack.44.place_ref, bf16[192,3072]{1,0:T(8,128)(2,1)} %pad_maximum_fusion.5.refs_0_, bf16[192,3072]{1,0:T(8,128)(2,1)} %copy-done.41, bf16[192,3072]{1,0:T(8,128)(2,1)} %collective-permute-done.11.refs_2_, ...), custom_call_target="tpu_custom_call" | custom-call | bytes 18874368 | tf_op jit(solution)/shard_map/assemble/pallas_call | solution.py:308
  268.4 7.3 %fusion.105 = f32[768,2048]{1,0:T(8,128)S(1)} fusion(bf16[1536,2048]{1,0:T(8,128)(2,1)} %get-tuple-element.107, bf16[192,1536]{1,0:T(8,128)(2,1)S(1)} %collective-permute-done.20, bf16[192,1536]{1,0:T(8,128)(2,1)S(1)} %collective-permute-done.19, bf16[192,1536]{1,0:T(8,128)(2,1)S(1)} %collective-permute-done.18, ...), kind=kOutput, calls=%fused_computation.255 | convolution fusion | flops 4841275392 | bytes 14942208 | tf_op jit(solution)/shard_map/dot_general | solution.py:378
  276.0 2.5 copy-done.71
  278.5 5.3 multiply_convert_fusion.2
  286.1 3.8 convolution_convert_fusion.4
  295.0 2.6 convolution_convert_fusion.8
  297.6 5.9 %convolution_add_fusion.2 = f32[384,1536]{1,0:T(8,128)S(1)} fusion(bf16[1536,2048]{1,0:T(8,128)(2,1)} %get-tuple-element.107, bf16[384,1536]{1,0:T(8,128)(2,1)} %collective-permute-done.26, bf16[192,2048]{1,0:T(8,128)(2,1)S(1)} %copy-done.45, bf16[192,2048]{1,0:T(8,128)(2,1)S(1)} %copy-done.44), kind=kOutput, calls=%fused_computation.24 | convolution fusion | flops 2420244480 | bytes 11403264 | tf_op jit(solution)/shard_map/dot_general | solution.py:378
  310.0 4.2 convolution_convert_fusion
  314.3 7.5 %collective-permute-done.27 = bf16[192,1536]{1,0:T(8,128)(2,1)} collective-permute-done((bf16[192,1536]{1,0:T(8,128)(2,1)}, bf16[192,1536]{1,0:T(8,128)(2,1)}, u32[]{:S(2)}, u32[]{:S(2)}) %collective-permute-start.27) | collective-permute-done | bytes 589856 | tf_op jit(solution)/shard_map/ppermute | solution.py:332
  323.7 2.9 fusion.106
  328.1 2.5 convolution_convert_fusion.5
  330.6 2.6 convolution_convert_fusion.7
  335.0 6.7 %collective-permute-done.29 = bf16[192,1536]{1,0:T(8,128)(2,1)} collective-permute-done((bf16[192,1536]{1,0:T(8,128)(2,1)}, bf16[192,1536]{1,0:T(8,128)(2,1)}, u32[]{:S(2)}, u32[]{:S(2)}) %collective-permute-start.29) | collective-permute-done | bytes 589856 | tf_op jit(solution)/shard_map/ppermute | solution.py:332
  341.7 4.9 fusion.34
  346.6 3.0 fusion.32
  353.3 2.8 convolution_add_fusion.3
  357.7 2.5 fusion.116.dog_ref
  360.2 34.6 %attend_bwd.1 = (bf16[768,1536]{1,0:T(8,128)(2,1)}, f32[3,1,768]{2,1,0:T(1,128)}) custom-call(s32[1]{0:T(128)} %bitcast.3.order_ref, bf16[768,1536]{1,0:T(8,128)(2,1)} %convolution_convert_fusion.2.proj_ref, f32[3,1,768]{2,1,0:T(1,128)} %reshape.176.lg_ref, f32[768,384]{1,0:T(8,128)} %fusion.116.dog_ref, f32[3,768,768]{2,1,0:T(8,128)} %get-tuple-element.123.pr_ref, ...), custom_call_target="tpu_custom_call" | custom-call | flops 15000000512 | bytes 10000000 | tf_op jit(solution)/shard_map/attend_bwd/pallas_call | solution.py:280
  400.4 2.0 fusion.70
  403.6 5.5 fusion.4
  410.4 4.2 all-to-all-start.2
  414.9 5.3 convolution_convert_fusion.1
  421.8 2.2 convert_add_fusion.2
  428.7 4.8 fusion.3
  439.1 10.7 %collective-permute-done.35 = bf16[192,1536]{1,0:T(8,128)(2,1)} collective-permute-done((bf16[192,1536]{1,0:T(8,128)(2,1)}, bf16[192,1536]{1,0:T(8,128)(2,1)}, u32[]{:S(2)}, u32[]{:S(2)}) %collective-permute-start.35) | collective-permute-done | bytes 589856 | tf_op jit(solution)/shard_map/ppermute | solution.py:332
  449.8 2.7 multiply_reduce_fusion.3
  458.4 2.2 add_convert_fusion
  461.3 2.1 fusion.50
  463.3 2.2 collective-permute-start.48
  465.6 4.2 convolution_convert_fusion.3
  470.8 3.8 all-to-all-start.3
  477.0 4.4 convert_add_fusion
  489.6 15.3 %all-to-all-done.3 = bf16[208,4,384]{2,0,1:T(8,128)(2,1)S(1)} async-done(((bf16[208,4,384]{2,0,1:T(8,128)(2,1)}), bf16[208,4,384]{2,0,1:T(8,128)(2,1)S(1)}, u32[]{:S(2)}, u32[]{:S(2)}) %all-to-all-start.3) | async-done | bytes 639008 | tf_op jit(solution)/shard_map/all_to_all | solution.py:471
  507.5 2.1 fusion.48
  509.6 2.0 convert_bitcast_fusion
  517.2 3.5 collective-permute-done.42
  522.8 2.3 fusion.51
  525.1 14.1 %collective-permute-done.40 = bf16[384,1536]{1,0:T(8,128)(2,1)} collective-permute-done((bf16[384,1536]{1,0:T(8,128)(2,1)}, bf16[384,1536]{1,0:T(8,128)(2,1)}, u32[]{:S(2)}, u32[]{:S(2)}) %collective-permute-start.40) | collective-permute-done | bytes 1179680 | tf_op jit(solution)/shard_map/ppermute | solution.py:332
  539.2 2.4 fusion.26
  541.6 2.0 slice.304
  547.5 2.3 fusion.49
  556.7 2.7 bitcast_convert_fusion
  560.6 13.1 %collective-permute-done.46 = bf16[192,1536]{1,0:T(8,128)(2,1)} collective-permute-done((bf16[192,1536]{1,0:T(8,128)(2,1)}, bf16[192,1536]{1,0:T(8,128)(2,1)}, u32[]{:S(2)}, u32[]{:S(2)}) %collective-permute-start.46) | collective-permute-done | bytes 589856 | tf_op jit(solution)/shard_map/ppermute | solution.py:332
  (361 shorter events, 130.6 us)
Async XLA Ops:
  9.7 37.0 %all-to-all-start = ((bf16[4,192,384]{2,1,0:T(8,128)(2,1)}), bf16[4,192,384]{2,1,0:T(8,128)(2,1)S(1)}, u32[]{:S(2)}, u32[]{:S(2)}) async-start(bf16[4,192,384]{2,1,0:T(8,128)(2,1)} %dynamic-slice_bitcast_fusion.1), calls=%async_computation | async-start | bytes 1179648 | tf_op jit(solution)/shard_map/all_to_all | solution.py:385
  16.1 186.4 %all-gather.2.cloned.1.call-start = ((), (), s32[]{:S(2)}) async-start(), calls=%async_computation.6 | async-start | bytes 1327104 | tf_op jit(solution)/shard_map/all_gather | solution.py:481
  17.4 76.8 %copy-start.54 = (bf16[1024,192]{0,1:T(8,128)(2,1)S(1)}, bf16[1024,192]{0,1:T(8,128)(2,1)}, u32[]{:S(2)}) copy-start(bf16[1024,192]{0,1:T(8,128)(2,1)} %param.21) | copy-start | bytes 1179652
  18.1 80.0 %copy-start.21 = (bf16[192,1664]{1,0:T(8,128)(2,1)}, bf16[192,1664]{1,0:T(8,128)(2,1)S(1)}, u32[]{:S(2)}) copy-start(bf16[192,1664]{1,0:T(8,128)(2,1)S(1)} %concatenate.104.refs_0_) | copy-start | bytes 1916932
  18.1 30.2 %collective-permute-start.4 = (bf16[192,1664]{1,0:T(8,128)(2,1)S(1)}, bf16[192,1664]{1,0:T(8,128)(2,1)}, u32[]{:S(2)}, u32[]{:S(2)}) collective-permute-start(bf16[192,1664]{1,0:T(8,128)(2,1)S(1)} %concatenate.104.refs_0_), channel_id=1, source_target_pairs={{0,1},{1,2},{2,3},{3,0},{4,5},{5,6},{6,7},{7,4},{8,9},{9,10},{10,1... | collective-permute-start | bytes 1916936 | tf_op jit(solution)/shard_map/ppermute | solution.py:489
  20.2 35.2 %collective-permute-start.6 = (bf16[192,1664]{1,0:T(8,128)(2,1)S(1)}, bf16[192,1664]{1,0:T(8,128)(2,1)}, u32[]{:S(2)}, u32[]{:S(2)}) collective-permute-start(bf16[192,1664]{1,0:T(8,128)(2,1)S(1)} %concatenate.104.refs_0_), channel_id=1, source_target_pairs={{0,3},{1,0},{2,1},{3,2},{4,7},{5,4},{6,5},{7,6},{8,11},{9,8},{10,9... | collective-permute-start | bytes 1916936 | tf_op jit(solution)/shard_map/ppermute | solution.py:489
  22.0 33.4 %collective-permute-start.3 = (bf16[192,1664]{1,0:T(8,128)(2,1)S(1)}, bf16[192,1664]{1,0:T(8,128)(2,1)}, u32[]{:S(2)}, u32[]{:S(2)}) collective-permute-start(bf16[192,1664]{1,0:T(8,128)(2,1)S(1)} %concatenate.104.refs_0_), channel_id=1, source_target_pairs={{0,16},{16,0},{1,17},{17,1},{2,18},{18,2},{3,19},{19,3},{4,20},{20... | collective-permute-start | bytes 1916936 | tf_op jit(solution)/shard_map/ppermute | solution.py:332
  46.8 13.1 %collective-permute-start.1 = (bf16[192,1536]{1,0:T(8,128)(2,1)S(1)}, bf16[192,1536]{1,0:T(8,128)(2,1)S(1)}, u32[]{:S(2)}, u32[]{:S(2)}) collective-permute-start(bf16[192,1536]{1,0:T(8,128)(2,1)S(1)} %bitcast.178), channel_id=1, source_target_pairs={{0,8},{4,12},{8,0},{12,4},{1,9},{5,13},{9,1},{13,5},{2,10},{6,14},... | collective-permute-start | bytes 1769480 | tf_op jit(solution)/shard_map/ppermute | solution.py:332
  59.9 32.7 %collective-permute-start.8 = (bf16[192,1664]{1,0:T(8,128)(2,1)S(1)}, bf16[192,1664]{1,0:T(8,128)(2,1)}, u32[]{:S(2)}, u32[]{:S(2)}) collective-permute-start(bf16[192,1664]{1,0:T(8,128)(2,1)S(1)} %concatenate.104.refs_0_), channel_id=1, source_target_pairs={{0,2},{1,3},{2,0},{3,1},{4,6},{5,7},{6,4},{7,5},{8,10},{9,11},{10,... | collective-permute-start | bytes 1916936 | tf_op jit(solution)/shard_map/ppermute | solution.py:489
  60.1 36.9 %collective-permute-start = (bf16[192,1536]{1,0:T(8,128)(2,1)S(1)}, bf16[192,1536]{1,0:T(8,128)(2,1)S(1)}, u32[]{:S(2)}, u32[]{:S(2)}) collective-permute-start(bf16[192,1536]{1,0:T(8,128)(2,1)S(1)} %bitcast.179), channel_id=1, source_target_pairs={{0,4},{4,0},{8,12},{12,8},{1,5},{5,1},{9,13},{13,9},{2,6},{6,2},{1... | collective-permute-start | bytes 1769480 | tf_op jit(solution)/shard_map/ppermute | solution.py:332
  60.1 37.4 %collective-permute-start.2 = (bf16[192,1536]{1,0:T(8,128)(2,1)S(1)}, bf16[192,1536]{1,0:T(8,128)(2,1)S(1)}, u32[]{:S(2)}, u32[]{:S(2)}) collective-permute-start(bf16[192,1536]{1,0:T(8,128)(2,1)S(1)} %collective-permute-done.1), channel_id=1, source_target_pairs={{0,4},{4,0},{8,12},{12,8},{1,5},{5,1},{9,13},{13,9},{2,6},{6,2},{1... | collective-permute-start | bytes 1769480 | tf_op jit(solution)/shard_map/ppermute | solution.py:332
  60.6 37.5 %collective-permute-start.5 = (bf16[192,1664]{1,0:T(8,128)(2,1)}, bf16[192,1664]{1,0:T(8,128)(2,1)}, u32[]{:S(2)}, u32[]{:S(2)}) collective-permute-start(bf16[192,1664]{1,0:T(8,128)(2,1)} %collective-permute-done.4.refs_2_), channel_id=1, source_target_pairs={{0,16},{16,0},{1,17},{17,1},{2,18},{18,2},{3,19},{19,3},{4,20},{20... | collective-permute-start | bytes 1916936 | tf_op jit(solution)/shard_map/ppermute | solution.py:332
  62.2 39.8 %collective-permute-start.7 = (bf16[192,1664]{1,0:T(8,128)(2,1)}, bf16[192,1664]{1,0:T(8,128)(2,1)}, u32[]{:S(2)}, u32[]{:S(2)}) collective-permute-start(bf16[192,1664]{1,0:T(8,128)(2,1)} %collective-permute-done.6.refs_4_), channel_id=1, source_target_pairs={{0,16},{16,0},{1,17},{17,1},{2,18},{18,2},{3,19},{19,3},{4,20},{20... | collective-permute-start | bytes 1916936 | tf_op jit(solution)/shard_map/ppermute | solution.py:332
  92.6 24.0 %collective-permute-start.9 = (bf16[192,1664]{1,0:T(8,128)(2,1)}, bf16[192,1664]{1,0:T(8,128)(2,1)}, u32[]{:S(2)}, u32[]{:S(2)}) collective-permute-start(bf16[192,1664]{1,0:T(8,128)(2,1)} %collective-permute-done.8.refs_6_), channel_id=1, source_target_pairs={{0,16},{16,0},{1,17},{17,1},{2,18},{18,2},{3,19},{19,3},{4,20},{20... | collective-permute-start | bytes 1916936 | tf_op jit(solution)/shard_map/ppermute | solution.py:332
  97.0 24.6 %copy-start.6 = (bf16[192,1536]{1,0:T(8,128)(2,1)}, bf16[192,1536]{1,0:T(8,128)(2,1)S(1)}, u32[]{:S(2)}) copy-start(bf16[192,1536]{1,0:T(8,128)(2,1)S(1)} %collective-permute-done) | copy-start | bytes 1769476
  97.0 41.9 %collective-permute-start.10 = (bf16[192,3072]{1,0:T(8,128)(2,1)}, bf16[192,3072]{1,0:T(8,128)(2,1)S(1)}, u32[]{:S(2)}, u32[]{:S(2)}) collective-permute-start(bf16[192,3072]{1,0:T(8,128)(2,1)} %pad_maximum_fusion.5.refs_0_), channel_id=1, source_target_pairs={{0,16},{16,0},{1,17},{17,1},{2,18},{18,2},{3,19},{19,3},{4,20},{20... | collective-permute-start | bytes 3538952 | tf_op jit(solution)/shard_map/ppermute | solution.py:332
  97.4 24.2 %copy-start.8 = (bf16[192,1536]{1,0:T(8,128)(2,1)}, bf16[192,1536]{1,0:T(8,128)(2,1)S(1)}, u32[]{:S(2)}) copy-start(bf16[192,1536]{1,0:T(8,128)(2,1)S(1)} %collective-permute-done.2) | copy-start | bytes 1769476
  98.1 53.0 %collective-permute-start.11 = (bf16[192,3072]{1,0:T(8,128)(2,1)}, bf16[192,3072]{1,0:T(8,128)(2,1)}, u32[]{:S(2)}, u32[]{:S(2)}) collective-permute-start(bf16[192,3072]{1,0:T(8,128)(2,1)} %pad_maximum_fusion.5.refs_0_), channel_id=1, source_target_pairs={{0,1},{1,2},{2,3},{3,0},{4,5},{5,6},{6,7},{7,4},{8,9},{9,10},{10,1... | collective-permute-start | bytes 3538952 | tf_op jit(solution)/shard_map/ppermute | solution.py:489
  98.2 63.8 %collective-permute-start.12 = (bf16[192,3072]{1,0:T(8,128)(2,1)}, bf16[192,3072]{1,0:T(8,128)(2,1)}, u32[]{:S(2)}, u32[]{:S(2)}) collective-permute-start(bf16[192,3072]{1,0:T(8,128)(2,1)} %pad_maximum_fusion.5.refs_0_), channel_id=1, source_target_pairs={{0,3},{1,0},{2,1},{3,2},{4,7},{5,4},{6,5},{7,6},{8,11},{9,8},{10,9... | collective-permute-start | bytes 3538952 | tf_op jit(solution)/shard_map/ppermute | solution.py:489
  146.7 51.9 %all-to-all-start.1 = ((bf16[4,192,384]{2,1,0:T(8,128)(2,1)}), bf16[4,192,384]{2,1,0:T(8,128)(2,1)}, u32[]{:S(2)}, u32[]{:S(2)}) async-start(bf16[4,192,384]{2,1,0:T(8,128)(2,1)} %dynamic-slice_bitcast_fusion), calls=%async_computation.1 | async-start | bytes 1179648 | tf_op jit(solution)/shard_map/all_to_all | solution.py:385
  150.9 358.8 %reduce-scatter.5.cloned.1.call-start = ((), (), s32[]{:S(2)}) async-start(), calls=%async_computation.8 | async-start | bytes 3538944 | tf_op jit(solution)/shard_map/reduce_scatter | solution.py:553
  161.9 61.5 %collective-permute-start.15 = (bf16[192,3072]{1,0:T(8,128)(2,1)}, bf16[192,3072]{1,0:T(8,128)(2,1)}, u32[]{:S(2)}, u32[]{:S(2)}) collective-permute-start(bf16[192,3072]{1,0:T(8,128)(2,1)} %pad_maximum_fusion.5.refs_0_), channel_id=1, source_target_pairs={{0,2},{1,3},{2,0},{3,1},{4,6},{5,7},{6,4},{7,5},{8,10},{9,11},{10,... | collective-permute-start | bytes 3538952 | tf_op jit(solution)/shard_map/ppermute | solution.py:489
  163.2 37.3 %collective-permute-start.13 = (bf16[192,3072]{1,0:T(8,128)(2,1)}, bf16[192,3072]{1,0:T(8,128)(2,1)}, u32[]{:S(2)}, u32[]{:S(2)}) collective-permute-start(bf16[192,3072]{1,0:T(8,128)(2,1)} %collective-permute-done.11.refs_2_), channel_id=1, source_target_pairs={{0,16},{16,0},{1,17},{17,1},{2,18},{18,2},{3,19},{19,3},{4,20},{20... | collective-permute-start | bytes 3538952 | tf_op jit(solution)/shard_map/ppermute | solution.py:332
  204.8 18.6 %collective-permute-start.14 = (bf16[384,1536]{1,0:T(8,128)(2,1)S(1)}, bf16[384,1536]{1,0:T(8,128)(2,1)S(1)}, u32[]{:S(2)}, u32[]{:S(2)}) collective-permute-start(bf16[384,1536]{1,0:T(8,128)(2,1)S(1)} %convolution_convert_fusion.6), channel_id=1, source_target_pairs={{0,4},{4,0},{8,12},{12,8},{1,5},{5,1},{9,13},{13,9},{2,6},{6,2},{1... | collective-permute-start | bytes 3538952 | tf_op jit(solution)/shard_map/ppermute | solution.py:332
  204.9 29.0 %collective-permute-start.17 = (bf16[192,3072]{1,0:T(8,128)(2,1)}, bf16[192,3072]{1,0:T(8,128)(2,1)S(1)}, u32[]{:S(2)}, u32[]{:S(2)}) collective-permute-start(bf16[192,3072]{1,0:T(8,128)(2,1)} %collective-permute-done.12.refs_4_), channel_id=1, source_target_pairs={{0,16},{16,0},{1,17},{17,1},{2,18},{18,2},{3,19},{19,3},{4,20},{20... | collective-permute-start | bytes 3538952 | tf_op jit(solution)/shard_map/ppermute | solution.py:332
  224.4 15.0 %collective-permute-start.16 = (bf16[192,1536]{1,0:T(8,128)(2,1)S(1)}, bf16[192,1536]{1,0:T(8,128)(2,1)S(1)}, u32[]{:S(2)}, u32[]{:S(2)}) collective-permute-start(bf16[192,1536]{1,0:T(8,128)(2,1)S(1)} %slice.505), channel_id=1, source_target_pairs={{0,8},{4,12},{8,0},{12,4},{1,9},{5,13},{9,1},{13,5},{2,10},{6,14},... | collective-permute-start | bytes 1769480 | tf_op jit(solution)/shard_map/ppermute | solution.py:332
  226.6 32.2 %collective-permute-start.21 = (bf16[192,3072]{1,0:T(8,128)(2,1)}, bf16[192,3072]{1,0:T(8,128)(2,1)S(1)}, u32[]{:S(2)}, u32[]{:S(2)}) collective-permute-start(bf16[192,3072]{1,0:T(8,128)(2,1)} %collective-permute-done.15.refs_6_), channel_id=1, source_target_pairs={{0,16},{16,0},{1,17},{17,1},{2,18},{18,2},{3,19},{19,3},{4,20},{20... | collective-permute-start | bytes 3538952 | tf_op jit(solution)/shard_map/ppermute | solution.py:332
  241.0 27.4 %copy-start.22 = (bf16[192,1536]{1,0:T(8,128)(2,1)}, bf16[192,1536]{1,0:T(8,128)(2,1)S(1)}, u32[]{:S(2)}) copy-start(bf16[192,1536]{1,0:T(8,128)(2,1)S(1)} %multiply_convert_fusion.4) | copy-start | bytes 1769476
  241.0 16.3 %collective-permute-start.19 = (bf16[192,1536]{1,0:T(8,128)(2,1)S(1)}, bf16[192,1536]{1,0:T(8,128)(2,1)S(1)}, u32[]{:S(2)}, u32[]{:S(2)}) collective-permute-start(bf16[192,1536]{1,0:T(8,128)(2,1)S(1)} %multiply_convert_fusion.4), channel_id=1, source_target_pairs={{0,8},{4,12},{8,0},{12,4},{1,9},{5,13},{9,1},{13,5},{2,10},{6,14},... | collective-permute-start | bytes 1769480 | tf_op jit(solution)/shard_map/ppermute | solution.py:332
  242.5 25.3 %collective-permute-start.18 = (bf16[192,1536]{1,0:T(8,128)(2,1)S(1)}, bf16[192,1536]{1,0:T(8,128)(2,1)S(1)}, u32[]{:S(2)}, u32[]{:S(2)}) collective-permute-start(bf16[192,1536]{1,0:T(8,128)(2,1)S(1)} %multiply_convert_fusion.4), channel_id=1, source_target_pairs={{0,4},{4,0},{8,12},{12,8},{1,5},{5,1},{9,13},{13,9},{2,6},{6,2},{1... | collective-permute-start | bytes 1769480 | tf_op jit(solution)/shard_map/ppermute | solution.py:332
  242.5 25.3 %collective-permute-start.24 = (bf16[192,1536]{1,0:T(8,128)(2,1)S(1)}, bf16[192,1536]{1,0:T(8,128)(2,1)S(1)}, u32[]{:S(2)}, u32[]{:S(2)}) collective-permute-start(bf16[192,1536]{1,0:T(8,128)(2,1)S(1)} %bitcast.184), channel_id=1, source_target_pairs={{0,8},{4,12},{8,0},{12,4},{1,9},{5,13},{9,1},{13,5},{2,10},{6,14},... | collective-permute-start | bytes 1769480 | tf_op jit(solution)/shard_map/ppermute | solution.py:332
  257.3 11.1 %collective-permute-start.20 = (bf16[192,1536]{1,0:T(8,128)(2,1)S(1)}, bf16[192,1536]{1,0:T(8,128)(2,1)S(1)}, u32[]{:S(2)}, u32[]{:S(2)}) collective-permute-start(bf16[192,1536]{1,0:T(8,128)(2,1)S(1)} %collective-permute-done.19), channel_id=1, source_target_pairs={{0,4},{4,0},{8,12},{12,8},{1,5},{5,1},{9,13},{13,9},{2,6},{6,2},{1... | collective-permute-start | bytes 1769480 | tf_op jit(solution)/shard_map/ppermute | solution.py:332
  267.7 8.0 %collective-permute-start.22 = (bf16[192,1536]{1,0:T(8,128)(2,1)S(1)}, bf16[192,1536]{1,0:T(8,128)(2,1)S(1)}, u32[]{:S(2)}, u32[]{:S(2)}) collective-permute-start(bf16[192,1536]{1,0:T(8,128)(2,1)S(1)} %bitcast.186), channel_id=1, source_target_pairs={{0,4},{4,0},{8,12},{12,8},{1,5},{5,1},{9,13},{13,9},{2,6},{6,2},{1... | collective-permute-start | bytes 1769480 | tf_op jit(solution)/shard_map/ppermute | solution.py:332
  267.9 8.0 %collective-permute-start.25 = (bf16[192,1536]{1,0:T(8,128)(2,1)S(1)}, bf16[192,1536]{1,0:T(8,128)(2,1)S(1)}, u32[]{:S(2)}, u32[]{:S(2)}) collective-permute-start(bf16[192,1536]{1,0:T(8,128)(2,1)S(1)} %collective-permute-done.24), channel_id=1, source_target_pairs={{0,4},{4,0},{8,12},{12,8},{1,5},{5,1},{9,13},{13,9},{2,6},{6,2},{1... | collective-permute-start | bytes 1769480 | tf_op jit(solution)/shard_map/ppermute | solution.py:332
  289.8 7.7 %collective-permute-start.26 = (bf16[384,1536]{1,0:T(8,128)(2,1)}, bf16[384,1536]{1,0:T(8,128)(2,1)}, u32[]{:S(2)}, u32[]{:S(2)}) collective-permute-start(bf16[384,1536]{1,0:T(8,128)(2,1)} %convolution_convert_fusion.4), channel_id=1, source_target_pairs={{0,4},{4,0},{8,12},{12,8},{1,5},{5,1},{9,13},{13,9},{2,6},{6,2},{1... | collective-permute-start | bytes 3538952 | tf_op jit(solution)/shard_map/ppermute | solution.py:332
  305.9 15.9 %collective-permute-start.27 = (bf16[192,1536]{1,0:T(8,128)(2,1)}, bf16[192,1536]{1,0:T(8,128)(2,1)}, u32[]{:S(2)}, u32[]{:S(2)}) collective-permute-start(bf16[192,1536]{1,0:T(8,128)(2,1)} %slice.504), channel_id=1, source_target_pairs={{0,8},{4,12},{8,0},{12,4},{1,9},{5,13},{9,1},{13,5},{2,10},{6,14},... | collective-permute-start | bytes 1769480 | tf_op jit(solution)/shard_map/ppermute | solution.py:332
  308.5 43.8 %collective-permute-start.31 = (bf16[768,1024]{1,0:T(8,128)(2,1)}, bf16[768,1024]{1,0:T(8,128)(2,1)}, u32[]{:S(2)}, u32[]{:S(2)}) collective-permute-start(bf16[768,1024]{1,0:T(8,128)(2,1)} %convolution_convert_fusion.8), channel_id=1, source_target_pairs={{0,16},{16,0},{1,17},{17,1},{2,18},{18,2},{3,19},{19,3},{4,20},{20... | collective-permute-start | bytes 4718600 | tf_op jit(solution)/shard_map/ppermute | solution.py:332
  326.6 15.1 %collective-permute-start.29 = (bf16[192,1536]{1,0:T(8,128)(2,1)}, bf16[192,1536]{1,0:T(8,128)(2,1)}, u32[]{:S(2)}, u32[]{:S(2)}) collective-permute-start(bf16[192,1536]{1,0:T(8,128)(2,1)} %get-tuple-element.116), channel_id=1, source_target_pairs={{0,8},{4,12},{8,0},{12,4},{1,9},{5,13},{9,1},{13,5},{2,10},{6,14},... | collective-permute-start | bytes 1769480 | tf_op jit(solution)/shard_map/ppermute | solution.py:332
  330.6 21.8 %collective-permute-start.23 = (bf16[384,1536]{1,0:T(8,128)(2,1)}, bf16[384,1536]{1,0:T(8,128)(2,1)}, u32[]{:S(2)}, u32[]{:S(2)}) collective-permute-start(bf16[384,1536]{1,0:T(8,128)(2,1)} %convolution_convert_fusion.5), channel_id=1, source_target_pairs={{0,4},{4,0},{8,12},{12,8},{1,5},{5,1},{9,13},{13,9},{2,6},{6,2},{1... | collective-permute-start | bytes 3538952 | tf_op jit(solution)/shard_map/ppermute | solution.py:332
  333.2 69.2 %collective-permute-start.33 = (bf16[768,1024]{1,0:T(8,128)(2,1)}, bf16[768,1024]{1,0:T(8,128)(2,1)}, u32[]{:S(2)}, u32[]{:S(2)}) collective-permute-start(bf16[768,1024]{1,0:T(8,128)(2,1)} %convolution_convert_fusion.7), channel_id=1, source_target_pairs={{0,16},{16,0},{1,17},{17,1},{2,18},{18,2},{3,19},{19,3},{4,20},{20... | collective-permute-start | bytes 4718600 | tf_op jit(solution)/shard_map/ppermute | solution.py:332
  334.7 15.6 %collective-permute-start.28 = (bf16[192,1536]{1,0:T(8,128)(2,1)}, bf16[192,1536]{1,0:T(8,128)(2,1)}, u32[]{:S(2)}, u32[]{:S(2)}) collective-permute-start(bf16[192,1536]{1,0:T(8,128)(2,1)} %get-tuple-element.116), channel_id=1, source_target_pairs={{0,4},{4,0},{8,12},{12,8},{1,5},{5,1},{9,13},{13,9},{2,6},{6,2},{1... | collective-permute-start | bytes 1769480 | tf_op jit(solution)/shard_map/ppermute | solution.py:332
  341.7 8.6 %collective-permute-start.30 = (bf16[192,1536]{1,0:T(8,128)(2,1)}, bf16[192,1536]{1,0:T(8,128)(2,1)}, u32[]{:S(2)}, u32[]{:S(2)}) collective-permute-start(bf16[192,1536]{1,0:T(8,128)(2,1)} %collective-permute-done.29), channel_id=1, source_target_pairs={{0,4},{4,0},{8,12},{12,8},{1,5},{5,1},{9,13},{13,9},{2,6},{6,2},{1... | collective-permute-start | bytes 1769480 | tf_op jit(solution)/shard_map/ppermute | solution.py:332
  356.2 46.2 %collective-permute-start.32 = (bf16[192,1536]{1,0:T(8,128)(2,1)S(1)}, bf16[192,1536]{1,0:T(8,128)(2,1)S(1)}, u32[]{:S(2)}, u32[]{:S(2)}) collective-permute-start(bf16[192,1536]{1,0:T(8,128)(2,1)S(1)} %slice.503), channel_id=1, source_target_pairs={{0,8},{4,12},{8,0},{12,4},{1,9},{5,13},{9,1},{13,5},{2,10},{6,14},... | collective-permute-start | bytes 1769480 | tf_op jit(solution)/shard_map/ppermute | solution.py:332
  360.2 35.6 %copy-start.19 = (f32[768,1024]{1,0:T(8,128)S(1)}, f32[768,1024]{1,0:T(8,128)}, u32[]{:S(2)}) copy-start(f32[768,1024]{1,0:T(8,128)} %fusion.34) | copy-start | bytes 9437188
  399.1 40.0 %collective-permute-start.47 = (bf16[384,1024]{1,0:T(8,128)(2,1)}, bf16[384,1024]{1,0:T(8,128)(2,1)}, u32[]{:S(2)}, u32[]{:S(2)}) collective-permute-start(bf16[384,1024]{1,0:T(8,128)(2,1)} %pad_maximum_fusion.8), channel_id=1, source_target_pairs={{0,1},{1,0},{2,3},{3,2},{4,5},{5,4},{6,7},{7,6},{8,9},{9,8},{10,11... | collective-permute-start | bytes 2359304 | tf_op jit(solution)/shard_map/ppermute | solution.py:332
  409.1 19.6 %collective-permute-start.34 = (bf16[384,1536]{1,0:T(8,128)(2,1)}, bf16[384,1536]{1,0:T(8,128)(2,1)}, u32[]{:S(2)}, u32[]{:S(2)}) collective-permute-start(bf16[384,1536]{1,0:T(8,128)(2,1)} %fusion.4), channel_id=1, source_target_pairs={{0,4},{4,0},{8,12},{12,8},{1,5},{5,1},{9,13},{13,9},{2,6},{6,2},{1... | collective-permute-start | bytes 3538952 | tf_op jit(solution)/shard_map/ppermute | solution.py:332
  410.4 50.2 %all-to-all-start.2 = ((bf16[192,4,384]{2,0,1:T(8,128)(2,1)}), bf16[192,4,384]{2,0,1:T(8,128)(2,1)}, u32[]{:S(2)}, u32[]{:S(2)}) async-start(bf16[192,4,384]{2,0,1:T(8,128)(2,1)} %bitcast.164), calls=%async_computation.2 | async-start | bytes 1179648 | tf_op jit(solution)/shard_map/all_to_all | solution.py:471
  414.6 131.2 %reduce-scatter.3.cloned.1.call-start = ((), (), s32[]{:S(2)}) async-start(), calls=%async_computation.7 | async-start | bytes 1327104 | tf_op jit(solution)/shard_map/reduce_scatter | solution.py:553
  420.2 56.8 %collective-permute-start.39 = (bf16[768,1536]{1,0:T(8,128)(2,1)}, bf16[768,1536]{1,0:T(8,128)(2,1)}, u32[]{:S(2)}, u32[]{:S(2)}) collective-permute-start(bf16[768,1536]{1,0:T(8,128)(2,1)} %convolution_convert_fusion.1), channel_id=1, source_target_pairs={{0,16},{16,0},{1,17},{17,1},{2,18},{18,2},{3,19},{19,3},{4,20},{20... | collective-permute-start | bytes 7077896 | tf_op jit(solution)/shard_map/ppermute | solution.py:332
  426.7 80.8 %collective-permute-start.45 = (bf16[384,1024]{1,0:T(8,128)(2,1)}, bf16[384,1024]{1,0:T(8,128)(2,1)}, u32[]{:S(2)}, u32[]{:S(2)}) collective-permute-start(bf16[384,1024]{1,0:T(8,128)(2,1)} %pad_maximum_fusion.7), channel_id=1, source_target_pairs={{0,1},{1,0},{2,3},{3,2},{4,5},{5,4},{6,7},{7,6},{8,9},{9,8},{10,11... | collective-permute-start | bytes 2359304 | tf_op jit(solution)/shard_map/ppermute | solution.py:332
  434.5 15.3 %collective-permute-start.35 = (bf16[192,1536]{1,0:T(8,128)(2,1)}, bf16[192,1536]{1,0:T(8,128)(2,1)}, u32[]{:S(2)}, u32[]{:S(2)}) collective-permute-start(bf16[192,1536]{1,0:T(8,128)(2,1)} %slice.502), channel_id=1, source_target_pairs={{0,8},{4,12},{8,0},{12,4},{1,9},{5,13},{9,1},{13,5},{2,10},{6,14},... | collective-permute-start | bytes 1769480 | tf_op jit(solution)/shard_map/ppermute | solution.py:332
  435.6 22.8 %copy-start.14 = (f32[192,1536]{1,0:T(8,128)S(1)}, f32[192,1536]{1,0:T(8,128)}, u32[]{:S(2)}) copy-start(f32[192,1536]{1,0:T(8,128)} %get-tuple-element.211) | copy-start | bytes 3538948
  460.7 15.8 %collective-permute-start.37 = (bf16[4,1,192,384]{3,2,1,0:T(8,128)(2,1)}, bf16[4,1,192,384]{3,2,1,0:T(8,128)(2,1)}, u32[]{:S(2)}, u32[]{:S(2)}) collective-permute-start(bf16[4,1,192,384]{3,2,1,0:T(8,128)(2,1)} %bitcast.31), channel_id=1, source_target_pairs={{0,8},{4,12},{8,0},{12,4},{1,9},{5,13},{9,1},{13,5},{2,10},{6,14},... | collective-permute-start | bytes 1769480 | tf_op jit(solution)/shard_map/ppermute | solution.py:332
  463.3 57.3 %collective-permute-start.48 = (bf16[192,1024]{1,0:T(8,128)(2,1)}, bf16[192,1024]{1,0:T(8,128)(2,1)S(1)}, u32[]{:S(2)}, u32[]{:S(2)}) collective-permute-start(bf16[192,1024]{1,0:T(8,128)(2,1)} %fusion.50), channel_id=1, source_target_pairs={{0,2},{1,3},{2,0},{3,1},{4,6},{5,7},{6,4},{7,5},{8,10},{9,11},{10,... | collective-permute-start | bytes 1179656 | tf_op jit(solution)/shard_map/ppermute | solution.py:332
  469.8 15.9 %collective-permute-start.36 = (bf16[4,1,192,384]{3,2,1,0:T(8,128)(2,1)}, bf16[4,1,192,384]{3,2,1,0:T(8,128)(2,1)}, u32[]{:S(2)}, u32[]{:S(2)}) collective-permute-start(bf16[4,1,192,384]{3,2,1,0:T(8,128)(2,1)} %bitcast.31), channel_id=1, source_target_pairs={{0,4},{4,0},{8,12},{12,8},{1,5},{5,1},{9,13},{13,9},{2,6},{6,2},{1... | collective-permute-start | bytes 1769480 | tf_op jit(solution)/shard_map/ppermute | solution.py:332
  470.8 34.1 %all-to-all-start.3 = ((bf16[208,4,384]{2,0,1:T(8,128)(2,1)}), bf16[208,4,384]{2,0,1:T(8,128)(2,1)S(1)}, u32[]{:S(2)}, u32[]{:S(2)}) async-start(bf16[208,4,384]{2,0,1:T(8,128)(2,1)} %bitcast.195), calls=%async_computation.3 | async-start | bytes 1277952 | tf_op jit(solution)/shard_map/all_to_all | solution.py:471
  476.5 35.1 %collective-permute-start.38 = (bf16[4,1,192,384]{3,2,1,0:T(8,128)(2,1)}, bf16[4,1,192,384]{3,2,1,0:T(8,128)(2,1)}, u32[]{:S(2)}, u32[]{:S(2)}) collective-permute-start(bf16[4,1,192,384]{3,2,1,0:T(8,128)(2,1)} %collective-permute-done.37), channel_id=1, source_target_pairs={{0,4},{4,0},{8,12},{12,8},{1,5},{5,1},{9,13},{13,9},{2,6},{6,2},{1... | collective-permute-start | bytes 1769480 | tf_op jit(solution)/shard_map/ppermute | solution.py:332
  484.0 55.2 %collective-permute-start.40 = (bf16[384,1536]{1,0:T(8,128)(2,1)}, bf16[384,1536]{1,0:T(8,128)(2,1)}, u32[]{:S(2)}, u32[]{:S(2)}) collective-permute-start(bf16[384,1536]{1,0:T(8,128)(2,1)} %pad_maximum_fusion.6), channel_id=1, source_target_pairs={{0,1},{1,0},{2,3},{3,2},{4,5},{5,4},{6,7},{7,6},{8,9},{9,8},{10,11... | collective-permute-start | bytes 3538952 | tf_op jit(solution)/shard_map/ppermute | solution.py:332
  504.9 15.7 %collective-permute-start.42 = (bf16[4,1,208,384]{3,2,1,0:T(8,128)(2,1)S(1)}, bf16[4,1,208,384]{3,2,1,0:T(8,128)(2,1)}, u32[]{:S(2)}, u32[]{:S(2)}) collective-permute-start(bf16[4,1,208,384]{3,2,1,0:T(8,128)(2,1)S(1)} %bitcast.191), channel_id=1, source_target_pairs={{0,8},{4,12},{8,0},{12,4},{1,9},{5,13},{9,1},{13,5},{2,10},{6,14},... | collective-permute-start | bytes 1916936 | tf_op jit(solution)/shard_map/ppermute | solution.py:332
  507.5 13.9 %collective-permute-start.41 = (bf16[4,1,208,384]{3,2,1,0:T(8,128)(2,1)S(1)}, bf16[4,1,208,384]{3,2,1,0:T(8,128)(2,1)S(1)}, u32[]{:S(2)}, u32[]{:S(2)}) collective-permute-start(bf16[4,1,208,384]{3,2,1,0:T(8,128)(2,1)S(1)} %bitcast.193), channel_id=1, source_target_pairs={{0,4},{4,0},{8,12},{12,8},{1,5},{5,1},{9,13},{13,9},{2,6},{6,2},{1... | collective-permute-start | bytes 1916936 | tf_op jit(solution)/shard_map/ppermute | solution.py:332
  511.6 34.2 %collective-permute-start.49 = (bf16[192,1024]{1,0:T(8,128)(2,1)}, bf16[192,1024]{1,0:T(8,128)(2,1)S(1)}, u32[]{:S(2)}, u32[]{:S(2)}) collective-permute-start(bf16[192,1024]{1,0:T(8,128)(2,1)} %fusion.48), channel_id=1, source_target_pairs={{0,2},{1,3},{2,0},{3,1},{4,6},{5,7},{6,4},{7,5},{8,10},{9,11},{10,... | collective-permute-start | bytes 1179656 | tf_op jit(solution)/shard_map/ppermute | solution.py:332
  520.6 29.1 %collective-permute-start.43 = (bf16[4,1,208,384]{3,2,1,0:T(8,128)(2,1)}, bf16[4,1,208,384]{3,2,1,0:T(8,128)(2,1)S(1)}, u32[]{:S(2)}, u32[]{:S(2)}) collective-permute-start(bf16[4,1,208,384]{3,2,1,0:T(8,128)(2,1)} %collective-permute-done.42), channel_id=1, source_target_pairs={{0,4},{4,0},{8,12},{12,8},{1,5},{5,1},{9,13},{13,9},{2,6},{6,2},{1... | collective-permute-start | bytes 1916936 | tf_op jit(solution)/shard_map/ppermute | solution.py:332
  544.5 29.2 %collective-permute-start.46 = (bf16[192,1536]{1,0:T(8,128)(2,1)}, bf16[192,1536]{1,0:T(8,128)(2,1)}, u32[]{:S(2)}, u32[]{:S(2)}) collective-permute-start(bf16[192,1536]{1,0:T(8,128)(2,1)} %fusion.26), channel_id=1, source_target_pairs={{0,2},{1,3},{2,0},{3,1},{4,6},{5,7},{6,4},{7,5},{8,10},{9,11},{10,... | collective-permute-start | bytes 1769480 | tf_op jit(solution)/shard_map/ppermute | solution.py:332
  554.8 4.6 collective-permute-start.44
  (70 other events, 465.7 us)
Sparse Core Ops, SparseCore 0:
  60.7 79.7 all-gather.1
  334.8 95.1 reduce-scatter.4
  469.9 72.6 reduce-scatter.2

commit v4 on v3

--- a/solution.py
+++ b/solution.py
@@ -189,13 +189,13 @@
         here = pl.ds(i * width, width)
         upto = (i + 1) * width
         prob = pr_ref[0, here, :upto]
-        dprob = mm(split(do_ref[here, :]), v_ref[:upto, :], 1, 1)
+        dprob = mm(do_ref[here, :].astype(BF), v_ref[:upto, :], 1, 1)
         delta = jnp.sum(prob * dprob, axis=1, keepdims=True)
         ds_ref[here, :upto] = prob * (dprob - delta) * width ** (-0.5)
     for j in range(blocks):
         here = pl.ds(j * width, width)
         below = pl.ds(j * width, length - j * width)
-        dv_ref[here, :] = mm(split(pr_ref[0, below, here]), split(do_ref[below, :]), 0, 0)
+        dv_ref[here, :] = mm(pr_ref[0, below, here].astype(BF), do_ref[below, :].astype(BF), 0, 0)
 
     zero = jnp.zeros((width, width), F32)
     dqt_ref[0:width, :] = zero
@@ -207,14 +207,14 @@
     for j in range(blocks - 1):
         here = pl.ds(j * width, width)
         below = pl.ds((j + 1) * width, length - (j + 1) * width)
-        dsj = split(ds_ref[below, here])
-        moved = split(qm_ref[0, j, below, :])
+        dsj = ds_ref[below, here].astype(BF)
+        moved = qm_ref[0, j, below, :].astype(BF)
         dkt_ref[here, :] = mm(dsj, moved, 0, 0)
-        fresh = mm(dsj, split(kt_ref[0, here, :]), 1, 0)
+        fresh = mm(dsj, kt_ref[0, here, :].astype(BF), 1, 0)
         if j:
-            old = split(grad)
+            old = grad.astype(BF)
             dp_ref[here, :] = mm(moved, old, 0, 0)
-            fresh = fresh + mm(old, split(p_ref[0, here, :]), 1, 1)
+            fresh = fresh + mm(old, p_ref[0, here, :].astype(BF), 1, 1)
         dqt_ref[pl.ds((j + 1) * width, width), :] = fresh[:width]
         grad = fresh[width:]
 
@@ -384,12 +384,12 @@
             mine = lax.dynamic_index_in_dim(array.reshape(wid, hid, quarter, slice_width), me_hid, 1, keepdims=False)
             return lax.all_to_all(mine.reshape(wid * quarter, slice_width), "wid", split_axis=0, concat_axis=1, tiled=True)
 
-        def gather_hid(own):
+        def gather_hid(own, before=()):
             pieces = {0: own}
             bit = hid // 2
             while bit:
                 for k in list(pieces):
-                    pieces[k | bit] = swap(pieces[k], bit)
+                    pieces[k | bit] = swap(after(pieces[k], *before) if before and k else pieces[k], bit)
                 bit //= 2
             return [pieces[k] for k in range(hid)]
 
@@ -528,7 +528,7 @@
         late += [over_dp(a) for a in late_along[1:3]]
         token_grad = to_tokens(after(cotangent, projected))
         attended, *saved = attend_fwd(order, after(projected, *late_along[1:3]), logits, segments, quarter)
-        attended = after(attended, late[1][-1], token_grad)
+        attended = after(attended, late[1][-1])
 
         branch_flow = Flow(summing_hid(lambda ks: dot(rows_of(attended, ks), weight_out, 1, 1)))
         branch_flow.step()
@@ -570,7 +570,7 @@
         up_flow.step()
         grad_gain_two, grad_middle = norm_back(middle, scale_two, gain_two, grad_mixed)
         grad_middle = grad_middle + token_grad.astype(F32)
-        quarters = gather_hid(grad_middle.astype(BF))
+        quarters = gather_hid(grad_middle.astype(BF), kept)
         grad_branch = after(jnp.concatenate(quarters, axis=0), gate_flow.got, *kept)
         grad_attended = dot(grad_branch, weight_out, 1, 0)
         gate_flow.step(grad_branch)

time: 591 us -> 579 us (0.980)
  waiting for transfers between devices: 222 us -> 210 us
    ppermute x43, waiting for transfers between devices: 115 us -> 98.3 us  [send(): self.done.append(lax.ppermute(value, axis, pairs))]
    unnamed x165 -> x159, local copies, waits for them, and re-layouts: 19.5 us -> 18.2 us
  transfers between devices with their start and end apart: 57 -> 57, of which waited for: 20 -> 19; matrix products, arithmetic and copies ran while one was open for 29% -> 32% of each run, Pallas kernels for 13% -> 13%
where the time goes in v4:
time: 579 us; the launch traced here: 574 us
  waiting for transfers between devices  210 us (36%)
  matrix products  82.4 us (14%)
  Pallas kernels  73.9 us (13%)
  other arithmetic  66.3 us (11%)
  starting transfers between devices  66.2 us (11%)
  local copies, waits for them, and re-layouts  59.8 us (10%)
  between operations  15.4 us (3%)
    ppermute x43, waiting for transfers between devices, send(): self.done.append(lax.ppermute(value, axis, pairs))  98.3 us
    dot_general x24, matrix products, dot(): lax.dot_general(a, b, (((ca,), (cb,)), ((), ())), preferred_element_type=...  82.4 us
    ppermute x6, waiting for transfers between devices, hop(): lax.ppermute(after(own, *first) if first else own, 'wid', [(i, (i + k) %...  65.4 us
    ppermute x43, starting transfers between devices, send(): self.done.append(lax.ppermute(value, axis, pairs))  35.2 us
    pallas_call x1, Pallas kernels, attend_bwd(): pl.pallas_call(functools.partial(bwd_kernel, quarter // STEP), grid=(head...  31.6 us
    all_to_all x2, waiting for transfers between devices, to_tokens(): lax.all_to_all(mine.reshape(wid * quarter, slice_width), 'wid', split_axi...  30.4 us
    pallas_call x1, Pallas kernels, attend_fwd(): pl.pallas_call(functools.partial(fwd_kernel, quarter // STEP), grid=(head...  29.2 us
    unnamed x159, local copies, waits for them, and re-layouts  18.2 us
  transfers between devices with their start and end apart: 57, of which 19 were waited for; matrix products, arithmetic and copies ran while one was open for 32% of the time, Pallas kernels for 13%

profile of v4, /device:TPU:0, one launch (start us, length us, event | category | flops | bytes accessed | tf_op | source)
XLA Modules:
  0.0 573.6 jit_solution(8990679766732481592)
XLA Ops:
  9.7 6.3 %all-to-all-start = ((bf16[4,192,384]{2,1,0:T(8,128)(2,1)}), bf16[4,192,384]{2,1,0:T(8,128)(2,1)S(1)}, u32[]{:S(2)}, u32[]{:S(2)}) async-start(bf16[4,192,384]{2,1,0:T(8,128)(2,1)} %dynamic-slice_bitcast_fusion.1), calls=%async_computation | async-start | bytes 1179648 | tf_op jit(solution)/shard_map/all_to_all | solution.py:385
  18.1 2.1 collective-permute-start.4
  23.5 23.1 %all-to-all-done = bf16[4,192,384]{2,1,0:T(8,128)(2,1)S(1)} async-done(((bf16[4,192,384]{2,1,0:T(8,128)(2,1)}), bf16[4,192,384]{2,1,0:T(8,128)(2,1)S(1)}, u32[]{:S(2)}, u32[]{:S(2)}) %all-to-all-start) | async-done | bytes 589856 | tf_op jit(solution)/shard_map/all_to_all | solution.py:385
  48.3 7.1 %collective-permute-done.6.refs_4_ = bf16[192,1664]{1,0:T(8,128)(2,1)} collective-permute-done((bf16[192,1664]{1,0:T(8,128)(2,1)S(1)}, bf16[192,1664]{1,0:T(8,128)(2,1)}, u32[]{:S(2)}, u32[]{:S(2)}) %collective-permute-start.6) | collective-permute-done | bytes 639008 | tf_op jit(solution)/shard_map/ppermute | solution.py:489
  55.4 4.5 collective-permute-done.1
  62.7 29.8 %collective-permute-done.8.refs_6_ = bf16[192,1664]{1,0:T(8,128)(2,1)} collective-permute-done((bf16[192,1664]{1,0:T(8,128)(2,1)S(1)}, bf16[192,1664]{1,0:T(8,128)(2,1)}, u32[]{:S(2)}, u32[]{:S(2)}) %collective-permute-start.8) | collective-permute-done | bytes 639008 | tf_op jit(solution)/shard_map/ppermute | solution.py:489
  94.1 2.2 pad_maximum_fusion.5.refs_0_
  98.1 4.0 collective-permute-start.12
  102.1 14.4 %collective-permute-done.9.refs_7_ = bf16[192,1664]{1,0:T(8,128)(2,1)} collective-permute-done((bf16[192,1664]{1,0:T(8,128)(2,1)}, bf16[192,1664]{1,0:T(8,128)(2,1)}, u32[]{:S(2)}, u32[]{:S(2)}) %collective-permute-start.9) | collective-permute-done | bytes 639008 | tf_op jit(solution)/shard_map/ppermute | solution.py:332
  116.5 5.1 assemble.2
  126.0 12.9 %collective-permute-done.10.refs_1_ = bf16[192,3072]{1,0:T(8,128)(2,1)S(1)} collective-permute-done((bf16[192,3072]{1,0:T(8,128)(2,1)}, bf16[192,3072]{1,0:T(8,128)(2,1)S(1)}, u32[]{:S(2)}, u32[]{:S(2)}) %collective-permute-start.10) | collective-permute-done | bytes 1179680 | tf_op jit(solution)/shard_map/ppermute | solution.py:332
  139.9 5.0 convolution_convert_fusion.2.proj_ref
  144.9 14.2 %collective-permute-done.12.refs_4_ = bf16[192,3072]{1,0:T(8,128)(2,1)} collective-permute-done((bf16[192,3072]{1,0:T(8,128)(2,1)}, bf16[192,3072]{1,0:T(8,128)(2,1)}, u32[]{:S(2)}, u32[]{:S(2)}) %collective-permute-start.12) | collective-permute-done | bytes 1179680 | tf_op jit(solution)/shard_map/ppermute | solution.py:489
  159.0 2.1 collective-permute-start.15
  162.7 29.2 %attend_fwd.1 = (bf16[768,384]{1,0:T(8,128)(2,1)}, f32[3,768,768]{2,1,0:T(8,128)}, f32[3,6,768,128]{3,2,1,0:T(8,128)}, f32[3,768,128]{2,1,0:T(8,128)}, f32[3,768...) custom-call(s32[1]{0:T(128)} %bitcast.3.order_ref, ...), custom_call_target="tpu_custom_call" | custom-call | flops 32999999488 | bytes 30000000 | tf_op jit(solution)/shard_map/attend_fwd/pallas_call | solution.py:157
  194.9 2.3 convolution_convert_fusion.6
  197.9 14.3 %collective-permute-done.15.refs_6_ = bf16[192,3072]{1,0:T(8,128)(2,1)} collective-permute-done((bf16[192,3072]{1,0:T(8,128)(2,1)}, bf16[192,3072]{1,0:T(8,128)(2,1)}, u32[]{:S(2)}, u32[]{:S(2)}) %collective-permute-start.15) | collective-permute-done | bytes 1179680 | tf_op jit(solution)/shard_map/ppermute | solution.py:489
  216.9 2.8 maximum_convert_fusion
  221.6 4.1 all-to-all-start.1
  228.8 2.1 multiply_reduce_fusion.5
  233.9 7.3 %all-to-all-done.1 = bf16[4,192,384]{2,1,0:T(8,128)(2,1)} async-done(((bf16[4,192,384]{2,1,0:T(8,128)(2,1)}), bf16[4,192,384]{2,1,0:T(8,128)(2,1)}, u32[]{:S(2)}, u32[]{:S(2)}) %all-to-all-start.1) | async-done | bytes 589856 | tf_op jit(solution)/shard_map/all_to_all | solution.py:385
  243.1 2.6 collective-permute-done.19
  245.6 7.8 %collective-permute-done.21.refs_7_ = bf16[192,3072]{1,0:T(8,128)(2,1)} collective-permute-done((bf16[192,3072]{1,0:T(8,128)(2,1)}, bf16[192,3072]{1,0:T(8,128)(2,1)}, u32[]{:S(2)}, u32[]{:S(2)}) %collective-permute-start.21) | collective-permute-done | bytes 1179680 | tf_op jit(solution)/shard_map/ppermute | solution.py:332
  253.5 8.0 %assemble.3 = (bf16[1536,2048]{1,0:T(8,128)(2,1)}, bf16[1536,1024]{1,0:T(8,128)(2,1)}) custom-call(s32[8]{0:T(128)} %stack.44.place_ref, bf16[192,3072]{1,0:T(8,128)(2,1)} %pad_maximum_fusion.5.refs_0_, bf16[192,3072]{1,0:T(8,128)(2,1)} %copy-done.39, bf16[192,3072]{1,0:T(8,128)(2,1)} %copy-done.40, bf16[192,3072]{1,0:T(8,128)(2,1)} %copy-done.41, ...), custom_call_target="tpu_custom_call" | custom-call | bytes 18874368 | tf_op jit(solution)/shard_map/assemble/pallas_call | solution.py:308
  262.1 7.6 %fusion.105 = f32[768,2048]{1,0:T(8,128)S(1)} fusion(bf16[1536,2048]{1,0:T(8,128)(2,1)} %get-tuple-element.107, bf16[192,1536]{1,0:T(8,128)(2,1)S(1)} %collective-permute-done.20, bf16[192,1536]{1,0:T(8,128)(2,1)} %collective-permute-done.19, bf16[192,1536]{1,0:T(8,128)(2,1)S(1)} %collective-permute-done.18, bf16[192,1536]{1,0:T(8,128)(2,1)} %multiply_convert_fusion.4), kind=kOutput, calls=%fused_computation.255 | convolution fusion | flops 4841275392 | bytes 14942208 | tf_op jit(solution)/shard_map/dot_general | solution.py:378
  270.0 2.5 copy-done.66
  272.6 5.0 multiply_convert_fusion.2
  279.7 3.7 convolution_convert_fusion.4
  283.6 2.6 fusion.109
  286.2 2.5 convolution_convert_fusion.5
  290.6 4.8 convolution_add_fusion.2
  296.9 2.6 convolution_convert_fusion.8
  301.1 4.2 convolution_convert_fusion
  305.3 6.8 %collective-permute-done.27 = bf16[192,1536]{1,0:T(8,128)(2,1)} collective-permute-done((bf16[192,1536]{1,0:T(8,128)(2,1)}, bf16[192,1536]{1,0:T(8,128)(2,1)}, u32[]{:S(2)}, u32[]{:S(2)}) %collective-permute-start.27) | collective-permute-done | bytes 589856 | tf_op jit(solution)/shard_map/ppermute | solution.py:332
  312.1 2.4 multiply_reduce_fusion.1
  314.5 2.9 fusion.106
  318.0 3.1 fusion.36
  321.1 3.1 fusion.34
  324.2 8.1 %collective-permute-done.29 = bf16[192,1536]{1,0:T(8,128)(2,1)} collective-permute-done((bf16[192,1536]{1,0:T(8,128)(2,1)}, bf16[192,1536]{1,0:T(8,128)(2,1)}, u32[]{:S(2)}, u32[]{:S(2)}) %collective-permute-start.29) | collective-permute-done | bytes 589856 | tf_op jit(solution)/shard_map/ppermute | solution.py:332
  334.1 4.3 convolution_convert_fusion.7
  345.4 2.8 convolution_add_fusion.3
  349.0 2.5 fusion.116.dog_ref
  351.5 31.6 %attend_bwd.1 = (bf16[768,1536]{1,0:T(8,128)(2,1)}, f32[3,1,768]{2,1,0:T(1,128)}) custom-call(s32[1]{0:T(128)} %bitcast.3.order_ref, bf16[768,1536]{1,0:T(8,128)(2,1)} %convolution_convert_fusion.2.proj_ref, f32[3,1,768]{2,1,0:T(1,128)} %reshape.176.lg_ref, f32[768,384]{1,0:T(8,128)} %fusion.116.dog_ref, f32[3,768,768]{2,1,0:T(8,128)} %get-tuple-element.125.pr_ref, ...), custom_call_target="tpu_custom_call" | custom-call | flops 15000000512 | bytes 10000000 | tf_op jit(solution)/shard_map/attend_bwd/pallas_call | solution.py:280
  393.6 5.6 fusion.4
  400.3 4.2 all-to-all-start.2
  404.8 5.3 convolution_convert_fusion.1
  410.9 2.2 convert_add_fusion.2
  417.8 4.8 fusion.3
  428.7 10.2 %collective-permute-done.35 = bf16[192,1536]{1,0:T(8,128)(2,1)} collective-permute-done((bf16[192,1536]{1,0:T(8,128)(2,1)}, bf16[192,1536]{1,0:T(8,128)(2,1)}, u32[]{:S(2)}, u32[]{:S(2)}) %collective-permute-start.35) | collective-permute-done | bytes 589856 | tf_op jit(solution)/shard_map/ppermute | solution.py:332
  438.8 2.7 multiply_reduce_fusion.3
  447.4 2.2 add_convert_fusion
  453.1 2.4 collective-permute-start.48
  455.4 4.2 convolution_convert_fusion.3
  460.6 3.8 all-to-all-start.3
  466.9 4.4 convert_add_fusion
  479.4 15.3 %all-to-all-done.3 = bf16[208,4,384]{2,0,1:T(8,128)(2,1)S(1)} async-done(((bf16[208,4,384]{2,0,1:T(8,128)(2,1)}), bf16[208,4,384]{2,0,1:T(8,128)(2,1)S(1)}, u32[]{:S(2)}, u32[]{:S(2)}) %all-to-all-start.3) | async-done | bytes 639008 | tf_op jit(solution)/shard_map/all_to_all | solution.py:471
  496.1 2.1 fusion.48
  505.7 4.6 collective-permute-done.42
  512.5 2.3 fusion.51
  514.8 14.2 %collective-permute-done.40 = bf16[384,1536]{1,0:T(8,128)(2,1)} collective-permute-done((bf16[384,1536]{1,0:T(8,128)(2,1)}, bf16[384,1536]{1,0:T(8,128)(2,1)}, u32[]{:S(2)}, u32[]{:S(2)}) %collective-permute-start.40) | collective-permute-done | bytes 1179680 | tf_op jit(solution)/shard_map/ppermute | solution.py:332
  529.0 2.4 fusion.26
  537.9 2.3 fusion.49
  548.4 2.7 bitcast_convert_fusion
  552.3 11.1 %collective-permute-done.46 = bf16[192,1536]{1,0:T(8,128)(2,1)} collective-permute-done((bf16[192,1536]{1,0:T(8,128)(2,1)}, bf16[192,1536]{1,0:T(8,128)(2,1)}, u32[]{:S(2)}, u32[]{:S(2)}) %collective-permute-start.46) | collective-permute-done | bytes 589856 | tf_op jit(solution)/shard_map/ppermute | solution.py:332
  (356 shorter events, 132.5 us)
Async XLA Ops:
  9.7 37.0 %all-to-all-start = ((bf16[4,192,384]{2,1,0:T(8,128)(2,1)}), bf16[4,192,384]{2,1,0:T(8,128)(2,1)S(1)}, u32[]{:S(2)}, u32[]{:S(2)}) async-start(bf16[4,192,384]{2,1,0:T(8,128)(2,1)} %dynamic-slice_bitcast_fusion.1), calls=%async_computation | async-start | bytes 1179648 | tf_op jit(solution)/shard_map/all_to_all | solution.py:385
  16.1 178.8 %all-gather.2.cloned.1.call-start = ((), (), s32[]{:S(2)}) async-start(), calls=%async_computation.6 | async-start | bytes 1327104 | tf_op jit(solution)/shard_map/all_gather | solution.py:481
  17.4 76.8 %copy-start.53 = (bf16[1024,192]{0,1:T(8,128)(2,1)S(1)}, bf16[1024,192]{0,1:T(8,128)(2,1)}, u32[]{:S(2)}) copy-start(bf16[1024,192]{0,1:T(8,128)(2,1)} %param.21) | copy-start | bytes 1179652
  18.1 80.0 %copy-start.21 = (bf16[192,1664]{1,0:T(8,128)(2,1)}, bf16[192,1664]{1,0:T(8,128)(2,1)S(1)}, u32[]{:S(2)}) copy-start(bf16[192,1664]{1,0:T(8,128)(2,1)S(1)} %concatenate.104.refs_0_) | copy-start | bytes 1916932
  18.1 30.2 %collective-permute-start.4 = (bf16[192,1664]{1,0:T(8,128)(2,1)S(1)}, bf16[192,1664]{1,0:T(8,128)(2,1)}, u32[]{:S(2)}, u32[]{:S(2)}) collective-permute-start(bf16[192,1664]{1,0:T(8,128)(2,1)S(1)} %concatenate.104.refs_0_), channel_id=1, source_target_pairs={{0,1},{1,2},{2,3},{3,0},{4,5},{5,6},{6,7},{7,4},{8,9},{9,10},{10,1... | collective-permute-start | bytes 1916936 | tf_op jit(solution)/shard_map/ppermute | solution.py:489
  20.2 35.2 %collective-permute-start.6 = (bf16[192,1664]{1,0:T(8,128)(2,1)S(1)}, bf16[192,1664]{1,0:T(8,128)(2,1)}, u32[]{:S(2)}, u32[]{:S(2)}) collective-permute-start(bf16[192,1664]{1,0:T(8,128)(2,1)S(1)} %concatenate.104.refs_0_), channel_id=1, source_target_pairs={{0,3},{1,0},{2,1},{3,2},{4,7},{5,4},{6,5},{7,6},{8,11},{9,8},{10,9... | collective-permute-start | bytes 1916936 | tf_op jit(solution)/shard_map/ppermute | solution.py:489
  22.0 33.4 %collective-permute-start.3 = (bf16[192,1664]{1,0:T(8,128)(2,1)S(1)}, bf16[192,1664]{1,0:T(8,128)(2,1)}, u32[]{:S(2)}, u32[]{:S(2)}) collective-permute-start(bf16[192,1664]{1,0:T(8,128)(2,1)S(1)} %concatenate.104.refs_0_), channel_id=1, source_target_pairs={{0,16},{16,0},{1,17},{17,1},{2,18},{18,2},{3,19},{19,3},{4,20},{20... | collective-permute-start | bytes 1916936 | tf_op jit(solution)/shard_map/ppermute | solution.py:332
  46.8 13.1 %collective-permute-start.1 = (bf16[192,1536]{1,0:T(8,128)(2,1)S(1)}, bf16[192,1536]{1,0:T(8,128)(2,1)S(1)}, u32[]{:S(2)}, u32[]{:S(2)}) collective-permute-start(bf16[192,1536]{1,0:T(8,128)(2,1)S(1)} %bitcast.178), channel_id=1, source_target_pairs={{0,8},{4,12},{8,0},{12,4},{1,9},{5,13},{9,1},{13,5},{2,10},{6,14},... | collective-permute-start | bytes 1769480 | tf_op jit(solution)/shard_map/ppermute | solution.py:332
  59.9 32.7 %collective-permute-start.8 = (bf16[192,1664]{1,0:T(8,128)(2,1)S(1)}, bf16[192,1664]{1,0:T(8,128)(2,1)}, u32[]{:S(2)}, u32[]{:S(2)}) collective-permute-start(bf16[192,1664]{1,0:T(8,128)(2,1)S(1)} %concatenate.104.refs_0_), channel_id=1, source_target_pairs={{0,2},{1,3},{2,0},{3,1},{4,6},{5,7},{6,4},{7,5},{8,10},{9,11},{10,... | collective-permute-start | bytes 1916936 | tf_op jit(solution)/shard_map/ppermute | solution.py:489
  60.1 36.9 %collective-permute-start = (bf16[192,1536]{1,0:T(8,128)(2,1)S(1)}, bf16[192,1536]{1,0:T(8,128)(2,1)S(1)}, u32[]{:S(2)}, u32[]{:S(2)}) collective-permute-start(bf16[192,1536]{1,0:T(8,128)(2,1)S(1)} %bitcast.179), channel_id=1, source_target_pairs={{0,4},{4,0},{8,12},{12,8},{1,5},{5,1},{9,13},{13,9},{2,6},{6,2},{1... | collective-permute-start | bytes 1769480 | tf_op jit(solution)/shard_map/ppermute | solution.py:332
  60.1 37.3 %collective-permute-start.2 = (bf16[192,1536]{1,0:T(8,128)(2,1)S(1)}, bf16[192,1536]{1,0:T(8,128)(2,1)S(1)}, u32[]{:S(2)}, u32[]{:S(2)}) collective-permute-start(bf16[192,1536]{1,0:T(8,128)(2,1)S(1)} %collective-permute-done.1), channel_id=1, source_target_pairs={{0,4},{4,0},{8,12},{12,8},{1,5},{5,1},{9,13},{13,9},{2,6},{6,2},{1... | collective-permute-start | bytes 1769480 | tf_op jit(solution)/shard_map/ppermute | solution.py:332
  60.6 37.5 %collective-permute-start.5 = (bf16[192,1664]{1,0:T(8,128)(2,1)}, bf16[192,1664]{1,0:T(8,128)(2,1)}, u32[]{:S(2)}, u32[]{:S(2)}) collective-permute-start(bf16[192,1664]{1,0:T(8,128)(2,1)} %collective-permute-done.4.refs_2_), channel_id=1, source_target_pairs={{0,16},{16,0},{1,17},{17,1},{2,18},{18,2},{3,19},{19,3},{4,20},{20... | collective-permute-start | bytes 1916936 | tf_op jit(solution)/shard_map/ppermute | solution.py:332
  62.2 39.9 %collective-permute-start.7 = (bf16[192,1664]{1,0:T(8,128)(2,1)}, bf16[192,1664]{1,0:T(8,128)(2,1)}, u32[]{:S(2)}, u32[]{:S(2)}) collective-permute-start(bf16[192,1664]{1,0:T(8,128)(2,1)} %collective-permute-done.6.refs_4_), channel_id=1, source_target_pairs={{0,16},{16,0},{1,17},{17,1},{2,18},{18,2},{3,19},{19,3},{4,20},{20... | collective-permute-start | bytes 1916936 | tf_op jit(solution)/shard_map/ppermute | solution.py:332
  92.6 24.0 %collective-permute-start.9 = (bf16[192,1664]{1,0:T(8,128)(2,1)}, bf16[192,1664]{1,0:T(8,128)(2,1)}, u32[]{:S(2)}, u32[]{:S(2)}) collective-permute-start(bf16[192,1664]{1,0:T(8,128)(2,1)} %collective-permute-done.8.refs_6_), channel_id=1, source_target_pairs={{0,16},{16,0},{1,17},{17,1},{2,18},{18,2},{3,19},{19,3},{4,20},{20... | collective-permute-start | bytes 1916936 | tf_op jit(solution)/shard_map/ppermute | solution.py:332
  97.0 24.7 %copy-start.6 = (bf16[192,1536]{1,0:T(8,128)(2,1)}, bf16[192,1536]{1,0:T(8,128)(2,1)S(1)}, u32[]{:S(2)}) copy-start(bf16[192,1536]{1,0:T(8,128)(2,1)S(1)} %collective-permute-done) | copy-start | bytes 1769476
  97.0 42.0 %collective-permute-start.10 = (bf16[192,3072]{1,0:T(8,128)(2,1)}, bf16[192,3072]{1,0:T(8,128)(2,1)S(1)}, u32[]{:S(2)}, u32[]{:S(2)}) collective-permute-start(bf16[192,3072]{1,0:T(8,128)(2,1)} %pad_maximum_fusion.5.refs_0_), channel_id=1, source_target_pairs={{0,16},{16,0},{1,17},{17,1},{2,18},{18,2},{3,19},{19,3},{4,20},{20... | collective-permute-start | bytes 3538952 | tf_op jit(solution)/shard_map/ppermute | solution.py:332
  97.4 24.2 %copy-start.8 = (bf16[192,1536]{1,0:T(8,128)(2,1)}, bf16[192,1536]{1,0:T(8,128)(2,1)S(1)}, u32[]{:S(2)}) copy-start(bf16[192,1536]{1,0:T(8,128)(2,1)S(1)} %collective-permute-done.2) | copy-start | bytes 1769476
  98.0 46.8 %collective-permute-start.11 = (bf16[192,3072]{1,0:T(8,128)(2,1)}, bf16[192,3072]{1,0:T(8,128)(2,1)S(1)}, u32[]{:S(2)}, u32[]{:S(2)}) collective-permute-start(bf16[192,3072]{1,0:T(8,128)(2,1)} %pad_maximum_fusion.5.refs_0_), channel_id=1, source_target_pairs={{0,1},{1,2},{2,3},{3,0},{4,5},{5,6},{6,7},{7,4},{8,9},{9,10},{10,1... | collective-permute-start | bytes 3538952 | tf_op jit(solution)/shard_map/ppermute | solution.py:489
  98.1 60.9 %collective-permute-start.12 = (bf16[192,3072]{1,0:T(8,128)(2,1)}, bf16[192,3072]{1,0:T(8,128)(2,1)}, u32[]{:S(2)}, u32[]{:S(2)}) collective-permute-start(bf16[192,3072]{1,0:T(8,128)(2,1)} %pad_maximum_fusion.5.refs_0_), channel_id=1, source_target_pairs={{0,3},{1,0},{2,1},{3,2},{4,7},{5,4},{6,5},{7,6},{8,11},{9,8},{10,9... | collective-permute-start | bytes 3538952 | tf_op jit(solution)/shard_map/ppermute | solution.py:489
  144.9 47.0 %copy-start.40 = (bf16[192,3072]{1,0:T(8,128)(2,1)}, bf16[192,3072]{1,0:T(8,128)(2,1)S(1)}, u32[]{:S(2)}) copy-start(bf16[192,3072]{1,0:T(8,128)(2,1)S(1)} %collective-permute-done.11.refs_2_) | copy-start | bytes 3538948
  159.0 53.2 %collective-permute-start.15 = (bf16[192,3072]{1,0:T(8,128)(2,1)}, bf16[192,3072]{1,0:T(8,128)(2,1)}, u32[]{:S(2)}, u32[]{:S(2)}) collective-permute-start(bf16[192,3072]{1,0:T(8,128)(2,1)} %pad_maximum_fusion.5.refs_0_), channel_id=1, source_target_pairs={{0,2},{1,3},{2,0},{3,1},{4,6},{5,7},{6,4},{7,5},{8,10},{9,11},{10,... | collective-permute-start | bytes 3538952 | tf_op jit(solution)/shard_map/ppermute | solution.py:489
  161.2 30.7 %collective-permute-start.13 = (bf16[192,3072]{1,0:T(8,128)(2,1)S(1)}, bf16[192,3072]{1,0:T(8,128)(2,1)S(1)}, u32[]{:S(2)}, u32[]{:S(2)}) collective-permute-start(bf16[192,3072]{1,0:T(8,128)(2,1)S(1)} %collective-permute-done.11.refs_2_), channel_id=1, source_target_pairs={{0,16},{16,0},{1,17},{17,1},{2,18},{18,2},{3,19},{19,3},{4,20},{20... | collective-permute-start | bytes 3538952 | tf_op jit(solution)/shard_map/ppermute | solution.py:332
  197.2 15.0 %collective-permute-start.14 = (bf16[384,1536]{1,0:T(8,128)(2,1)S(1)}, bf16[384,1536]{1,0:T(8,128)(2,1)S(1)}, u32[]{:S(2)}, u32[]{:S(2)}) collective-permute-start(bf16[384,1536]{1,0:T(8,128)(2,1)S(1)} %convolution_convert_fusion.6), channel_id=1, source_target_pairs={{0,4},{4,0},{8,12},{12,8},{1,5},{5,1},{9,13},{13,9},{2,6},{6,2},{1... | collective-permute-start | bytes 3538952 | tf_op jit(solution)/shard_map/ppermute | solution.py:332
  197.3 30.5 %collective-permute-start.17 = (bf16[192,3072]{1,0:T(8,128)(2,1)}, bf16[192,3072]{1,0:T(8,128)(2,1)}, u32[]{:S(2)}, u32[]{:S(2)}) collective-permute-start(bf16[192,3072]{1,0:T(8,128)(2,1)} %collective-permute-done.12.refs_4_), channel_id=1, source_target_pairs={{0,16},{16,0},{1,17},{17,1},{2,18},{18,2},{3,19},{19,3},{4,20},{20... | collective-permute-start | bytes 3538952 | tf_op jit(solution)/shard_map/ppermute | solution.py:332
  215.4 13.4 %collective-permute-start.16 = (bf16[192,1536]{1,0:T(8,128)(2,1)}, bf16[192,1536]{1,0:T(8,128)(2,1)}, u32[]{:S(2)}, u32[]{:S(2)}) collective-permute-start(bf16[192,1536]{1,0:T(8,128)(2,1)} %slice.505), channel_id=1, source_target_pairs={{0,8},{4,12},{8,0},{12,4},{1,9},{5,13},{9,1},{13,5},{2,10},{6,14},... | collective-permute-start | bytes 1769480 | tf_op jit(solution)/shard_map/ppermute | solution.py:332
  221.6 19.6 %all-to-all-start.1 = ((bf16[4,192,384]{2,1,0:T(8,128)(2,1)}), bf16[4,192,384]{2,1,0:T(8,128)(2,1)}, u32[]{:S(2)}, u32[]{:S(2)}) async-start(bf16[4,192,384]{2,1,0:T(8,128)(2,1)} %dynamic-slice_bitcast_fusion), calls=%async_computation.1 | async-start | bytes 1179648 | tf_op jit(solution)/shard_map/all_to_all | solution.py:385
  225.8 272.4 %reduce-scatter.5.cloned.1.call-start = ((), (), s32[]{:S(2)}) async-start(), calls=%async_computation.8 | async-start | bytes 3538944 | tf_op jit(solution)/shard_map/reduce_scatter | solution.py:553
  226.2 27.2 %collective-permute-start.21 = (bf16[192,3072]{1,0:T(8,128)(2,1)}, bf16[192,3072]{1,0:T(8,128)(2,1)}, u32[]{:S(2)}, u32[]{:S(2)}) collective-permute-start(bf16[192,3072]{1,0:T(8,128)(2,1)} %collective-permute-done.15.refs_6_), channel_id=1, source_target_pairs={{0,16},{16,0},{1,17},{17,1},{2,18},{18,2},{3,19},{19,3},{4,20},{20... | collective-permute-start | bytes 3538952 | tf_op jit(solution)/shard_map/ppermute | solution.py:332
  232.4 13.2 %collective-permute-start.19 = (bf16[192,1536]{1,0:T(8,128)(2,1)}, bf16[192,1536]{1,0:T(8,128)(2,1)}, u32[]{:S(2)}, u32[]{:S(2)}) collective-permute-start(bf16[192,1536]{1,0:T(8,128)(2,1)} %multiply_convert_fusion.4), channel_id=1, source_target_pairs={{0,8},{4,12},{8,0},{12,4},{1,9},{5,13},{9,1},{13,5},{2,10},{6,14},... | collective-permute-start | bytes 1769480 | tf_op jit(solution)/shard_map/ppermute | solution.py:332
  242.4 19.2 %collective-permute-start.18 = (bf16[192,1536]{1,0:T(8,128)(2,1)}, bf16[192,1536]{1,0:T(8,128)(2,1)S(1)}, u32[]{:S(2)}, u32[]{:S(2)}) collective-permute-start(bf16[192,1536]{1,0:T(8,128)(2,1)} %multiply_convert_fusion.4), channel_id=1, source_target_pairs={{0,4},{4,0},{8,12},{12,8},{1,5},{5,1},{9,13},{13,9},{2,6},{6,2},{1... | collective-permute-start | bytes 1769480 | tf_op jit(solution)/shard_map/ppermute | solution.py:332
  242.4 19.1 %collective-permute-start.24 = (bf16[192,1536]{1,0:T(8,128)(2,1)S(1)}, bf16[192,1536]{1,0:T(8,128)(2,1)S(1)}, u32[]{:S(2)}, u32[]{:S(2)}) collective-permute-start(bf16[192,1536]{1,0:T(8,128)(2,1)S(1)} %bitcast.184), channel_id=1, source_target_pairs={{0,8},{4,12},{8,0},{12,4},{1,9},{5,13},{9,1},{13,5},{2,10},{6,14},... | collective-permute-start | bytes 1769480 | tf_op jit(solution)/shard_map/ppermute | solution.py:332
  245.6 16.5 %collective-permute-start.20 = (bf16[192,1536]{1,0:T(8,128)(2,1)}, bf16[192,1536]{1,0:T(8,128)(2,1)S(1)}, u32[]{:S(2)}, u32[]{:S(2)}) collective-permute-start(bf16[192,1536]{1,0:T(8,128)(2,1)} %collective-permute-done.19), channel_id=1, source_target_pairs={{0,4},{4,0},{8,12},{12,8},{1,5},{5,1},{9,13},{13,9},{2,6},{6,2},{1... | collective-permute-start | bytes 1769480 | tf_op jit(solution)/shard_map/ppermute | solution.py:332
  261.5 8.3 %collective-permute-start.22 = (bf16[192,1536]{1,0:T(8,128)(2,1)S(1)}, bf16[192,1536]{1,0:T(8,128)(2,1)S(1)}, u32[]{:S(2)}, u32[]{:S(2)}) collective-permute-start(bf16[192,1536]{1,0:T(8,128)(2,1)S(1)} %bitcast.186), channel_id=1, source_target_pairs={{0,4},{4,0},{8,12},{12,8},{1,5},{5,1},{9,13},{13,9},{2,6},{6,2},{1... | collective-permute-start | bytes 1769480 | tf_op jit(solution)/shard_map/ppermute | solution.py:332
  261.6 8.3 %collective-permute-start.25 = (bf16[192,1536]{1,0:T(8,128)(2,1)S(1)}, bf16[192,1536]{1,0:T(8,128)(2,1)S(1)}, u32[]{:S(2)}, u32[]{:S(2)}) collective-permute-start(bf16[192,1536]{1,0:T(8,128)(2,1)S(1)} %collective-permute-done.24), channel_id=1, source_target_pairs={{0,4},{4,0},{8,12},{12,8},{1,5},{5,1},{9,13},{13,9},{2,6},{6,2},{1... | collective-permute-start | bytes 1769480 | tf_op jit(solution)/shard_map/ppermute | solution.py:332
  283.5 7.1 %collective-permute-start.26 = (bf16[384,1536]{1,0:T(8,128)(2,1)}, bf16[384,1536]{1,0:T(8,128)(2,1)}, u32[]{:S(2)}, u32[]{:S(2)}) collective-permute-start(bf16[384,1536]{1,0:T(8,128)(2,1)} %convolution_convert_fusion.4), channel_id=1, source_target_pairs={{0,4},{4,0},{8,12},{12,8},{1,5},{5,1},{9,13},{13,9},{2,6},{6,2},{1... | collective-permute-start | bytes 3538952 | tf_op jit(solution)/shard_map/ppermute | solution.py:332
  288.7 55.8 %collective-permute-start.23 = (bf16[384,1536]{1,0:T(8,128)(2,1)}, bf16[384,1536]{1,0:T(8,128)(2,1)}, u32[]{:S(2)}, u32[]{:S(2)}) collective-permute-start(bf16[384,1536]{1,0:T(8,128)(2,1)} %convolution_convert_fusion.5), channel_id=1, source_target_pairs={{0,4},{4,0},{8,12},{12,8},{1,5},{5,1},{9,13},{13,9},{2,6},{6,2},{1... | collective-permute-start | bytes 3538952 | tf_op jit(solution)/shard_map/ppermute | solution.py:332
  296.4 15.7 %collective-permute-start.27 = (bf16[192,1536]{1,0:T(8,128)(2,1)}, bf16[192,1536]{1,0:T(8,128)(2,1)}, u32[]{:S(2)}, u32[]{:S(2)}) collective-permute-start(bf16[192,1536]{1,0:T(8,128)(2,1)} %slice.504), channel_id=1, source_target_pairs={{0,8},{4,12},{8,0},{12,4},{1,9},{5,13},{9,1},{13,5},{2,10},{6,14},... | collective-permute-start | bytes 1769480 | tf_op jit(solution)/shard_map/ppermute | solution.py:332
  299.6 44.9 %collective-permute-start.31 = (bf16[768,1024]{1,0:T(8,128)(2,1)}, bf16[768,1024]{1,0:T(8,128)(2,1)}, u32[]{:S(2)}, u32[]{:S(2)}) collective-permute-start(bf16[768,1024]{1,0:T(8,128)(2,1)} %convolution_convert_fusion.8), channel_id=1, source_target_pairs={{0,16},{16,0},{1,17},{17,1},{2,18},{18,2},{3,19},{19,3},{4,20},{20... | collective-permute-start | bytes 4718600 | tf_op jit(solution)/shard_map/ppermute | solution.py:332
  317.5 14.9 %collective-permute-start.29 = (bf16[192,1536]{1,0:T(8,128)(2,1)}, bf16[192,1536]{1,0:T(8,128)(2,1)}, u32[]{:S(2)}, u32[]{:S(2)}) collective-permute-start(bf16[192,1536]{1,0:T(8,128)(2,1)} %get-tuple-element.117), channel_id=1, source_target_pairs={{0,8},{4,12},{8,0},{12,4},{1,9},{5,13},{9,1},{13,5},{2,10},{6,14},... | collective-permute-start | bytes 1769480 | tf_op jit(solution)/shard_map/ppermute | solution.py:332
  324.2 18.4 %collective-permute-start.28 = (bf16[192,1536]{1,0:T(8,128)(2,1)}, bf16[192,1536]{1,0:T(8,128)(2,1)}, u32[]{:S(2)}, u32[]{:S(2)}) collective-permute-start(bf16[192,1536]{1,0:T(8,128)(2,1)} %get-tuple-element.117), channel_id=1, source_target_pairs={{0,4},{4,0},{8,12},{12,8},{1,5},{5,1},{9,13},{13,9},{2,6},{6,2},{1... | collective-permute-start | bytes 1769480 | tf_op jit(solution)/shard_map/ppermute | solution.py:332
  332.3 10.3 %collective-permute-start.30 = (bf16[192,1536]{1,0:T(8,128)(2,1)}, bf16[192,1536]{1,0:T(8,128)(2,1)}, u32[]{:S(2)}, u32[]{:S(2)}) collective-permute-start(bf16[192,1536]{1,0:T(8,128)(2,1)} %collective-permute-done.29), channel_id=1, source_target_pairs={{0,4},{4,0},{8,12},{12,8},{1,5},{5,1},{9,13},{13,9},{2,6},{6,2},{1... | collective-permute-start | bytes 1769480 | tf_op jit(solution)/shard_map/ppermute | solution.py:332
  338.4 53.9 %collective-permute-start.33 = (bf16[768,1024]{1,0:T(8,128)(2,1)}, bf16[768,1024]{1,0:T(8,128)(2,1)}, u32[]{:S(2)}, u32[]{:S(2)}) collective-permute-start(bf16[768,1024]{1,0:T(8,128)(2,1)} %convolution_convert_fusion.7), channel_id=1, source_target_pairs={{0,16},{16,0},{1,17},{17,1},{2,18},{18,2},{3,19},{19,3},{4,20},{20... | collective-permute-start | bytes 4718600 | tf_op jit(solution)/shard_map/ppermute | solution.py:332
  348.3 44.1 %collective-permute-start.32 = (bf16[192,1536]{1,0:T(8,128)(2,1)S(1)}, bf16[192,1536]{1,0:T(8,128)(2,1)S(1)}, u32[]{:S(2)}, u32[]{:S(2)}) collective-permute-start(bf16[192,1536]{1,0:T(8,128)(2,1)S(1)} %slice.503), channel_id=1, source_target_pairs={{0,8},{4,12},{8,0},{12,4},{1,9},{5,13},{9,1},{13,5},{2,10},{6,14},... | collective-permute-start | bytes 1769480 | tf_op jit(solution)/shard_map/ppermute | solution.py:332
  351.5 32.6 %copy-start.19 = (f32[768,1024]{1,0:T(8,128)S(1)}, f32[768,1024]{1,0:T(8,128)}, u32[]{:S(2)}) copy-start(f32[768,1024]{1,0:T(8,128)} %fusion.36) | copy-start | bytes 9437188
  387.4 41.2 %collective-permute-start.47 = (bf16[384,1024]{1,0:T(8,128)(2,1)}, bf16[384,1024]{1,0:T(8,128)(2,1)}, u32[]{:S(2)}, u32[]{:S(2)}) collective-permute-start(bf16[384,1024]{1,0:T(8,128)(2,1)} %pad_maximum_fusion.8), channel_id=1, source_target_pairs={{0,1},{1,0},{2,3},{3,2},{4,5},{5,4},{6,7},{7,6},{8,9},{9,8},{10,11... | collective-permute-start | bytes 2359304 | tf_op jit(solution)/shard_map/ppermute | solution.py:332
  399.2 18.6 %collective-permute-start.34 = (bf16[384,1536]{1,0:T(8,128)(2,1)}, bf16[384,1536]{1,0:T(8,128)(2,1)}, u32[]{:S(2)}, u32[]{:S(2)}) collective-permute-start(bf16[384,1536]{1,0:T(8,128)(2,1)} %fusion.4), channel_id=1, source_target_pairs={{0,4},{4,0},{8,12},{12,8},{1,5},{5,1},{9,13},{13,9},{2,6},{6,2},{1... | collective-permute-start | bytes 3538952 | tf_op jit(solution)/shard_map/ppermute | solution.py:332
  400.3 49.4 %all-to-all-start.2 = ((bf16[192,4,384]{2,0,1:T(8,128)(2,1)}), bf16[192,4,384]{2,0,1:T(8,128)(2,1)}, u32[]{:S(2)}, u32[]{:S(2)}) async-start(bf16[192,4,384]{2,0,1:T(8,128)(2,1)} %bitcast.164), calls=%async_computation.2 | async-start | bytes 1179648 | tf_op jit(solution)/shard_map/all_to_all | solution.py:471
  404.5 131.8 %reduce-scatter.3.cloned.1.call-start = ((), (), s32[]{:S(2)}) async-start(), calls=%async_computation.7 | async-start | bytes 1327104 | tf_op jit(solution)/shard_map/reduce_scatter | solution.py:553
  410.1 56.8 %collective-permute-start.39 = (bf16[768,1536]{1,0:T(8,128)(2,1)}, bf16[768,1536]{1,0:T(8,128)(2,1)}, u32[]{:S(2)}, u32[]{:S(2)}) collective-permute-start(bf16[768,1536]{1,0:T(8,128)(2,1)} %convolution_convert_fusion.1), channel_id=1, source_target_pairs={{0,16},{16,0},{1,17},{17,1},{2,18},{18,2},{3,19},{19,3},{4,20},{20... | collective-permute-start | bytes 7077896 | tf_op jit(solution)/shard_map/ppermute | solution.py:332
  415.9 80.2 %collective-permute-start.45 = (bf16[384,1024]{1,0:T(8,128)(2,1)}, bf16[384,1024]{1,0:T(8,128)(2,1)}, u32[]{:S(2)}, u32[]{:S(2)}) collective-permute-start(bf16[384,1024]{1,0:T(8,128)(2,1)} %pad_maximum_fusion.7), channel_id=1, source_target_pairs={{0,1},{1,0},{2,3},{3,2},{4,5},{5,4},{6,7},{7,6},{8,9},{9,8},{10,11... | collective-permute-start | bytes 2359304 | tf_op jit(solution)/shard_map/ppermute | solution.py:332
  423.6 15.2 %collective-permute-start.35 = (bf16[192,1536]{1,0:T(8,128)(2,1)}, bf16[192,1536]{1,0:T(8,128)(2,1)}, u32[]{:S(2)}, u32[]{:S(2)}) collective-permute-start(bf16[192,1536]{1,0:T(8,128)(2,1)} %slice.502), channel_id=1, source_target_pairs={{0,8},{4,12},{8,0},{12,4},{1,9},{5,13},{9,1},{13,5},{2,10},{6,14},... | collective-permute-start | bytes 1769480 | tf_op jit(solution)/shard_map/ppermute | solution.py:332
  425.2 22.2 %copy-start.14 = (f32[192,1536]{1,0:T(8,128)S(1)}, f32[192,1536]{1,0:T(8,128)}, u32[]{:S(2)}) copy-start(f32[192,1536]{1,0:T(8,128)} %get-tuple-element.213) | copy-start | bytes 3538948
  449.7 16.6 %collective-permute-start.37 = (bf16[4,1,192,384]{3,2,1,0:T(8,128)(2,1)}, bf16[4,1,192,384]{3,2,1,0:T(8,128)(2,1)}, u32[]{:S(2)}, u32[]{:S(2)}) collective-permute-start(bf16[4,1,192,384]{3,2,1,0:T(8,128)(2,1)} %bitcast.31), channel_id=1, source_target_pairs={{0,8},{4,12},{8,0},{12,4},{1,9},{5,13},{9,1},{13,5},{2,10},{6,14},... | collective-permute-start | bytes 1769480 | tf_op jit(solution)/shard_map/ppermute | solution.py:332
  453.1 57.3 %collective-permute-start.48 = (bf16[192,1024]{1,0:T(8,128)(2,1)}, bf16[192,1024]{1,0:T(8,128)(2,1)S(1)}, u32[]{:S(2)}, u32[]{:S(2)}) collective-permute-start(bf16[192,1024]{1,0:T(8,128)(2,1)} %fusion.50), channel_id=1, source_target_pairs={{0,2},{1,3},{2,0},{3,1},{4,6},{5,7},{6,4},{7,5},{8,10},{9,11},{10,... | collective-permute-start | bytes 1179656 | tf_op jit(solution)/shard_map/ppermute | solution.py:332
  459.7 15.9 %collective-permute-start.36 = (bf16[4,1,192,384]{3,2,1,0:T(8,128)(2,1)}, bf16[4,1,192,384]{3,2,1,0:T(8,128)(2,1)}, u32[]{:S(2)}, u32[]{:S(2)}) collective-permute-start(bf16[4,1,192,384]{3,2,1,0:T(8,128)(2,1)} %bitcast.31), channel_id=1, source_target_pairs={{0,4},{4,0},{8,12},{12,8},{1,5},{5,1},{9,13},{13,9},{2,6},{6,2},{1... | collective-permute-start | bytes 1769480 | tf_op jit(solution)/shard_map/ppermute | solution.py:332
  460.6 34.1 %all-to-all-start.3 = ((bf16[208,4,384]{2,0,1:T(8,128)(2,1)}), bf16[208,4,384]{2,0,1:T(8,128)(2,1)S(1)}, u32[]{:S(2)}, u32[]{:S(2)}) async-start(bf16[208,4,384]{2,0,1:T(8,128)(2,1)} %bitcast.195), calls=%async_computation.3 | async-start | bytes 1277952 | tf_op jit(solution)/shard_map/all_to_all | solution.py:471
  466.4 33.8 %collective-permute-start.38 = (bf16[4,1,192,384]{3,2,1,0:T(8,128)(2,1)}, bf16[4,1,192,384]{3,2,1,0:T(8,128)(2,1)}, u32[]{:S(2)}, u32[]{:S(2)}) collective-permute-start(bf16[4,1,192,384]{3,2,1,0:T(8,128)(2,1)} %collective-permute-done.37), channel_id=1, source_target_pairs={{0,4},{4,0},{8,12},{12,8},{1,5},{5,1},{9,13},{13,9},{2,6},{6,2},{1... | collective-permute-start | bytes 1769480 | tf_op jit(solution)/shard_map/ppermute | solution.py:332
  473.8 55.2 %collective-permute-start.40 = (bf16[384,1536]{1,0:T(8,128)(2,1)}, bf16[384,1536]{1,0:T(8,128)(2,1)}, u32[]{:S(2)}, u32[]{:S(2)}) collective-permute-start(bf16[384,1536]{1,0:T(8,128)(2,1)} %pad_maximum_fusion.6), channel_id=1, source_target_pairs={{0,1},{1,0},{2,3},{3,2},{4,5},{5,4},{6,7},{7,6},{8,9},{9,8},{10,11... | collective-permute-start | bytes 3538952 | tf_op jit(solution)/shard_map/ppermute | solution.py:332
  494.8 15.6 %collective-permute-start.42 = (bf16[4,1,208,384]{3,2,1,0:T(8,128)(2,1)S(1)}, bf16[4,1,208,384]{3,2,1,0:T(8,128)(2,1)}, u32[]{:S(2)}, u32[]{:S(2)}) collective-permute-start(bf16[4,1,208,384]{3,2,1,0:T(8,128)(2,1)S(1)} %bitcast.191), channel_id=1, source_target_pairs={{0,8},{4,12},{8,0},{12,4},{1,9},{5,13},{9,1},{13,5},{2,10},{6,14},... | collective-permute-start | bytes 1916936 | tf_op jit(solution)/shard_map/ppermute | solution.py:332
  496.1 15.1 %collective-permute-start.41 = (bf16[4,1,208,384]{3,2,1,0:T(8,128)(2,1)S(1)}, bf16[4,1,208,384]{3,2,1,0:T(8,128)(2,1)S(1)}, u32[]{:S(2)}, u32[]{:S(2)}) collective-permute-start(bf16[4,1,208,384]{3,2,1,0:T(8,128)(2,1)S(1)} %bitcast.193), channel_id=1, source_target_pairs={{0,4},{4,0},{8,12},{12,8},{1,5},{5,1},{9,13},{13,9},{2,6},{6,2},{1... | collective-permute-start | bytes 1916936 | tf_op jit(solution)/shard_map/ppermute | solution.py:332
  500.2 36.1 %collective-permute-start.49 = (bf16[192,1024]{1,0:T(8,128)(2,1)}, bf16[192,1024]{1,0:T(8,128)(2,1)S(1)}, u32[]{:S(2)}, u32[]{:S(2)}) collective-permute-start(bf16[192,1024]{1,0:T(8,128)(2,1)} %fusion.48), channel_id=1, source_target_pairs={{0,2},{1,3},{2,0},{3,1},{4,6},{5,7},{6,4},{7,5},{8,10},{9,11},{10,... | collective-permute-start | bytes 1179656 | tf_op jit(solution)/shard_map/ppermute | solution.py:332
  510.4 29.8 %collective-permute-start.43 = (bf16[4,1,208,384]{3,2,1,0:T(8,128)(2,1)}, bf16[4,1,208,384]{3,2,1,0:T(8,128)(2,1)S(1)}, u32[]{:S(2)}, u32[]{:S(2)}) collective-permute-start(bf16[4,1,208,384]{3,2,1,0:T(8,128)(2,1)} %collective-permute-done.42), channel_id=1, source_target_pairs={{0,4},{4,0},{8,12},{12,8},{1,5},{5,1},{9,13},{13,9},{2,6},{6,2},{1... | collective-permute-start | bytes 1916936 | tf_op jit(solution)/shard_map/ppermute | solution.py:332
  534.2 29.2 %collective-permute-start.46 = (bf16[192,1536]{1,0:T(8,128)(2,1)}, bf16[192,1536]{1,0:T(8,128)(2,1)}, u32[]{:S(2)}, u32[]{:S(2)}) collective-permute-start(bf16[192,1536]{1,0:T(8,128)(2,1)} %fusion.26), channel_id=1, source_target_pairs={{0,2},{1,3},{2,0},{3,1},{4,6},{5,7},{6,4},{7,5},{8,10},{9,11},{10,... | collective-permute-start | bytes 1769480 | tf_op jit(solution)/shard_map/ppermute | solution.py:332
  545.2 5.9 %collective-permute-start.44 = (f32[5,192]{1,0:T(8,128)S(1)}, f32[5,192]{1,0:T(8,128)S(1)}, u32[]{:S(2)}, u32[]{:S(2)}) collective-permute-start(f32[5,192]{1,0:T(8,128)S(1)} %bitcast.213), channel_id=1, source_target_pairs={{0,16},{16,0},{1,17},{17,1},{2,18},{18,2},{3,19},{19,3},{4,20},{20... | collective-permute-start | bytes 11528 | tf_op jit(solution)/shard_map/ppermute | solution.py:630
  (67 other events, 410.8 us)
Sparse Core Ops, SparseCore 0:
  60.7 79.7 all-gather.1
  334.2 97.0 reduce-scatter.4
  459.8 72.5 reduce-scatter.2

commit v5 on v4

--- a/solution.py
+++ b/solution.py
@@ -141,7 +141,7 @@
         ex = jnp.exp(score - top)
         prob = ex / jnp.sum(ex, axis=1, keepdims=True)
         pr_ref[0, here, :upto] = prob
-        att = mm(split(prob), v_ref[:upto, :], 1, 0).astype(att_ref.dtype)
+        att = mm(prob.astype(BF), v_ref[:upto, :], 1, 0).astype(att_ref.dtype)
         for b in range(width // STEP):
             att_ref[place_of(order_ref, i * width // STEP + b, per), :] = att[b * STEP : (b + 1) * STEP]
 

time: 579 us -> 579 us (level)
  no operation moved by 1% of the time
where the time goes in v5:
time: 579 us; the launch traced here: 573 us
  waiting for transfers between devices  210 us (36%)
  matrix products  82.6 us (14%)
  Pallas kernels  73.3 us (13%)
  other arithmetic  66.3 us (11%)
  starting transfers between devices  65.8 us (11%)
  local copies, waits for them, and re-layouts  59.8 us (10%)
  between operations  15.4 us (3%)
    ppermute x43, waiting for transfers between devices, send(): self.done.append(lax.ppermute(value, axis, pairs))  98.5 us
    dot_general x24, matrix products, dot(): lax.dot_general(a, b, (((ca,), (cb,)), ((), ())), preferred_element_type=...  82.6 us
    ppermute x6, waiting for transfers between devices, hop(): lax.ppermute(after(own, *first) if first else own, 'wid', [(i, (i + k) %...  65.9 us
    ppermute x43, starting transfers between devices, send(): self.done.append(lax.ppermute(value, axis, pairs))  35.5 us
    pallas_call x1, Pallas kernels, attend_bwd(): pl.pallas_call(functools.partial(bwd_kernel, quarter // STEP), grid=(head...  31.6 us
    all_to_all x2, waiting for transfers between devices, to_tokens(): lax.all_to_all(mine.reshape(wid * quarter, slice_width), 'wid', split_axi...  30.4 us
    pallas_call x1, Pallas kernels, attend_fwd(): pl.pallas_call(functools.partial(fwd_kernel, quarter // STEP), grid=(head...  28.6 us
    unnamed x159, local copies, waits for them, and re-layouts  18.2 us
  transfers between devices with their start and end apart: 57, of which 19 were waited for; matrix products, arithmetic and copies ran while one was open for 32% of the time, Pallas kernels for 13%

profile of v5, /device:TPU:0, one launch (start us, length us, event | category | flops | bytes accessed | tf_op | source)
XLA Modules:
  0.0 573.5 jit_solution(13807372112108218441)
XLA Ops:
  9.7 6.3 %all-to-all-start = ((bf16[4,192,384]{2,1,0:T(8,128)(2,1)}), bf16[4,192,384]{2,1,0:T(8,128)(2,1)S(1)}, u32[]{:S(2)}, u32[]{:S(2)}) async-start(bf16[4,192,384]{2,1,0:T(8,128)(2,1)} %dynamic-slice_bitcast_fusion.1), calls=%async_computation | async-start | bytes 1179648 | tf_op jit(solution)/shard_map/all_to_all | solution.py:385
  18.1 2.1 collective-permute-start.4
  23.5 23.1 %all-to-all-done = bf16[4,192,384]{2,1,0:T(8,128)(2,1)S(1)} async-done(((bf16[4,192,384]{2,1,0:T(8,128)(2,1)}), bf16[4,192,384]{2,1,0:T(8,128)(2,1)S(1)}, u32[]{:S(2)}, u32[]{:S(2)}) %all-to-all-start) | async-done | bytes 589856 | tf_op jit(solution)/shard_map/all_to_all | solution.py:385
  48.3 7.1 %collective-permute-done.6.refs_4_ = bf16[192,1664]{1,0:T(8,128)(2,1)} collective-permute-done((bf16[192,1664]{1,0:T(8,128)(2,1)S(1)}, bf16[192,1664]{1,0:T(8,128)(2,1)}, u32[]{:S(2)}, u32[]{:S(2)}) %collective-permute-start.6) | collective-permute-done | bytes 639008 | tf_op jit(solution)/shard_map/ppermute | solution.py:489
  55.4 4.5 collective-permute-done.1
  62.7 29.8 %collective-permute-done.8.refs_6_ = bf16[192,1664]{1,0:T(8,128)(2,1)} collective-permute-done((bf16[192,1664]{1,0:T(8,128)(2,1)S(1)}, bf16[192,1664]{1,0:T(8,128)(2,1)}, u32[]{:S(2)}, u32[]{:S(2)}) %collective-permute-start.8) | collective-permute-done | bytes 639008 | tf_op jit(solution)/shard_map/ppermute | solution.py:489
  94.1 2.2 pad_maximum_fusion.5.refs_0_
  98.1 4.0 collective-permute-start.12
  102.1 14.4 %collective-permute-done.9.refs_7_ = bf16[192,1664]{1,0:T(8,128)(2,1)} collective-permute-done((bf16[192,1664]{1,0:T(8,128)(2,1)}, bf16[192,1664]{1,0:T(8,128)(2,1)}, u32[]{:S(2)}, u32[]{:S(2)}) %collective-permute-start.9) | collective-permute-done | bytes 639008 | tf_op jit(solution)/shard_map/ppermute | solution.py:332
  116.5 5.1 assemble.2
  126.0 12.9 %collective-permute-done.10.refs_1_ = bf16[192,3072]{1,0:T(8,128)(2,1)S(1)} collective-permute-done((bf16[192,3072]{1,0:T(8,128)(2,1)}, bf16[192,3072]{1,0:T(8,128)(2,1)S(1)}, u32[]{:S(2)}, u32[]{:S(2)}) %collective-permute-start.10) | collective-permute-done | bytes 1179680 | tf_op jit(solution)/shard_map/ppermute | solution.py:332
  139.9 5.0 convolution_convert_fusion.2.proj_ref
  144.9 14.2 %collective-permute-done.12.refs_4_ = bf16[192,3072]{1,0:T(8,128)(2,1)} collective-permute-done((bf16[192,3072]{1,0:T(8,128)(2,1)}, bf16[192,3072]{1,0:T(8,128)(2,1)}, u32[]{:S(2)}, u32[]{:S(2)}) %collective-permute-start.12) | collective-permute-done | bytes 1179680 | tf_op jit(solution)/shard_map/ppermute | solution.py:489
  159.0 2.1 collective-permute-start.15
  162.7 28.6 %attend_fwd.1 = (bf16[768,384]{1,0:T(8,128)(2,1)}, f32[3,768,768]{2,1,0:T(8,128)}, f32[3,6,768,128]{3,2,1,0:T(8,128)}, f32[3,768,128]{2,1,0:T(8,128)}, f32[3,768...) custom-call(s32[1]{0:T(128)} %bitcast.3.order_ref, ...), custom_call_target="tpu_custom_call" | custom-call | flops 32999999488 | bytes 30000000 | tf_op jit(solution)/shard_map/attend_fwd/pallas_call | solution.py:157
  194.4 2.3 convolution_convert_fusion.6
  197.4 14.8 %collective-permute-done.15.refs_6_ = bf16[192,3072]{1,0:T(8,128)(2,1)} collective-permute-done((bf16[192,3072]{1,0:T(8,128)(2,1)}, bf16[192,3072]{1,0:T(8,128)(2,1)}, u32[]{:S(2)}, u32[]{:S(2)}) %collective-permute-start.15) | collective-permute-done | bytes 1179680 | tf_op jit(solution)/shard_map/ppermute | solution.py:489
  216.9 2.8 maximum_convert_fusion
  221.6 4.1 all-to-all-start.1
  228.8 2.1 multiply_reduce_fusion.5
  233.9 7.3 %all-to-all-done.1 = bf16[4,192,384]{2,1,0:T(8,128)(2,1)} async-done(((bf16[4,192,384]{2,1,0:T(8,128)(2,1)}), bf16[4,192,384]{2,1,0:T(8,128)(2,1)}, u32[]{:S(2)}, u32[]{:S(2)}) %all-to-all-start.1) | async-done | bytes 589856 | tf_op jit(solution)/shard_map/all_to_all | solution.py:385
  243.1 2.1 collective-permute-done.19
  245.2 7.8 %collective-permute-done.21.refs_7_ = bf16[192,3072]{1,0:T(8,128)(2,1)} collective-permute-done((bf16[192,3072]{1,0:T(8,128)(2,1)}, bf16[192,3072]{1,0:T(8,128)(2,1)}, u32[]{:S(2)}, u32[]{:S(2)}) %collective-permute-start.21) | collective-permute-done | bytes 1179680 | tf_op jit(solution)/shard_map/ppermute | solution.py:332
  253.0 8.0 %assemble.3 = (bf16[1536,2048]{1,0:T(8,128)(2,1)}, bf16[1536,1024]{1,0:T(8,128)(2,1)}) custom-call(s32[8]{0:T(128)} %stack.44.place_ref, bf16[192,3072]{1,0:T(8,128)(2,1)} %pad_maximum_fusion.5.refs_0_, bf16[192,3072]{1,0:T(8,128)(2,1)} %copy-done.39, bf16[192,3072]{1,0:T(8,128)(2,1)} %copy-done.40, bf16[192,3072]{1,0:T(8,128)(2,1)} %copy-done.41, ...), custom_call_target="tpu_custom_call" | custom-call | bytes 18874368 | tf_op jit(solution)/shard_map/assemble/pallas_call | solution.py:308
  261.7 7.8 %fusion.105 = f32[768,2048]{1,0:T(8,128)S(1)} fusion(bf16[1536,2048]{1,0:T(8,128)(2,1)} %get-tuple-element.107, bf16[192,1536]{1,0:T(8,128)(2,1)S(1)} %collective-permute-done.20, bf16[192,1536]{1,0:T(8,128)(2,1)} %collective-permute-done.19, bf16[192,1536]{1,0:T(8,128)(2,1)S(1)} %collective-permute-done.18, bf16[192,1536]{1,0:T(8,128)(2,1)} %multiply_convert_fusion.4), kind=kOutput, calls=%fused_computation.255 | convolution fusion | flops 4841275392 | bytes 14942208 | tf_op jit(solution)/shard_map/dot_general | solution.py:378
  269.7 2.5 copy-done.66
  272.3 5.0 multiply_convert_fusion.2
  279.4 3.7 convolution_convert_fusion.4
  283.2 2.6 fusion.109
  285.8 2.5 convolution_convert_fusion.5
  290.3 4.8 convolution_add_fusion.2
  296.6 2.6 convolution_convert_fusion.8
  300.7 4.2 convolution_convert_fusion
  304.9 6.8 %collective-permute-done.27 = bf16[192,1536]{1,0:T(8,128)(2,1)} collective-permute-done((bf16[192,1536]{1,0:T(8,128)(2,1)}, bf16[192,1536]{1,0:T(8,128)(2,1)}, u32[]{:S(2)}, u32[]{:S(2)}) %collective-permute-start.27) | collective-permute-done | bytes 589856 | tf_op jit(solution)/shard_map/ppermute | solution.py:332
  311.7 2.4 multiply_reduce_fusion.1
  314.2 2.9 fusion.106
  317.6 3.1 fusion.36
  320.8 3.1 fusion.34
  323.8 8.1 %collective-permute-done.29 = bf16[192,1536]{1,0:T(8,128)(2,1)} collective-permute-done((bf16[192,1536]{1,0:T(8,128)(2,1)}, bf16[192,1536]{1,0:T(8,128)(2,1)}, u32[]{:S(2)}, u32[]{:S(2)}) %collective-permute-start.29) | collective-permute-done | bytes 589856 | tf_op jit(solution)/shard_map/ppermute | solution.py:332
  333.7 4.3 convolution_convert_fusion.7
  345.1 2.8 convolution_add_fusion.3
  348.8 2.5 fusion.116.dog_ref
  351.3 31.6 %attend_bwd.1 = (bf16[768,1536]{1,0:T(8,128)(2,1)}, f32[3,1,768]{2,1,0:T(1,128)}) custom-call(s32[1]{0:T(128)} %bitcast.3.order_ref, bf16[768,1536]{1,0:T(8,128)(2,1)} %convolution_convert_fusion.2.proj_ref, f32[3,1,768]{2,1,0:T(1,128)} %reshape.176.lg_ref, f32[768,384]{1,0:T(8,128)} %fusion.116.dog_ref, f32[3,768,768]{2,1,0:T(8,128)} %get-tuple-element.125.pr_ref, ...), custom_call_target="tpu_custom_call" | custom-call | flops 15000000512 | bytes 10000000 | tf_op jit(solution)/shard_map/attend_bwd/pallas_call | solution.py:280
  393.5 5.5 fusion.4
  400.2 4.2 all-to-all-start.2
  404.6 5.3 convolution_convert_fusion.1
  410.9 2.2 convert_add_fusion.2
  417.8 4.8 fusion.3
  428.6 10.2 %collective-permute-done.35 = bf16[192,1536]{1,0:T(8,128)(2,1)} collective-permute-done((bf16[192,1536]{1,0:T(8,128)(2,1)}, bf16[192,1536]{1,0:T(8,128)(2,1)}, u32[]{:S(2)}, u32[]{:S(2)}) %collective-permute-start.35) | collective-permute-done | bytes 589856 | tf_op jit(solution)/shard_map/ppermute | solution.py:332
  438.8 2.7 multiply_reduce_fusion.3
  447.4 2.2 add_convert_fusion
  452.9 2.4 collective-permute-start.48
  455.3 4.2 convolution_convert_fusion.3
  460.5 3.8 all-to-all-start.3
  466.8 4.4 convert_add_fusion
  479.3 15.3 %all-to-all-done.3 = bf16[208,4,384]{2,0,1:T(8,128)(2,1)S(1)} async-done(((bf16[208,4,384]{2,0,1:T(8,128)(2,1)}), bf16[208,4,384]{2,0,1:T(8,128)(2,1)S(1)}, u32[]{:S(2)}, u32[]{:S(2)}) %all-to-all-start.3) | async-done | bytes 639008 | tf_op jit(solution)/shard_map/all_to_all | solution.py:471
  496.1 2.1 fusion.48
  505.7 4.5 collective-permute-done.42
  512.3 2.3 fusion.51
  514.6 14.3 %collective-permute-done.40 = bf16[384,1536]{1,0:T(8,128)(2,1)} collective-permute-done((bf16[384,1536]{1,0:T(8,128)(2,1)}, bf16[384,1536]{1,0:T(8,128)(2,1)}, u32[]{:S(2)}, u32[]{:S(2)}) %collective-permute-start.40) | collective-permute-done | bytes 1179680 | tf_op jit(solution)/shard_map/ppermute | solution.py:332
  528.9 2.4 fusion.26
  537.8 2.3 fusion.49
  548.0 2.7 bitcast_convert_fusion
  551.9 11.4 %collective-permute-done.46 = bf16[192,1536]{1,0:T(8,128)(2,1)} collective-permute-done((bf16[192,1536]{1,0:T(8,128)(2,1)}, bf16[192,1536]{1,0:T(8,128)(2,1)}, u32[]{:S(2)}, u32[]{:S(2)}) %collective-permute-start.46) | collective-permute-done | bytes 589856 | tf_op jit(solution)/shard_map/ppermute | solution.py:332
  (356 shorter events, 132.5 us)
Async XLA Ops:
  9.7 37.0 %all-to-all-start = ((bf16[4,192,384]{2,1,0:T(8,128)(2,1)}), bf16[4,192,384]{2,1,0:T(8,128)(2,1)S(1)}, u32[]{:S(2)}, u32[]{:S(2)}) async-start(bf16[4,192,384]{2,1,0:T(8,128)(2,1)} %dynamic-slice_bitcast_fusion.1), calls=%async_computation | async-start | bytes 1179648 | tf_op jit(solution)/shard_map/all_to_all | solution.py:385
  16.1 178.3 %all-gather.2.cloned.1.call-start = ((), (), s32[]{:S(2)}) async-start(), calls=%async_computation.6 | async-start | bytes 1327104 | tf_op jit(solution)/shard_map/all_gather | solution.py:481
  17.4 76.8 %copy-start.53 = (bf16[1024,192]{0,1:T(8,128)(2,1)S(1)}, bf16[1024,192]{0,1:T(8,128)(2,1)}, u32[]{:S(2)}) copy-start(bf16[1024,192]{0,1:T(8,128)(2,1)} %param.21) | copy-start | bytes 1179652
  18.1 80.0 %copy-start.21 = (bf16[192,1664]{1,0:T(8,128)(2,1)}, bf16[192,1664]{1,0:T(8,128)(2,1)S(1)}, u32[]{:S(2)}) copy-start(bf16[192,1664]{1,0:T(8,128)(2,1)S(1)} %concatenate.104.refs_0_) | copy-start | bytes 1916932
  18.1 30.2 %collective-permute-start.4 = (bf16[192,1664]{1,0:T(8,128)(2,1)S(1)}, bf16[192,1664]{1,0:T(8,128)(2,1)}, u32[]{:S(2)}, u32[]{:S(2)}) collective-permute-start(bf16[192,1664]{1,0:T(8,128)(2,1)S(1)} %concatenate.104.refs_0_), channel_id=1, source_target_pairs={{0,1},{1,2},{2,3},{3,0},{4,5},{5,6},{6,7},{7,4},{8,9},{9,10},{10,1... | collective-permute-start | bytes 1916936 | tf_op jit(solution)/shard_map/ppermute | solution.py:489
  20.2 35.2 %collective-permute-start.6 = (bf16[192,1664]{1,0:T(8,128)(2,1)S(1)}, bf16[192,1664]{1,0:T(8,128)(2,1)}, u32[]{:S(2)}, u32[]{:S(2)}) collective-permute-start(bf16[192,1664]{1,0:T(8,128)(2,1)S(1)} %concatenate.104.refs_0_), channel_id=1, source_target_pairs={{0,3},{1,0},{2,1},{3,2},{4,7},{5,4},{6,5},{7,6},{8,11},{9,8},{10,9... | collective-permute-start | bytes 1916936 | tf_op jit(solution)/shard_map/ppermute | solution.py:489
  22.0 33.4 %collective-permute-start.3 = (bf16[192,1664]{1,0:T(8,128)(2,1)S(1)}, bf16[192,1664]{1,0:T(8,128)(2,1)}, u32[]{:S(2)}, u32[]{:S(2)}) collective-permute-start(bf16[192,1664]{1,0:T(8,128)(2,1)S(1)} %concatenate.104.refs_0_), channel_id=1, source_target_pairs={{0,16},{16,0},{1,17},{17,1},{2,18},{18,2},{3,19},{19,3},{4,20},{20... | collective-permute-start | bytes 1916936 | tf_op jit(solution)/shard_map/ppermute | solution.py:332
  46.8 13.1 %collective-permute-start.1 = (bf16[192,1536]{1,0:T(8,128)(2,1)S(1)}, bf16[192,1536]{1,0:T(8,128)(2,1)S(1)}, u32[]{:S(2)}, u32[]{:S(2)}) collective-permute-start(bf16[192,1536]{1,0:T(8,128)(2,1)S(1)} %bitcast.178), channel_id=1, source_target_pairs={{0,8},{4,12},{8,0},{12,4},{1,9},{5,13},{9,1},{13,5},{2,10},{6,14},... | collective-permute-start | bytes 1769480 | tf_op jit(solution)/shard_map/ppermute | solution.py:332
  59.9 32.7 %collective-permute-start.8 = (bf16[192,1664]{1,0:T(8,128)(2,1)S(1)}, bf16[192,1664]{1,0:T(8,128)(2,1)}, u32[]{:S(2)}, u32[]{:S(2)}) collective-permute-start(bf16[192,1664]{1,0:T(8,128)(2,1)S(1)} %concatenate.104.refs_0_), channel_id=1, source_target_pairs={{0,2},{1,3},{2,0},{3,1},{4,6},{5,7},{6,4},{7,5},{8,10},{9,11},{10,... | collective-permute-start | bytes 1916936 | tf_op jit(solution)/shard_map/ppermute | solution.py:489
  60.1 36.9 %collective-permute-start = (bf16[192,1536]{1,0:T(8,128)(2,1)S(1)}, bf16[192,1536]{1,0:T(8,128)(2,1)S(1)}, u32[]{:S(2)}, u32[]{:S(2)}) collective-permute-start(bf16[192,1536]{1,0:T(8,128)(2,1)S(1)} %bitcast.179), channel_id=1, source_target_pairs={{0,4},{4,0},{8,12},{12,8},{1,5},{5,1},{9,13},{13,9},{2,6},{6,2},{1... | collective-permute-start | bytes 1769480 | tf_op jit(solution)/shard_map/ppermute | solution.py:332
  60.1 37.3 %collective-permute-start.2 = (bf16[192,1536]{1,0:T(8,128)(2,1)S(1)}, bf16[192,1536]{1,0:T(8,128)(2,1)S(1)}, u32[]{:S(2)}, u32[]{:S(2)}) collective-permute-start(bf16[192,1536]{1,0:T(8,128)(2,1)S(1)} %collective-permute-done.1), channel_id=1, source_target_pairs={{0,4},{4,0},{8,12},{12,8},{1,5},{5,1},{9,13},{13,9},{2,6},{6,2},{1... | collective-permute-start | bytes 1769480 | tf_op jit(solution)/shard_map/ppermute | solution.py:332
  60.6 37.5 %collective-permute-start.5 = (bf16[192,1664]{1,0:T(8,128)(2,1)}, bf16[192,1664]{1,0:T(8,128)(2,1)}, u32[]{:S(2)}, u32[]{:S(2)}) collective-permute-start(bf16[192,1664]{1,0:T(8,128)(2,1)} %collective-permute-done.4.refs_2_), channel_id=1, source_target_pairs={{0,16},{16,0},{1,17},{17,1},{2,18},{18,2},{3,19},{19,3},{4,20},{20... | collective-permute-start | bytes 1916936 | tf_op jit(solution)/shard_map/ppermute | solution.py:332
  62.2 39.9 %collective-permute-start.7 = (bf16[192,1664]{1,0:T(8,128)(2,1)}, bf16[192,1664]{1,0:T(8,128)(2,1)}, u32[]{:S(2)}, u32[]{:S(2)}) collective-permute-start(bf16[192,1664]{1,0:T(8,128)(2,1)} %collective-permute-done.6.refs_4_), channel_id=1, source_target_pairs={{0,16},{16,0},{1,17},{17,1},{2,18},{18,2},{3,19},{19,3},{4,20},{20... | collective-permute-start | bytes 1916936 | tf_op jit(solution)/shard_map/ppermute | solution.py:332
  92.6 24.0 %collective-permute-start.9 = (bf16[192,1664]{1,0:T(8,128)(2,1)}, bf16[192,1664]{1,0:T(8,128)(2,1)}, u32[]{:S(2)}, u32[]{:S(2)}) collective-permute-start(bf16[192,1664]{1,0:T(8,128)(2,1)} %collective-permute-done.8.refs_6_), channel_id=1, source_target_pairs={{0,16},{16,0},{1,17},{17,1},{2,18},{18,2},{3,19},{19,3},{4,20},{20... | collective-permute-start | bytes 1916936 | tf_op jit(solution)/shard_map/ppermute | solution.py:332
  97.0 24.7 %copy-start.6 = (bf16[192,1536]{1,0:T(8,128)(2,1)}, bf16[192,1536]{1,0:T(8,128)(2,1)S(1)}, u32[]{:S(2)}) copy-start(bf16[192,1536]{1,0:T(8,128)(2,1)S(1)} %collective-permute-done) | copy-start | bytes 1769476
  97.0 42.0 %collective-permute-start.10 = (bf16[192,3072]{1,0:T(8,128)(2,1)}, bf16[192,3072]{1,0:T(8,128)(2,1)S(1)}, u32[]{:S(2)}, u32[]{:S(2)}) collective-permute-start(bf16[192,3072]{1,0:T(8,128)(2,1)} %pad_maximum_fusion.5.refs_0_), channel_id=1, source_target_pairs={{0,16},{16,0},{1,17},{17,1},{2,18},{18,2},{3,19},{19,3},{4,20},{20... | collective-permute-start | bytes 3538952 | tf_op jit(solution)/shard_map/ppermute | solution.py:332
  97.4 24.2 %copy-start.8 = (bf16[192,1536]{1,0:T(8,128)(2,1)}, bf16[192,1536]{1,0:T(8,128)(2,1)S(1)}, u32[]{:S(2)}) copy-start(bf16[192,1536]{1,0:T(8,128)(2,1)S(1)} %collective-permute-done.2) | copy-start | bytes 1769476
  98.0 46.8 %collective-permute-start.11 = (bf16[192,3072]{1,0:T(8,128)(2,1)}, bf16[192,3072]{1,0:T(8,128)(2,1)S(1)}, u32[]{:S(2)}, u32[]{:S(2)}) collective-permute-start(bf16[192,3072]{1,0:T(8,128)(2,1)} %pad_maximum_fusion.5.refs_0_), channel_id=1, source_target_pairs={{0,1},{1,2},{2,3},{3,0},{4,5},{5,6},{6,7},{7,4},{8,9},{9,10},{10,1... | collective-permute-start | bytes 3538952 | tf_op jit(solution)/shard_map/ppermute | solution.py:489
  98.1 60.9 %collective-permute-start.12 = (bf16[192,3072]{1,0:T(8,128)(2,1)}, bf16[192,3072]{1,0:T(8,128)(2,1)}, u32[]{:S(2)}, u32[]{:S(2)}) collective-permute-start(bf16[192,3072]{1,0:T(8,128)(2,1)} %pad_maximum_fusion.5.refs_0_), channel_id=1, source_target_pairs={{0,3},{1,0},{2,1},{3,2},{4,7},{5,4},{6,5},{7,6},{8,11},{9,8},{10,9... | collective-permute-start | bytes 3538952 | tf_op jit(solution)/shard_map/ppermute | solution.py:489
  144.9 46.5 %copy-start.40 = (bf16[192,3072]{1,0:T(8,128)(2,1)}, bf16[192,3072]{1,0:T(8,128)(2,1)S(1)}, u32[]{:S(2)}) copy-start(bf16[192,3072]{1,0:T(8,128)(2,1)S(1)} %collective-permute-done.11.refs_2_) | copy-start | bytes 3538948
  159.0 53.2 %collective-permute-start.15 = (bf16[192,3072]{1,0:T(8,128)(2,1)}, bf16[192,3072]{1,0:T(8,128)(2,1)}, u32[]{:S(2)}, u32[]{:S(2)}) collective-permute-start(bf16[192,3072]{1,0:T(8,128)(2,1)} %pad_maximum_fusion.5.refs_0_), channel_id=1, source_target_pairs={{0,2},{1,3},{2,0},{3,1},{4,6},{5,7},{6,4},{7,5},{8,10},{9,11},{10,... | collective-permute-start | bytes 3538952 | tf_op jit(solution)/shard_map/ppermute | solution.py:489
  161.2 30.2 %collective-permute-start.13 = (bf16[192,3072]{1,0:T(8,128)(2,1)S(1)}, bf16[192,3072]{1,0:T(8,128)(2,1)S(1)}, u32[]{:S(2)}, u32[]{:S(2)}) collective-permute-start(bf16[192,3072]{1,0:T(8,128)(2,1)S(1)} %collective-permute-done.11.refs_2_), channel_id=1, source_target_pairs={{0,16},{16,0},{1,17},{17,1},{2,18},{18,2},{3,19},{19,3},{4,20},{20... | collective-permute-start | bytes 3538952 | tf_op jit(solution)/shard_map/ppermute | solution.py:332
  196.7 15.5 %collective-permute-start.14 = (bf16[384,1536]{1,0:T(8,128)(2,1)S(1)}, bf16[384,1536]{1,0:T(8,128)(2,1)S(1)}, u32[]{:S(2)}, u32[]{:S(2)}) collective-permute-start(bf16[384,1536]{1,0:T(8,128)(2,1)S(1)} %convolution_convert_fusion.6), channel_id=1, source_target_pairs={{0,4},{4,0},{8,12},{12,8},{1,5},{5,1},{9,13},{13,9},{2,6},{6,2},{1... | collective-permute-start | bytes 3538952 | tf_op jit(solution)/shard_map/ppermute | solution.py:332
  196.8 30.7 %collective-permute-start.17 = (bf16[192,3072]{1,0:T(8,128)(2,1)}, bf16[192,3072]{1,0:T(8,128)(2,1)}, u32[]{:S(2)}, u32[]{:S(2)}) collective-permute-start(bf16[192,3072]{1,0:T(8,128)(2,1)} %collective-permute-done.12.refs_4_), channel_id=1, source_target_pairs={{0,16},{16,0},{1,17},{17,1},{2,18},{18,2},{3,19},{19,3},{4,20},{20... | collective-permute-start | bytes 3538952 | tf_op jit(solution)/shard_map/ppermute | solution.py:332
  215.4 13.4 %collective-permute-start.16 = (bf16[192,1536]{1,0:T(8,128)(2,1)}, bf16[192,1536]{1,0:T(8,128)(2,1)}, u32[]{:S(2)}, u32[]{:S(2)}) collective-permute-start(bf16[192,1536]{1,0:T(8,128)(2,1)} %slice.505), channel_id=1, source_target_pairs={{0,8},{4,12},{8,0},{12,4},{1,9},{5,13},{9,1},{13,5},{2,10},{6,14},... | collective-permute-start | bytes 1769480 | tf_op jit(solution)/shard_map/ppermute | solution.py:332
  221.6 19.6 %all-to-all-start.1 = ((bf16[4,192,384]{2,1,0:T(8,128)(2,1)}), bf16[4,192,384]{2,1,0:T(8,128)(2,1)}, u32[]{:S(2)}, u32[]{:S(2)}) async-start(bf16[4,192,384]{2,1,0:T(8,128)(2,1)} %dynamic-slice_bitcast_fusion), calls=%async_computation.1 | async-start | bytes 1179648 | tf_op jit(solution)/shard_map/all_to_all | solution.py:385
  225.8 272.4 %reduce-scatter.5.cloned.1.call-start = ((), (), s32[]{:S(2)}) async-start(), calls=%async_computation.8 | async-start | bytes 3538944 | tf_op jit(solution)/shard_map/reduce_scatter | solution.py:553
  225.8 27.1 %collective-permute-start.21 = (bf16[192,3072]{1,0:T(8,128)(2,1)}, bf16[192,3072]{1,0:T(8,128)(2,1)}, u32[]{:S(2)}, u32[]{:S(2)}) collective-permute-start(bf16[192,3072]{1,0:T(8,128)(2,1)} %collective-permute-done.15.refs_6_), channel_id=1, source_target_pairs={{0,16},{16,0},{1,17},{17,1},{2,18},{18,2},{3,19},{19,3},{4,20},{20... | collective-permute-start | bytes 3538952 | tf_op jit(solution)/shard_map/ppermute | solution.py:332
  232.4 12.7 %collective-permute-start.19 = (bf16[192,1536]{1,0:T(8,128)(2,1)}, bf16[192,1536]{1,0:T(8,128)(2,1)}, u32[]{:S(2)}, u32[]{:S(2)}) collective-permute-start(bf16[192,1536]{1,0:T(8,128)(2,1)} %multiply_convert_fusion.4), channel_id=1, source_target_pairs={{0,8},{4,12},{8,0},{12,4},{1,9},{5,13},{9,1},{13,5},{2,10},{6,14},... | collective-permute-start | bytes 1769480 | tf_op jit(solution)/shard_map/ppermute | solution.py:332
  242.4 18.7 %collective-permute-start.18 = (bf16[192,1536]{1,0:T(8,128)(2,1)}, bf16[192,1536]{1,0:T(8,128)(2,1)S(1)}, u32[]{:S(2)}, u32[]{:S(2)}) collective-permute-start(bf16[192,1536]{1,0:T(8,128)(2,1)} %multiply_convert_fusion.4), channel_id=1, source_target_pairs={{0,4},{4,0},{8,12},{12,8},{1,5},{5,1},{9,13},{13,9},{2,6},{6,2},{1... | collective-permute-start | bytes 1769480 | tf_op jit(solution)/shard_map/ppermute | solution.py:332
  242.4 18.7 %collective-permute-start.24 = (bf16[192,1536]{1,0:T(8,128)(2,1)S(1)}, bf16[192,1536]{1,0:T(8,128)(2,1)S(1)}, u32[]{:S(2)}, u32[]{:S(2)}) collective-permute-start(bf16[192,1536]{1,0:T(8,128)(2,1)S(1)} %bitcast.184), channel_id=1, source_target_pairs={{0,8},{4,12},{8,0},{12,4},{1,9},{5,13},{9,1},{13,5},{2,10},{6,14},... | collective-permute-start | bytes 1769480 | tf_op jit(solution)/shard_map/ppermute | solution.py:332
  245.2 16.5 %collective-permute-start.20 = (bf16[192,1536]{1,0:T(8,128)(2,1)}, bf16[192,1536]{1,0:T(8,128)(2,1)S(1)}, u32[]{:S(2)}, u32[]{:S(2)}) collective-permute-start(bf16[192,1536]{1,0:T(8,128)(2,1)} %collective-permute-done.19), channel_id=1, source_target_pairs={{0,4},{4,0},{8,12},{12,8},{1,5},{5,1},{9,13},{13,9},{2,6},{6,2},{1... | collective-permute-start | bytes 1769480 | tf_op jit(solution)/shard_map/ppermute | solution.py:332
  261.0 8.5 %collective-permute-start.22 = (bf16[192,1536]{1,0:T(8,128)(2,1)S(1)}, bf16[192,1536]{1,0:T(8,128)(2,1)S(1)}, u32[]{:S(2)}, u32[]{:S(2)}) collective-permute-start(bf16[192,1536]{1,0:T(8,128)(2,1)S(1)} %bitcast.186), channel_id=1, source_target_pairs={{0,4},{4,0},{8,12},{12,8},{1,5},{5,1},{9,13},{13,9},{2,6},{6,2},{1... | collective-permute-start | bytes 1769480 | tf_op jit(solution)/shard_map/ppermute | solution.py:332
  261.1 8.5 %collective-permute-start.25 = (bf16[192,1536]{1,0:T(8,128)(2,1)S(1)}, bf16[192,1536]{1,0:T(8,128)(2,1)S(1)}, u32[]{:S(2)}, u32[]{:S(2)}) collective-permute-start(bf16[192,1536]{1,0:T(8,128)(2,1)S(1)} %collective-permute-done.24), channel_id=1, source_target_pairs={{0,4},{4,0},{8,12},{12,8},{1,5},{5,1},{9,13},{13,9},{2,6},{6,2},{1... | collective-permute-start | bytes 1769480 | tf_op jit(solution)/shard_map/ppermute | solution.py:332
  283.2 7.0 %collective-permute-start.26 = (bf16[384,1536]{1,0:T(8,128)(2,1)}, bf16[384,1536]{1,0:T(8,128)(2,1)}, u32[]{:S(2)}, u32[]{:S(2)}) collective-permute-start(bf16[384,1536]{1,0:T(8,128)(2,1)} %convolution_convert_fusion.4), channel_id=1, source_target_pairs={{0,4},{4,0},{8,12},{12,8},{1,5},{5,1},{9,13},{13,9},{2,6},{6,2},{1... | collective-permute-start | bytes 3538952 | tf_op jit(solution)/shard_map/ppermute | solution.py:332
  288.3 55.8 %collective-permute-start.23 = (bf16[384,1536]{1,0:T(8,128)(2,1)}, bf16[384,1536]{1,0:T(8,128)(2,1)}, u32[]{:S(2)}, u32[]{:S(2)}) collective-permute-start(bf16[384,1536]{1,0:T(8,128)(2,1)} %convolution_convert_fusion.5), channel_id=1, source_target_pairs={{0,4},{4,0},{8,12},{12,8},{1,5},{5,1},{9,13},{13,9},{2,6},{6,2},{1... | collective-permute-start | bytes 3538952 | tf_op jit(solution)/shard_map/ppermute | solution.py:332
  296.1 15.7 %collective-permute-start.27 = (bf16[192,1536]{1,0:T(8,128)(2,1)}, bf16[192,1536]{1,0:T(8,128)(2,1)}, u32[]{:S(2)}, u32[]{:S(2)}) collective-permute-start(bf16[192,1536]{1,0:T(8,128)(2,1)} %slice.504), channel_id=1, source_target_pairs={{0,8},{4,12},{8,0},{12,4},{1,9},{5,13},{9,1},{13,5},{2,10},{6,14},... | collective-permute-start | bytes 1769480 | tf_op jit(solution)/shard_map/ppermute | solution.py:332
  299.2 44.9 %collective-permute-start.31 = (bf16[768,1024]{1,0:T(8,128)(2,1)}, bf16[768,1024]{1,0:T(8,128)(2,1)}, u32[]{:S(2)}, u32[]{:S(2)}) collective-permute-start(bf16[768,1024]{1,0:T(8,128)(2,1)} %convolution_convert_fusion.8), channel_id=1, source_target_pairs={{0,16},{16,0},{1,17},{17,1},{2,18},{18,2},{3,19},{19,3},{4,20},{20... | collective-permute-start | bytes 4718600 | tf_op jit(solution)/shard_map/ppermute | solution.py:332
  317.1 14.9 %collective-permute-start.29 = (bf16[192,1536]{1,0:T(8,128)(2,1)}, bf16[192,1536]{1,0:T(8,128)(2,1)}, u32[]{:S(2)}, u32[]{:S(2)}) collective-permute-start(bf16[192,1536]{1,0:T(8,128)(2,1)} %get-tuple-element.117), channel_id=1, source_target_pairs={{0,8},{4,12},{8,0},{12,4},{1,9},{5,13},{9,1},{13,5},{2,10},{6,14},... | collective-permute-start | bytes 1769480 | tf_op jit(solution)/shard_map/ppermute | solution.py:332
  323.8 18.4 %collective-permute-start.28 = (bf16[192,1536]{1,0:T(8,128)(2,1)}, bf16[192,1536]{1,0:T(8,128)(2,1)}, u32[]{:S(2)}, u32[]{:S(2)}) collective-permute-start(bf16[192,1536]{1,0:T(8,128)(2,1)} %get-tuple-element.117), channel_id=1, source_target_pairs={{0,4},{4,0},{8,12},{12,8},{1,5},{5,1},{9,13},{13,9},{2,6},{6,2},{1... | collective-permute-start | bytes 1769480 | tf_op jit(solution)/shard_map/ppermute | solution.py:332
  332.0 10.2 %collective-permute-start.30 = (bf16[192,1536]{1,0:T(8,128)(2,1)}, bf16[192,1536]{1,0:T(8,128)(2,1)}, u32[]{:S(2)}, u32[]{:S(2)}) collective-permute-start(bf16[192,1536]{1,0:T(8,128)(2,1)} %collective-permute-done.29), channel_id=1, source_target_pairs={{0,4},{4,0},{8,12},{12,8},{1,5},{5,1},{9,13},{13,9},{2,6},{6,2},{1... | collective-permute-start | bytes 1769480 | tf_op jit(solution)/shard_map/ppermute | solution.py:332
  338.1 54.2 %collective-permute-start.33 = (bf16[768,1024]{1,0:T(8,128)(2,1)}, bf16[768,1024]{1,0:T(8,128)(2,1)}, u32[]{:S(2)}, u32[]{:S(2)}) collective-permute-start(bf16[768,1024]{1,0:T(8,128)(2,1)} %convolution_convert_fusion.7), channel_id=1, source_target_pairs={{0,16},{16,0},{1,17},{17,1},{2,18},{18,2},{3,19},{19,3},{4,20},{20... | collective-permute-start | bytes 4718600 | tf_op jit(solution)/shard_map/ppermute | solution.py:332
  348.0 44.3 %collective-permute-start.32 = (bf16[192,1536]{1,0:T(8,128)(2,1)S(1)}, bf16[192,1536]{1,0:T(8,128)(2,1)S(1)}, u32[]{:S(2)}, u32[]{:S(2)}) collective-permute-start(bf16[192,1536]{1,0:T(8,128)(2,1)S(1)} %slice.503), channel_id=1, source_target_pairs={{0,8},{4,12},{8,0},{12,4},{1,9},{5,13},{9,1},{13,5},{2,10},{6,14},... | collective-permute-start | bytes 1769480 | tf_op jit(solution)/shard_map/ppermute | solution.py:332
  351.3 32.6 %copy-start.19 = (f32[768,1024]{1,0:T(8,128)S(1)}, f32[768,1024]{1,0:T(8,128)}, u32[]{:S(2)}) copy-start(f32[768,1024]{1,0:T(8,128)} %fusion.36) | copy-start | bytes 9437188
  387.2 41.4 %collective-permute-start.47 = (bf16[384,1024]{1,0:T(8,128)(2,1)}, bf16[384,1024]{1,0:T(8,128)(2,1)}, u32[]{:S(2)}, u32[]{:S(2)}) collective-permute-start(bf16[384,1024]{1,0:T(8,128)(2,1)} %pad_maximum_fusion.8), channel_id=1, source_target_pairs={{0,1},{1,0},{2,3},{3,2},{4,5},{5,4},{6,7},{7,6},{8,9},{9,8},{10,11... | collective-permute-start | bytes 2359304 | tf_op jit(solution)/shard_map/ppermute | solution.py:332
  399.0 18.7 %collective-permute-start.34 = (bf16[384,1536]{1,0:T(8,128)(2,1)}, bf16[384,1536]{1,0:T(8,128)(2,1)}, u32[]{:S(2)}, u32[]{:S(2)}) collective-permute-start(bf16[384,1536]{1,0:T(8,128)(2,1)} %fusion.4), channel_id=1, source_target_pairs={{0,4},{4,0},{8,12},{12,8},{1,5},{5,1},{9,13},{13,9},{2,6},{6,2},{1... | collective-permute-start | bytes 3538952 | tf_op jit(solution)/shard_map/ppermute | solution.py:332
  400.2 49.5 %all-to-all-start.2 = ((bf16[192,4,384]{2,0,1:T(8,128)(2,1)}), bf16[192,4,384]{2,0,1:T(8,128)(2,1)}, u32[]{:S(2)}, u32[]{:S(2)}) async-start(bf16[192,4,384]{2,0,1:T(8,128)(2,1)} %bitcast.164), calls=%async_computation.2 | async-start | bytes 1179648 | tf_op jit(solution)/shard_map/all_to_all | solution.py:471
  404.3 131.8 %reduce-scatter.3.cloned.1.call-start = ((), (), s32[]{:S(2)}) async-start(), calls=%async_computation.7 | async-start | bytes 1327104 | tf_op jit(solution)/shard_map/reduce_scatter | solution.py:553
  410.0 56.8 %collective-permute-start.39 = (bf16[768,1536]{1,0:T(8,128)(2,1)}, bf16[768,1536]{1,0:T(8,128)(2,1)}, u32[]{:S(2)}, u32[]{:S(2)}) collective-permute-start(bf16[768,1536]{1,0:T(8,128)(2,1)} %convolution_convert_fusion.1), channel_id=1, source_target_pairs={{0,16},{16,0},{1,17},{17,1},{2,18},{18,2},{3,19},{19,3},{4,20},{20... | collective-permute-start | bytes 7077896 | tf_op jit(solution)/shard_map/ppermute | solution.py:332
  415.8 80.3 %collective-permute-start.45 = (bf16[384,1024]{1,0:T(8,128)(2,1)}, bf16[384,1024]{1,0:T(8,128)(2,1)}, u32[]{:S(2)}, u32[]{:S(2)}) collective-permute-start(bf16[384,1024]{1,0:T(8,128)(2,1)} %pad_maximum_fusion.7), channel_id=1, source_target_pairs={{0,1},{1,0},{2,3},{3,2},{4,5},{5,4},{6,7},{7,6},{8,9},{9,8},{10,11... | collective-permute-start | bytes 2359304 | tf_op jit(solution)/shard_map/ppermute | solution.py:332
  423.6 15.2 %collective-permute-start.35 = (bf16[192,1536]{1,0:T(8,128)(2,1)}, bf16[192,1536]{1,0:T(8,128)(2,1)}, u32[]{:S(2)}, u32[]{:S(2)}) collective-permute-start(bf16[192,1536]{1,0:T(8,128)(2,1)} %slice.502), channel_id=1, source_target_pairs={{0,8},{4,12},{8,0},{12,4},{1,9},{5,13},{9,1},{13,5},{2,10},{6,14},... | collective-permute-start | bytes 1769480 | tf_op jit(solution)/shard_map/ppermute | solution.py:332
  425.1 22.3 %copy-start.14 = (f32[192,1536]{1,0:T(8,128)S(1)}, f32[192,1536]{1,0:T(8,128)}, u32[]{:S(2)}) copy-start(f32[192,1536]{1,0:T(8,128)} %get-tuple-element.213) | copy-start | bytes 3538948
  449.7 16.6 %collective-permute-start.37 = (bf16[4,1,192,384]{3,2,1,0:T(8,128)(2,1)}, bf16[4,1,192,384]{3,2,1,0:T(8,128)(2,1)}, u32[]{:S(2)}, u32[]{:S(2)}) collective-permute-start(bf16[4,1,192,384]{3,2,1,0:T(8,128)(2,1)} %bitcast.31), channel_id=1, source_target_pairs={{0,8},{4,12},{8,0},{12,4},{1,9},{5,13},{9,1},{13,5},{2,10},{6,14},... | collective-permute-start | bytes 1769480 | tf_op jit(solution)/shard_map/ppermute | solution.py:332
  452.9 57.2 %collective-permute-start.48 = (bf16[192,1024]{1,0:T(8,128)(2,1)}, bf16[192,1024]{1,0:T(8,128)(2,1)S(1)}, u32[]{:S(2)}, u32[]{:S(2)}) collective-permute-start(bf16[192,1024]{1,0:T(8,128)(2,1)} %fusion.50), channel_id=1, source_target_pairs={{0,2},{1,3},{2,0},{3,1},{4,6},{5,7},{6,4},{7,5},{8,10},{9,11},{10,... | collective-permute-start | bytes 1179656 | tf_op jit(solution)/shard_map/ppermute | solution.py:332
  459.6 15.9 %collective-permute-start.36 = (bf16[4,1,192,384]{3,2,1,0:T(8,128)(2,1)}, bf16[4,1,192,384]{3,2,1,0:T(8,128)(2,1)}, u32[]{:S(2)}, u32[]{:S(2)}) collective-permute-start(bf16[4,1,192,384]{3,2,1,0:T(8,128)(2,1)} %bitcast.31), channel_id=1, source_target_pairs={{0,4},{4,0},{8,12},{12,8},{1,5},{5,1},{9,13},{13,9},{2,6},{6,2},{1... | collective-permute-start | bytes 1769480 | tf_op jit(solution)/shard_map/ppermute | solution.py:332
  460.5 34.1 %all-to-all-start.3 = ((bf16[208,4,384]{2,0,1:T(8,128)(2,1)}), bf16[208,4,384]{2,0,1:T(8,128)(2,1)S(1)}, u32[]{:S(2)}, u32[]{:S(2)}) async-start(bf16[208,4,384]{2,0,1:T(8,128)(2,1)} %bitcast.195), calls=%async_computation.3 | async-start | bytes 1277952 | tf_op jit(solution)/shard_map/all_to_all | solution.py:471
  466.3 33.9 %collective-permute-start.38 = (bf16[4,1,192,384]{3,2,1,0:T(8,128)(2,1)}, bf16[4,1,192,384]{3,2,1,0:T(8,128)(2,1)}, u32[]{:S(2)}, u32[]{:S(2)}) collective-permute-start(bf16[4,1,192,384]{3,2,1,0:T(8,128)(2,1)} %collective-permute-done.37), channel_id=1, source_target_pairs={{0,4},{4,0},{8,12},{12,8},{1,5},{5,1},{9,13},{13,9},{2,6},{6,2},{1... | collective-permute-start | bytes 1769480 | tf_op jit(solution)/shard_map/ppermute | solution.py:332
  473.7 55.1 %collective-permute-start.40 = (bf16[384,1536]{1,0:T(8,128)(2,1)}, bf16[384,1536]{1,0:T(8,128)(2,1)}, u32[]{:S(2)}, u32[]{:S(2)}) collective-permute-start(bf16[384,1536]{1,0:T(8,128)(2,1)} %pad_maximum_fusion.6), channel_id=1, source_target_pairs={{0,1},{1,0},{2,3},{3,2},{4,5},{5,4},{6,7},{7,6},{8,9},{9,8},{10,11... | collective-permute-start | bytes 3538952 | tf_op jit(solution)/shard_map/ppermute | solution.py:332
  494.6 15.5 %collective-permute-start.42 = (bf16[4,1,208,384]{3,2,1,0:T(8,128)(2,1)S(1)}, bf16[4,1,208,384]{3,2,1,0:T(8,128)(2,1)}, u32[]{:S(2)}, u32[]{:S(2)}) collective-permute-start(bf16[4,1,208,384]{3,2,1,0:T(8,128)(2,1)S(1)} %bitcast.191), channel_id=1, source_target_pairs={{0,8},{4,12},{8,0},{12,4},{1,9},{5,13},{9,1},{13,5},{2,10},{6,14},... | collective-permute-start | bytes 1916936 | tf_op jit(solution)/shard_map/ppermute | solution.py:332
  496.1 14.9 %collective-permute-start.41 = (bf16[4,1,208,384]{3,2,1,0:T(8,128)(2,1)S(1)}, bf16[4,1,208,384]{3,2,1,0:T(8,128)(2,1)S(1)}, u32[]{:S(2)}, u32[]{:S(2)}) collective-permute-start(bf16[4,1,208,384]{3,2,1,0:T(8,128)(2,1)S(1)} %bitcast.193), channel_id=1, source_target_pairs={{0,4},{4,0},{8,12},{12,8},{1,5},{5,1},{9,13},{13,9},{2,6},{6,2},{1... | collective-permute-start | bytes 1916936 | tf_op jit(solution)/shard_map/ppermute | solution.py:332
  500.1 36.0 %collective-permute-start.49 = (bf16[192,1024]{1,0:T(8,128)(2,1)}, bf16[192,1024]{1,0:T(8,128)(2,1)S(1)}, u32[]{:S(2)}, u32[]{:S(2)}) collective-permute-start(bf16[192,1024]{1,0:T(8,128)(2,1)} %fusion.48), channel_id=1, source_target_pairs={{0,2},{1,3},{2,0},{3,1},{4,6},{5,7},{6,4},{7,5},{8,10},{9,11},{10,... | collective-permute-start | bytes 1179656 | tf_op jit(solution)/shard_map/ppermute | solution.py:332
  510.1 30.0 %collective-permute-start.43 = (bf16[4,1,208,384]{3,2,1,0:T(8,128)(2,1)}, bf16[4,1,208,384]{3,2,1,0:T(8,128)(2,1)S(1)}, u32[]{:S(2)}, u32[]{:S(2)}) collective-permute-start(bf16[4,1,208,384]{3,2,1,0:T(8,128)(2,1)} %collective-permute-done.42), channel_id=1, source_target_pairs={{0,4},{4,0},{8,12},{12,8},{1,5},{5,1},{9,13},{13,9},{2,6},{6,2},{1... | collective-permute-start | bytes 1916936 | tf_op jit(solution)/shard_map/ppermute | solution.py:332
  534.1 29.2 %collective-permute-start.46 = (bf16[192,1536]{1,0:T(8,128)(2,1)}, bf16[192,1536]{1,0:T(8,128)(2,1)}, u32[]{:S(2)}, u32[]{:S(2)}) collective-permute-start(bf16[192,1536]{1,0:T(8,128)(2,1)} %fusion.26), channel_id=1, source_target_pairs={{0,2},{1,3},{2,0},{3,1},{4,6},{5,7},{6,4},{7,5},{8,10},{9,11},{10,... | collective-permute-start | bytes 1769480 | tf_op jit(solution)/shard_map/ppermute | solution.py:332
  545.1 5.6 collective-permute-start.44
  (67 other events, 413.6 us)
Sparse Core Ops, SparseCore 0:
  60.7 79.7 all-gather.1
  333.9 97.3 reduce-scatter.4
  459.7 72.5 reduce-scatter.2
